TPU v7x, 32 devices: a whole 2x2x4 slice. The times are simulated.
32 devices in a mesh: pb: 8 (over y, x, core), ka: 4 (over z).
Axes of the slice: x: 2, y: 2, z: 4, core: 2. Of those that a mesh axis runs over, the one named last changes fastest.
Arguments:
- queries: bfloat16 [4096, 1024], P(('pb', 'ka')), may hold values from -200 to 200
- keys: bfloat16 [4096, 128], P(('pb', 'ka')), may hold values from -6 to 6
- values: bfloat16 [4096, 128], P(('pb', 'ka')), may hold values from -6 to 6
- positions: int32 [4096], replicated, may hold values from 0 to 4095, as said below
Outputs:
- attended: float32 [4096, 1024], P(('pb', 'ka'))
Inputs may be any that keep to these rules, and one draw needn't show every extreme that they name: A permutation of 0 to 4095; each aligned run of 128 slots holds consecutive positions in increasing order.
All inputs are finite; a program needn't handle non-finite values.
Results may differ from a plain program's by a relative error of at most 0.0003.
Values may be sent and summed in bfloat16 or wider, within the bound.
No kernel may reach another device: no remote copies, remote signals or barrier semaphores. Data moves between devices by JAX's collectives and lax.ppermute only.
A program may use at most 64 MiB of HBM per device.

v0:
```python
import functools
import math

import jax
import jax.numpy as jnp
from jax import lax
from jax.experimental import pallas as pl
from jax.experimental.pallas import tpu as pltpu
from jax.sharding import PartitionSpec as P


HD = 128
AXES = ("pb", "ka")
BIG = -1e30
STEP = 4
LIMIT = 24 << 20

VMEM = pl.BlockSpec(memory_space=pltpu.VMEM)
SMEM = pl.BlockSpec(memory_space=pltpu.SMEM)


def combine(rows, keys, values, largest, totals, summed, to_log2, mask=None):
    score = lax.dot_general(
        rows, keys, (((1,), (1,)), ((), ())), preferred_element_type=jnp.float32
    )
    if mask is not None:
        score = jnp.where(mask, score, BIG)
    parts = [score[:, at : at + HD] for at in range(0, keys.shape[0], HD)]
    top = jnp.max(functools.reduce(jnp.maximum, parts), axis=1, keepdims=True)
    if largest is None:
        top = jnp.broadcast_to(top, (rows.shape[0], HD))
    else:
        top = jnp.maximum(largest, top)
    weights = [jnp.exp2((part - top) * to_log2) for part in parts]
    if mask is not None:
        weights = [jnp.where(mask, weight, 0.0) for weight in weights]
    total = functools.reduce(jnp.add, weights)
    weight = jnp.concatenate(weights, axis=1) if len(weights) > 1 else weights[0]
    high = weight.astype(jnp.bfloat16)
    low = (weight - high.astype(jnp.float32)).astype(jnp.bfloat16)
    over = (((1,), (0,)), ((), ()))
    result = lax.dot_general(high, values, over, preferred_element_type=jnp.float32)
    result += lax.dot_general(low, values, over, preferred_element_type=jnp.float32)
    if largest is None:
        return top, total, result
    factor = jnp.exp2((largest - top) * to_log2)
    return top, totals * factor + total, summed * factor + result


def attend_kernel(masks, first, last, size_key, token, *refs):
    count = len(masks)
    queries_ref = refs[0]
    block_refs = refs[1 : 1 + count]
    rest = refs[1 + count :]
    if not first:
        starts_ref, rest = rest[0], rest[1:]
    state_in, rest = (None, rest) if first else (rest[:3], rest[3:])
    outs, (rows_ref, order_ref), state = (
        (rest[:1], rest[1:3], rest[3:6]) if last else (rest[:3], rest[3:5], rest[:3])
    )
    heads = queries_ref.shape[1] // HD
    to_log2 = math.log2(math.e) / HD**0.5
    for head in range(heads):
        rows_ref[head * token : (head + 1) * token, :] = queries_ref[:, head * HD : (head + 1) * HD]

    def pieces(ref, places):
        offsets = [pl.multiple_of(place * 2 * token, 2 * token) for place in places]
        keys = [ref[pl.ds(offset, token), :] for offset in offsets]
        values = [ref[pl.ds(offset + token, token), :] for offset in offsets]
        if len(places) == 1:
            return keys[0], values[0]
        return jnp.concatenate(keys, axis=0), jnp.concatenate(values, axis=0)

    def update(ref, places):
        keys, values = pieces(ref, places)
        new = combine(
            rows_ref[...], keys, values, state[0][...], state[1][...], state[2][...], to_log2
        )
        for held, value in zip(state, new):
            held[...] = value

    if first:
        shape = (heads, token, token)
        causal = lax.broadcasted_iota(jnp.int32, shape, 2) <= lax.broadcasted_iota(
            jnp.int32, shape, 1
        )
        keys, values = pieces(block_refs[0], [0])
        new = combine(
            rows_ref[...],
            keys,
            values,
            None,
            None,
            None,
            to_log2,
            causal.reshape(heads * token, token),
        )
        for held, value in zip(state, new):
            held[...] = value
        return
    for held, value in zip(state, state_in):
        held[...] = value[...]

    own_pb, own_ka = lax.axis_index("pb"), lax.axis_index("ka")
    own_start = starts_ref[own_pb * size_key + own_ka]
    core = own_pb % 2
    for ref, (mask_even, mask_odd) in zip(block_refs, masks):
        source = own_pb ^ jnp.where(core == 0, mask_even, mask_odd)

        def note(place, seen):
            start = starts_ref[source * size_key + (own_ka ^ place)]
            visible = start < own_start

            @pl.when(visible)
            def _():
                order_ref[seen] = place

            return seen + visible.astype(jnp.int32)

        seen = lax.fori_loop(0, size_key, note, jnp.int32(0))

        def many(index, _):
            update(ref, [order_ref[index * STEP + at] for at in range(STEP)])
            return 0

        lax.fori_loop(0, seen // STEP, many, 0)
        left = seen % STEP
        done = seen - left
        width = STEP // 2
        while width:

            @pl.when((left & width) != 0)
            def _():
                base = done + (left & ~(2 * width - 1))
                update(ref, [order_ref[base + at] for at in range(width)])

            width //= 2

    if last:
        (out_ref,) = outs
        for head in range(heads):
            rows = slice(head * token, (head + 1) * token)
            total = jnp.sum(state[1][rows, :], axis=1, keepdims=True)
            out_ref[:, head * HD : (head + 1) * HD] = state[2][rows, :] / total


def attend(starts, queries, blocks, state, size_key, last):
    token, width = queries.shape
    rows = width // HD * token
    buffers, masks = zip(*blocks)
    sums = [jax.ShapeDtypeStruct((rows, HD), jnp.float32)] * 3
    scratch = [pltpu.VMEM((rows, HD), jnp.bfloat16), pltpu.SMEM((size_key,), jnp.int32)]
    if last:
        scratch += [pltpu.VMEM((rows, HD), jnp.float32)] * 3
    kernel = functools.partial(attend_kernel, masks, state is None, last, size_key, token)
    operands = [queries, *buffers] + ([starts, *state] if state else [])
    result = pl.pallas_call(
        kernel,
        out_shape=[jax.ShapeDtypeStruct((token, width), jnp.float32)] if last else sums,
        in_specs=[SMEM if operand is starts else VMEM for operand in operands],
        out_specs=[VMEM] if last else [VMEM] * 3,
        scratch_shapes=scratch,
        compiler_params=pltpu.CompilerParams(vmem_limit_bytes=LIMIT),
        cost_estimate=pl.CostEstimate(
            flops=6 * rows * HD * token * size_key * len(buffers),
            transcendentals=rows * token * size_key * len(buffers),
            bytes_accessed=1 << 20,
        ),
    )(*operands)
    return result[0] if last else tuple(result)


def move(array, mask_even, mask_odd, place):
    size_query, size_key = lax.axis_size("pb"), lax.axis_size("ka")
    pairs = []
    for query in range(size_query):
        source = query ^ (mask_odd if query % 2 else mask_even)
        for key in range(size_key):
            pairs.append((source * size_key + (key ^ place), query * size_key + key))
    return lax.ppermute(array, AXES, pairs)


def stages(size_query):
    bits = [1 << at for at in range(1, size_query.bit_length() - 1)]
    return [bits[at : at + 2] for at in range(0, len(bits), 2)]


def swap(item):
    array, (even, odd) = item
    return move(array, 1, 1, 0), (1 ^ odd, 1 ^ even)


def gathered_attention(queries, keys, values, positions):
    token = queries.shape[0]
    size_query, size_key = lax.axis_size("pb"), lax.axis_size("ka")
    assert size_query & (size_query - 1) == 0 and size_key & (size_key - 1) == 0
    starts = positions.reshape(-1, token)[:, 0]
    own = jnp.concatenate([keys, values], axis=0)
    others = [move(own, 0, 0, place) for place in range(1, size_key)]
    column = jnp.concatenate([own] + others, axis=0)

    held = [(column, (0, 0))]
    groups = [[(own, (0, 0))], [held[0], swap(held[0])]]
    for bits in stages(size_query):
        one, two = bits[0], bits[-1]
        near, far = [], []
        for array, (even, odd) in held:
            first = move(array, one, two, 0)
            near.append((first, (even ^ one, odd ^ two)))
            if one != two:
                second = move(array, two, one, 0)
                near.append((second, (even ^ two, odd ^ one)))
                both = one ^ two
                far.append((move(first, two, one, 0), (even ^ both, odd ^ both)))
        held += near + far
        swapped = [swap(item) for item in near]
        groups.append(near)
        groups.append(swapped + far)
        if far:
            groups.append([swap(item) for item in far])

    state = None
    for at, group in enumerate(groups):
        state = attend(starts, queries, group, state, size_key, at == len(groups) - 1)
    return state


def solution(mesh):
    return jax.shard_map(
        gathered_attention,
        mesh=mesh,
        in_specs=(P(AXES, None), P(AXES, None), P(AXES, None), P()),
        out_specs=P(AXES, None),
        check_vma=False,
    )
```

profile of v0, /device:TPU:0, one launch (start us, length us, event | category | flops | bytes accessed | tf_op | source)
XLA Modules:
  0.0 44.2 jit_solution(4406794368948357608)
XLA Ops:
  0.0 0.8 %constant_dynamic-update-slice_fusion.1 = (bf16[256,128]{1,0:T(8,128)(2,1)S(1)}, bf16[1024,128]{1,0:T(8,128)(2,1)S(1)}) fusion(bf16[128,128]{1,0:T(8,128)(2,1)} %param.5), kind=kLoop, calls=%fused_computation.2 | loop fusion | bytes 98304
  0.8 0.0 copy-start
  0.8 3.1 %collective-permute-start = (bf16[256,128]{1,0:T(8,128)(2,1)S(1)}, bf16[256,128]{1,0:T(8,128)(2,1)S(1)}, u32[]{:S(2)}, u32[]{:S(2)}) collective-permute-start(bf16[256,128]{1,0:T(8,128)(2,1)S(1)} %get-tuple-element.29.refs_1_), channel_id=1, source_target_pairs={{1,0},{0,1},{3,2},{2,3},{5,4},{4,5},{7,6},{6,7},{9,8},{8,9},{11,10... | collective-permute-start | bytes 196616 | tf_op jit(solution)/shard_map/ppermute | solution.py:180
  3.9 2.6 %collective-permute-start.1 = (bf16[256,128]{1,0:T(8,128)(2,1)S(1)}, bf16[256,128]{1,0:T(8,128)(2,1)S(1)}, u32[]{:S(2)}, u32[]{:S(2)}) collective-permute-start(bf16[256,128]{1,0:T(8,128)(2,1)S(1)} %get-tuple-element.29.refs_1_), channel_id=1, source_target_pairs={{2,0},{3,1},{0,2},{1,3},{6,4},{7,5},{4,6},{5,7},{10,8},{11,9},{8,1... | collective-permute-start | bytes 196616 | tf_op jit(solution)/shard_map/ppermute | solution.py:180
  6.5 0.0 collective-permute-start.2
  6.5 4.7 %collective-permute-done.1 = bf16[256,128]{1,0:T(8,128)(2,1)S(1)} collective-permute-done((bf16[256,128]{1,0:T(8,128)(2,1)S(1)}, bf16[256,128]{1,0:T(8,128)(2,1)S(1)}, u32[]{:S(2)}, u32[]{:S(2)}) %collective-permute-start.1) | collective-permute-done | bytes 65568 | tf_op jit(solution)/shard_map/ppermute | solution.py:180
  11.2 1.4 %collective-permute-done.2 = bf16[256,128]{1,0:T(8,128)(2,1)S(1)} collective-permute-done((bf16[256,128]{1,0:T(8,128)(2,1)S(1)}, bf16[256,128]{1,0:T(8,128)(2,1)S(1)}, u32[]{:S(2)}, u32[]{:S(2)}) %collective-permute-start.2) | collective-permute-done | bytes 65568 | tf_op jit(solution)/shard_map/ppermute | solution.py:180
  12.6 0.0 copy-start.2
  12.6 1.6 %collective-permute-start.3 = (bf16[1024,128]{1,0:T(8,128)(2,1)S(1)}, bf16[1024,128]{1,0:T(8,128)(2,1)S(1)}, u32[]{:S(2)}, u32[]{:S(2)}) collective-permute-start(bf16[1024,128]{1,0:T(8,128)(2,1)S(1)} %constant_dynamic-update-slice_fusion.2.refs_1_), channel_id=1, source_target_pairs={{8,0},{9,1},{10,2},{11,3},{20,4},{21,5},{22,6},{23,7},{0,8},{1,9},... | collective-permute-start | bytes 786440 | tf_op jit(solution)/shard_map/ppermute | solution.py:180
  14.2 1.5 %collective-permute-start.7 = (bf16[1024,128]{1,0:T(8,128)(2,1)S(1)}, bf16[1024,128]{1,0:T(8,128)(2,1)S(1)}, u32[]{:S(2)}, u32[]{:S(2)}) collective-permute-start(bf16[1024,128]{1,0:T(8,128)(2,1)S(1)} %constant_dynamic-update-slice_fusion.2.refs_1_), channel_id=1, source_target_pairs={{16,0},{17,1},{18,2},{19,3},{12,4},{13,5},{14,6},{15,7},{24,8},{25... | collective-permute-start | bytes 786440 | tf_op jit(solution)/shard_map/ppermute | solution.py:180
  15.7 6.0 %collective-permute-done.3.refs_1_ = bf16[1024,128]{1,0:T(8,128)(2,1)S(1)} collective-permute-done((bf16[1024,128]{1,0:T(8,128)(2,1)S(1)}, bf16[1024,128]{1,0:T(8,128)(2,1)S(1)}, u32[]{:S(2)}, u32[]{:S(2)}) %collective-permute-start.3) | collective-permute-done | bytes 262176 | tf_op jit(solution)/shard_map/ppermute | solution.py:180
  21.7 0.0 collective-permute-start.4
  21.7 0.0 collective-permute-start.9
  21.7 0.6 %shard_map.46 = (f32[1024,128]{1,0:T(8,128)S(1)}, f32[1024,128]{1,0:T(8,128)S(1)}, f32[1024,128]{1,0:T(8,128)S(1)}) custom-call(bf16[128,1024]{1,0:T(8,128)(2,1)S(1)} %copy-done, bf16[256,128]{1,0:T(8,128)(2,1)S(1)} %get-tuple-element.29.refs_1_), custom_call_target="tpu_custom_call" | custom-call | flops 402653184 | bytes 1048576 | tf_op jit(solution)/shard_map/pallas_call | solution.py:157
  22.3 0.6 %collective-permute-start.6 = (bf16[1024,128]{1,0:T(8,128)(2,1)S(1)}, bf16[1024,128]{1,0:T(8,128)(2,1)S(1)}, u32[]{:S(2)}, u32[]{:S(2)}) collective-permute-start(bf16[1024,128]{1,0:T(8,128)(2,1)S(1)} %collective-permute-done.3.refs_1_), channel_id=1, source_target_pairs={{4,0},{5,1},{6,2},{7,3},{0,4},{1,5},{2,6},{3,7},{12,8},{13,9},{14,... | collective-permute-start | bytes 786440 | tf_op jit(solution)/shard_map/ppermute | solution.py:180
  22.9 0.1 collective-permute-start.8
  23.0 0.1 slice_reduce_fusion.refs_3_.refs_4_.refs_2_
  23.1 5.0 %collective-permute-done.4.refs_3_ = bf16[1024,128]{1,0:T(8,128)(2,1)S(1)} collective-permute-done((bf16[1024,128]{1,0:T(8,128)(2,1)S(1)}, bf16[1024,128]{1,0:T(8,128)(2,1)S(1)}, u32[]{:S(2)}, u32[]{:S(2)}) %collective-permute-start.4) | collective-permute-done | bytes 262176 | tf_op jit(solution)/shard_map/ppermute | solution.py:180
  28.1 0.0 collective-permute-start.5
  28.1 3.9 %shard_map.47 = (f32[1024,128]{1,0:T(8,128)S(1)}, f32[1024,128]{1,0:T(8,128)S(1)}, f32[1024,128]{1,0:T(8,128)S(1)}) custom-call(bf16[128,1024]{1,0:T(8,128)(2,1)S(1)} %copy-done, bf16[1024,128]{1,0:T(8,128)(2,1)S(1)} %constant_dynamic-update-slice_fusion.2.refs_1_, bf16[1024,128]{1,0:T(8,128)(2,1)S(1)} %collective-permute-done.9.refs_2_, ...), custom_call_target="tpu_custom_call" | custom-call | flops 805306368 | bytes 1048576 | tf_op jit(solution)/shard_map/pallas_call | solution.py:157
  32.0 3.7 %shard_map.48 = (f32[1024,128]{1,0:T(8,128)S(1)}, f32[1024,128]{1,0:T(8,128)S(1)}, f32[1024,128]{1,0:T(8,128)S(1)}) custom-call(bf16[128,1024]{1,0:T(8,128)(2,1)S(1)} %copy-done, bf16[1024,128]{1,0:T(8,128)(2,1)S(1)} %collective-permute-done.3.refs_1_, bf16[1024,128]{1,0:T(8,128)(2,1)S(1)} %collective-permute-done.7.refs_2_, ...), custom_call_target="tpu_custom_call" | custom-call | flops 805306368 | bytes 1048576 | tf_op jit(solution)/shard_map/pallas_call | solution.py:157
  35.6 0.0 collective-permute-done.6.refs_1_
  35.7 5.5 %shard_map.49 = (f32[1024,128]{1,0:T(8,128)S(1)}, f32[1024,128]{1,0:T(8,128)S(1)}, f32[1024,128]{1,0:T(8,128)S(1)}) custom-call(bf16[128,1024]{1,0:T(8,128)(2,1)S(1)} %copy-done, bf16[1024,128]{1,0:T(8,128)(2,1)S(1)} %collective-permute-done.6.refs_1_, bf16[1024,128]{1,0:T(8,128)(2,1)S(1)} %collective-permute-done.8.refs_2_, ...), custom_call_target="tpu_custom_call" | custom-call | flops 1207959552 | bytes 1048576 | tf_op jit(solution)/shard_map/pallas_call | solution.py:157
  41.1 3.1 %shard_map.50 = f32[128,1024]{1,0:T(8,128)} custom-call(bf16[128,1024]{1,0:T(8,128)(2,1)S(1)} %copy-done, bf16[1024,128]{1,0:T(8,128)(2,1)S(1)} %collective-permute-done.5.refs_1_, s32[32]{0:T(128)S(1)} %slice_reduce_fusion.refs_3_.refs_4_.refs_2_, f32[1024,128]{1,0:T(8,128)S(1)} %get-tuple-element.26.refs_3_, f32[1024,128]{1,0:T(8,128)S(1)} %get-tuple-element.27.refs_4_, ...), custom_call_target="tpu_custom_call" | custom-call | flops 402653184 | bytes 1048576 | tf_op jit(solution)/shard_map/pallas_call | solution.py:157
  (13 shorter events, 0.1 us)
Async XLA Ops:
  0.0 0.8 %copy-start.1 = (bf16[128,128]{1,0:T(8,128)(2,1)S(1)}, bf16[128,128]{1,0:T(8,128)(2,1)}, u32[]{:S(2)}) copy-start(bf16[128,128]{1,0:T(8,128)(2,1)} %param.6) | copy-start | bytes 98308
  0.8 20.9 %copy-start = (bf16[128,1024]{1,0:T(8,128)(2,1)S(1)}, bf16[128,1024]{1,0:T(8,128)(2,1)}, u32[]{:S(2)}) copy-start(bf16[128,1024]{1,0:T(8,128)(2,1)} %refs_0_.9) | copy-start | bytes 786436
  0.8 5.7 %collective-permute-start = (bf16[256,128]{1,0:T(8,128)(2,1)S(1)}, bf16[256,128]{1,0:T(8,128)(2,1)S(1)}, u32[]{:S(2)}, u32[]{:S(2)}) collective-permute-start(bf16[256,128]{1,0:T(8,128)(2,1)S(1)} %get-tuple-element.29.refs_1_), channel_id=1, source_target_pairs={{1,0},{0,1},{3,2},{2,3},{5,4},{4,5},{7,6},{6,7},{9,8},{8,9},{11,10... | collective-permute-start | bytes 196616 | tf_op jit(solution)/shard_map/ppermute | solution.py:180
  3.9 7.3 %collective-permute-start.1 = (bf16[256,128]{1,0:T(8,128)(2,1)S(1)}, bf16[256,128]{1,0:T(8,128)(2,1)S(1)}, u32[]{:S(2)}, u32[]{:S(2)}) collective-permute-start(bf16[256,128]{1,0:T(8,128)(2,1)S(1)} %get-tuple-element.29.refs_1_), channel_id=1, source_target_pairs={{2,0},{3,1},{0,2},{1,3},{6,4},{7,5},{4,6},{5,7},{10,8},{11,9},{8,1... | collective-permute-start | bytes 196616 | tf_op jit(solution)/shard_map/ppermute | solution.py:180
  6.5 6.1 %collective-permute-start.2 = (bf16[256,128]{1,0:T(8,128)(2,1)S(1)}, bf16[256,128]{1,0:T(8,128)(2,1)S(1)}, u32[]{:S(2)}, u32[]{:S(2)}) collective-permute-start(bf16[256,128]{1,0:T(8,128)(2,1)S(1)} %get-tuple-element.29.refs_1_), channel_id=1, source_target_pairs={{3,0},{2,1},{1,2},{0,3},{7,4},{6,5},{5,6},{4,7},{11,8},{10,9},{9,1... | collective-permute-start | bytes 196616 | tf_op jit(solution)/shard_map/ppermute | solution.py:180
  12.6 10.4 %copy-start.2 = (s32[4096]{0:T(1024)S(1)}, s32[4096]{0:T(1024)}, u32[]{:S(2)}) copy-start(s32[4096]{0:T(1024)} %param.7) | copy-start | bytes 49156
  12.6 9.1 %collective-permute-start.3 = (bf16[1024,128]{1,0:T(8,128)(2,1)S(1)}, bf16[1024,128]{1,0:T(8,128)(2,1)S(1)}, u32[]{:S(2)}, u32[]{:S(2)}) collective-permute-start(bf16[1024,128]{1,0:T(8,128)(2,1)S(1)} %constant_dynamic-update-slice_fusion.2.refs_1_), channel_id=1, source_target_pairs={{8,0},{9,1},{10,2},{11,3},{20,4},{21,5},{22,6},{23,7},{0,8},{1,9},... | collective-permute-start | bytes 786440 | tf_op jit(solution)/shard_map/ppermute | solution.py:180
  14.2 8.7 %collective-permute-start.7 = (bf16[1024,128]{1,0:T(8,128)(2,1)S(1)}, bf16[1024,128]{1,0:T(8,128)(2,1)S(1)}, u32[]{:S(2)}, u32[]{:S(2)}) collective-permute-start(bf16[1024,128]{1,0:T(8,128)(2,1)S(1)} %constant_dynamic-update-slice_fusion.2.refs_1_), channel_id=1, source_target_pairs={{16,0},{17,1},{18,2},{19,3},{12,4},{13,5},{14,6},{15,7},{24,8},{25... | collective-permute-start | bytes 786440 | tf_op jit(solution)/shard_map/ppermute | solution.py:180
  21.7 6.4 %collective-permute-start.4 = (bf16[1024,128]{1,0:T(8,128)(2,1)S(1)}, bf16[1024,128]{1,0:T(8,128)(2,1)S(1)}, u32[]{:S(2)}, u32[]{:S(2)}) collective-permute-start(bf16[1024,128]{1,0:T(8,128)(2,1)S(1)} %collective-permute-done.3.refs_1_), channel_id=1, source_target_pairs={{16,0},{17,1},{18,2},{19,3},{12,4},{13,5},{14,6},{15,7},{24,8},{25... | collective-permute-start | bytes 786440 | tf_op jit(solution)/shard_map/ppermute | solution.py:180
  21.7 6.4 %collective-permute-start.9 = (bf16[1024,128]{1,0:T(8,128)(2,1)S(1)}, bf16[1024,128]{1,0:T(8,128)(2,1)S(1)}, u32[]{:S(2)}, u32[]{:S(2)}) collective-permute-start(bf16[1024,128]{1,0:T(8,128)(2,1)S(1)} %constant_dynamic-update-slice_fusion.2.refs_1_), channel_id=1, source_target_pairs={{4,0},{5,1},{6,2},{7,3},{0,4},{1,5},{2,6},{3,7},{12,8},{13,9},{14,... | collective-permute-start | bytes 786440 | tf_op jit(solution)/shard_map/ppermute | solution.py:180
  22.3 13.3 %collective-permute-start.6 = (bf16[1024,128]{1,0:T(8,128)(2,1)S(1)}, bf16[1024,128]{1,0:T(8,128)(2,1)S(1)}, u32[]{:S(2)}, u32[]{:S(2)}) collective-permute-start(bf16[1024,128]{1,0:T(8,128)(2,1)S(1)} %collective-permute-done.3.refs_1_), channel_id=1, source_target_pairs={{4,0},{5,1},{6,2},{7,3},{0,4},{1,5},{2,6},{3,7},{12,8},{13,9},{14,... | collective-permute-start | bytes 786440 | tf_op jit(solution)/shard_map/ppermute | solution.py:180
  22.9 12.7 %collective-permute-start.8 = (bf16[1024,128]{1,0:T(8,128)(2,1)S(1)}, bf16[1024,128]{1,0:T(8,128)(2,1)S(1)}, u32[]{:S(2)}, u32[]{:S(2)}) collective-permute-start(bf16[1024,128]{1,0:T(8,128)(2,1)S(1)} %collective-permute-done.7.refs_2_), channel_id=1, source_target_pairs={{4,0},{5,1},{6,2},{7,3},{0,4},{1,5},{2,6},{3,7},{12,8},{13,9},{14,... | collective-permute-start | bytes 786440 | tf_op jit(solution)/shard_map/ppermute | solution.py:180
  28.1 13.1 %collective-permute-start.5 = (bf16[1024,128]{1,0:T(8,128)(2,1)S(1)}, bf16[1024,128]{1,0:T(8,128)(2,1)S(1)}, u32[]{:S(2)}, u32[]{:S(2)}) collective-permute-start(bf16[1024,128]{1,0:T(8,128)(2,1)S(1)} %collective-permute-done.4.refs_3_), channel_id=1, source_target_pairs={{4,0},{5,1},{6,2},{7,3},{0,4},{1,5},{2,6},{3,7},{12,8},{13,9},{14,... | collective-permute-start | bytes 786440 | tf_op jit(solution)/shard_map/ppermute | solution.py:180
where the time goes:
time: 44.4 us; the launch traced here: 44.2 us
  waiting for transfers between devices  17 us (38%)
  Pallas kernels  16.7 us (38%)
  starting transfers between devices  9.45 us (21%)
  local copies, waits for them, and re-layouts  0.95 us (2%)
    ppermute x10, waiting for transfers between devices, move(): return lax.ppermute(array, AXES, pairs)  17 us
    pallas_call x5, Pallas kernels, attend(): pl.pallas_call(kernel, out_shape=[jax.ShapeDtypeStruct((token, width), jn...  16.7 us
    ppermute x10, starting transfers between devices, move(): return lax.ppermute(array, AXES, pairs)  9.45 us
  transfers between devices with their start and end apart: 10, of which 4 were waited for; matrix products, arithmetic and copies ran while one was open for 0% of the time, Pallas kernels for 31%

commit v1 on v0

v1 whole, which is shorter than its diff:
```python
import functools
import math

import jax
import jax.numpy as jnp
from jax import lax
from jax.experimental import pallas as pl
from jax.experimental.pallas import tpu as pltpu
from jax.sharding import PartitionSpec as P


HD = 128
AXES = ("pb", "ka")
BIG = -1e30
STEP = 4
LIMIT = 24 << 20

VMEM = pl.BlockSpec(memory_space=pltpu.VMEM)
SMEM = pl.BlockSpec(memory_space=pltpu.SMEM)


def combine(rows, keys, values, sums, to_log2, mask=None):
    score = lax.dot_general(
        rows, keys, (((1,), (1,)), ((), ())), preferred_element_type=jnp.float32
    )
    if mask is not None:
        score = jnp.where(mask, score, BIG)
    parts = [score[:, at : at + HD] for at in range(0, keys.shape[0], HD)]
    top = jnp.max(functools.reduce(jnp.maximum, parts), axis=1, keepdims=True)
    if sums is None:
        top = jnp.broadcast_to(top, (rows.shape[0], HD))
    else:
        top = jnp.maximum(sums[0], top)
    weights = [jnp.exp2((part - top) * to_log2) for part in parts]
    if mask is not None:
        weights = [jnp.where(mask, weight, 0.0) for weight in weights]
    total = functools.reduce(jnp.add, weights)
    weight = jnp.concatenate(weights, axis=1) if len(weights) > 1 else weights[0]
    high = weight.astype(jnp.bfloat16)
    low = (weight - high.astype(jnp.float32)).astype(jnp.bfloat16)
    over = (((1,), (0,)), ((), ()))
    result = lax.dot_general(high, values, over, preferred_element_type=jnp.float32)
    result += lax.dot_general(low, values, over, preferred_element_type=jnp.float32)
    if sums is None:
        return top, total, result
    largest, totals, summed = sums
    factor = jnp.exp2((largest - top) * to_log2)
    return top, totals * factor + total, summed * factor + result


TO_LOG2 = math.log2(math.e) / HD**0.5


def own_kernel(queries_ref, own_ref, rows_ref, largest_ref, totals_ref, summed_ref):
    token, width = queries_ref.shape
    heads = width // HD
    for head in range(heads):
        rows_ref[head * token : (head + 1) * token, :] = queries_ref[:, head * HD : (head + 1) * HD]
    shape = (heads, token, token)
    causal = lax.broadcasted_iota(jnp.int32, shape, 2) <= lax.broadcasted_iota(jnp.int32, shape, 1)
    keys, values = own_ref[:token, :], own_ref[token:, :]
    mask = causal.reshape(heads * token, token)
    new = combine(rows_ref[...], keys, values, None, TO_LOG2, mask)
    for held, value in zip((largest_ref, totals_ref, summed_ref), new):
        held[...] = value


def attend_kernel(pieces, last, size_key, token, *refs):
    count = len(pieces)
    starts_ref, rows_ref = refs[:2]
    block_refs = refs[2 : 2 + count]
    outs, (keys_ref, values_ref) = refs[5 + count : -2], refs[-2:]
    state = outs[:3]
    own_pb, own_ka = lax.axis_index("pb"), lax.axis_index("ka")
    own_start = starts_ref[own_pb * size_key + own_ka]
    core = own_pb % 2

    seen = jnp.int32(0)
    for ref, (base, mask_even, mask_odd) in zip(block_refs, pieces):
        source = (own_pb ^ jnp.where(core == 0, mask_even, mask_odd)) * size_key

        def note(at, seen):
            visible = starts_ref[source + (own_ka ^ (base + at))] < own_start

            @pl.when(visible)
            def _():
                target = pl.ds(pl.multiple_of(seen * token, token), token)
                offset = pl.multiple_of(at * 2 * token, token)
                keys_ref[target, :] = ref[pl.ds(offset, token), :]
                values_ref[target, :] = ref[pl.ds(offset + token, token), :]

            return seen + visible.astype(jnp.int32)

        seen = lax.fori_loop(0, ref.shape[0] // (2 * token), note, seen)

    def update(first, number):
        part = pl.ds(pl.multiple_of(first * token, token), number * token)
        sums = [held[...] for held in state]
        new = combine(rows_ref[...], keys_ref[part, :], values_ref[part, :], sums, TO_LOG2)
        for held, value in zip(state, new):
            held[...] = value

    def many(index, _):
        update(index * STEP, STEP)
        return 0

    lax.fori_loop(0, seen // STEP, many, 0)
    left = seen % STEP
    done = seen - left
    number = STEP // 2
    while number:
        pl.when((left & number) != 0)(
            functools.partial(update, done + (left & ~(2 * number - 1)), number)
        )
        number //= 2

    if last:
        out_ref = outs[3]
        for head in range(out_ref.shape[1] // HD):
            rows = slice(head * token, (head + 1) * token)
            total = jnp.sum(state[1][rows, :], axis=1, keepdims=True)
            out_ref[:, head * HD : (head + 1) * HD] = state[2][rows, :] / total


def params(rows, token, blocks):
    return dict(
        compiler_params=pltpu.CompilerParams(vmem_limit_bytes=LIMIT),
        cost_estimate=pl.CostEstimate(
            flops=6 * rows * HD * token * blocks,
            transcendentals=rows * token * blocks,
            bytes_accessed=1 << 20,
        ),
    )


def attend_own(queries, own):
    token, width = queries.shape
    rows = width // HD * token
    sums = jax.ShapeDtypeStruct((rows, HD), jnp.float32)
    return pl.pallas_call(
        own_kernel,
        out_shape=[jax.ShapeDtypeStruct((rows, HD), jnp.bfloat16), sums, sums, sums],
        in_specs=[VMEM] * 2,
        out_specs=[VMEM] * 4,
        **params(rows, token, 1),
    )(queries, own)


def attend(starts, state, items, size_key, shape, last):
    token, width = shape
    rows = width // HD * token
    arrays, pieces = zip(*items)
    blocks = sum(array.shape[0] for array in arrays) // (2 * token)
    outs = [jax.ShapeDtypeStruct((rows, HD), jnp.float32)] * 3
    if last:
        outs.append(jax.ShapeDtypeStruct(shape, jnp.float32))
    operands = [starts, state[0], *arrays, *state[1:]]
    result = pl.pallas_call(
        functools.partial(attend_kernel, pieces, last, size_key, token),
        out_shape=outs,
        in_specs=[SMEM] + [VMEM] * (len(operands) - 1),
        out_specs=[VMEM] * len(outs),
        input_output_aliases={2 + len(arrays) + at: at for at in range(3)},
        scratch_shapes=[pltpu.VMEM((blocks * token, HD), jnp.bfloat16)] * 2,
        **params(rows, token, blocks),
    )(*operands)
    return result[3] if last else (state[0], *result)


def move(array, mask_even, mask_odd, place):
    size_query, size_key = lax.axis_size("pb"), lax.axis_size("ka")
    pairs = []
    for query in range(size_query):
        source = query ^ (mask_odd if query % 2 else mask_even)
        for key in range(size_key):
            pairs.append((source * size_key + (key ^ place), query * size_key + key))
    return lax.ppermute(array, AXES, pairs)


def stages(size_query):
    bits = [1 << at for at in range(1, size_query.bit_length() - 1)]
    return [bits[at : at + 2] for at in range(0, len(bits), 2)]


def paired(size_query, size_key):
    plan = stages(size_query)
    return len(plan) == 1 and len(plan[0]) == 2 and size_key > 1


def swap(item):
    array, (base, even, odd) = item
    return move(array, 1, 1, 0), (base, 1 ^ odd, 1 ^ even)


def spread(item, bits):
    array, (base, even, odd) = item
    one, two = bits[0], bits[-1]
    first = move(array, one, two, 0)
    near = [(first, (base, even ^ one, odd ^ two))]
    if one == two:
        return near, []
    second = move(array, two, one, 0)
    near.append((second, (base, even ^ two, odd ^ one)))
    both = one ^ two
    third = move(first, two, one, 0)
    return near, [(third, (base, even ^ both, odd ^ both))]


def gathered_attention(queries, keys, values, positions):
    token = queries.shape[0]
    size_query, size_key = lax.axis_size("pb"), lax.axis_size("ka")
    assert size_query & (size_query - 1) == 0 and size_key & (size_key - 1) == 0
    starts = positions.reshape(-1, token)[:, 0]
    own = jnp.concatenate([keys, values], axis=0)
    column = [own] + [move(own, 0, 0, place) for place in range(1, size_key)]
    half = max(size_key // 2, 1)
    held = [
        (jnp.concatenate(column[base : base + half], axis=0), (base, 0, 0))
        for base in range(0, size_key, half)
    ]

    state = attend_own(queries, own)
    groups = []
    plan = stages(size_query)
    if paired(size_query, size_key):
        (lower, upper), bits = held, plan[0]
        near, far = spread(lower, bits)
        near_up, far_up = spread(upper, bits)
        groups.append([lower, swap(lower)])
        groups.append(near + [swap(item) for item in near])
        groups.append([upper, swap(upper)] + far + [swap(item) for item in far])
        groups.append(near_up)
        groups.append([swap(item) for item in near_up] + far_up)
        groups.append([swap(item) for item in far_up])
    else:
        groups.append(held + [swap(item) for item in held])
        for bits in plan:
            near, far = [], []
            for item in held:
                more_near, more_far = spread(item, bits)
                near += more_near
                far += more_far
            groups.append(near)
            groups.append([swap(item) for item in near] + far)
            if far:
                groups.append([swap(item) for item in far])
            held += near + far

    for at, group in enumerate(groups):
        state = attend(starts, state, group, size_key, queries.shape, at == len(groups) - 1)
    return state


def solution(mesh):
    return jax.shard_map(
        gathered_attention,
        mesh=mesh,
        in_specs=(P(AXES, None), P(AXES, None), P(AXES, None), P()),
        out_specs=P(AXES, None),
        check_vma=False,
    )
```

time: 44.4 us -> 37.9 us (0.85)
  waiting for transfers between devices: 17 us -> 5.76 us
  starting transfers between devices: 9.45 us -> 15.3 us
  Pallas kernels: 16.7 us -> 15.6 us
    ppermute x10 -> x17, waiting for transfers between devices: 17 us -> 5.76 us  [move(): return lax.ppermute(array, AXES, pairs)]
    ppermute x10 -> x17, starting transfers between devices: 9.45 us -> 15.3 us  [move(): return lax.ppermute(array, AXES, pairs)]
    pallas_call x5 -> x7, Pallas kernels: 16.7 us -> 15.6 us  [the longest x6 14.9 us: attend(): pl.pallas_call(functools.partial(attend_kernel, pieces, last, size_key, t...]
  transfers between devices with their start and end apart: 10 -> 17, of which waited for: 4 -> 5; matrix products, arithmetic and copies ran while one was open for 0% -> 0% of each run, Pallas kernels for 31% -> 35%
where the time goes in v1:
time: 37.9 us; the launch traced here: 37.7 us
  Pallas kernels  15.6 us (41%)
  starting transfers between devices  15.3 us (40%)
  waiting for transfers between devices  5.76 us (15%)
  local copies, waits for them, and re-layouts  0.94 us (2%)
    ppermute x17, starting transfers between devices, move(): return lax.ppermute(array, AXES, pairs)  15.3 us
    pallas_call x6, Pallas kernels, attend(): pl.pallas_call(functools.partial(attend_kernel, pieces, last, size_key, t...  14.9 us
    ppermute x17, waiting for transfers between devices, move(): return lax.ppermute(array, AXES, pairs)  5.76 us
    unnamed x9, local copies, waits for them, and re-layouts  0.81 us
  transfers between devices with their start and end apart: 17, of which 5 were waited for; matrix products, arithmetic and copies ran while one was open for 0% of the time, Pallas kernels for 35%

profile of v1, /device:TPU:0, one launch (start us, length us, event | category | flops | bytes accessed | tf_op | source)
XLA Modules:
  0.0 37.7 jit_solution(15750226786247371286)
XLA Ops:
  0.0 0.8 %constant_dynamic-update-slice_fusion.6 = (bf16[512,128]{1,0:T(8,128)(2,1)S(1)}, bf16[256,128]{1,0:T(8,128)(2,1)S(1)}) fusion(bf16[128,128]{1,0:T(8,128)(2,1)} %param.5), kind=kLoop, calls=%fused_computation.7 | loop fusion | bytes 98304
  0.8 3.1 %collective-permute-start.9 = (bf16[256,128]{1,0:T(8,128)(2,1)S(1)}, bf16[256,128]{1,0:T(8,128)(2,1)S(1)}, u32[]{:S(2)}, u32[]{:S(2)}) collective-permute-start(bf16[256,128]{1,0:T(8,128)(2,1)S(1)} %get-tuple-element.46.own_ref), channel_id=1, source_target_pairs={{1,0},{0,1},{3,2},{2,3},{5,4},{4,5},{7,6},{6,7},{9,8},{8,9},{11,10... | collective-permute-start | bytes 196616 | tf_op jit(solution)/shard_map/ppermute | solution.py:177
  3.9 2.6 %collective-permute-start = (bf16[256,128]{1,0:T(8,128)(2,1)S(1)}, bf16[256,128]{1,0:T(8,128)(2,1)S(1)}, u32[]{:S(2)}, u32[]{:S(2)}) collective-permute-start(bf16[256,128]{1,0:T(8,128)(2,1)S(1)} %get-tuple-element.46.own_ref), channel_id=1, source_target_pairs={{2,0},{3,1},{0,2},{1,3},{6,4},{7,5},{4,6},{5,7},{10,8},{11,9},{8,1... | collective-permute-start | bytes 196616 | tf_op jit(solution)/shard_map/ppermute | solution.py:177
  6.6 1.8 %collective-permute-start.10 = (bf16[512,128]{1,0:T(8,128)(2,1)S(1)}, bf16[512,128]{1,0:T(8,128)(2,1)S(1)}, u32[]{:S(2)}, u32[]{:S(2)}) collective-permute-start(bf16[512,128]{1,0:T(8,128)(2,1)S(1)} %constant_dynamic-update-slice_fusion.4.refs_2_), channel_id=1, source_target_pairs={{8,0},{9,1},{10,2},{11,3},{20,4},{21,5},{22,6},{23,7},{0,8},{1,9},... | collective-permute-start | bytes 393224 | tf_op jit(solution)/shard_map/ppermute | solution.py:177
  8.4 1.5 %collective-permute-start.13 = (bf16[512,128]{1,0:T(8,128)(2,1)S(1)}, bf16[512,128]{1,0:T(8,128)(2,1)S(1)}, u32[]{:S(2)}, u32[]{:S(2)}) collective-permute-start(bf16[512,128]{1,0:T(8,128)(2,1)S(1)} %constant_dynamic-update-slice_fusion.4.refs_2_), channel_id=1, source_target_pairs={{16,0},{17,1},{18,2},{19,3},{12,4},{13,5},{14,6},{15,7},{24,8},{25... | collective-permute-start | bytes 393224 | tf_op jit(solution)/shard_map/ppermute | solution.py:177
  9.9 1.3 %collective-permute-done = bf16[256,128]{1,0:T(8,128)(2,1)S(1)} collective-permute-done((bf16[256,128]{1,0:T(8,128)(2,1)S(1)}, bf16[256,128]{1,0:T(8,128)(2,1)S(1)}, u32[]{:S(2)}, u32[]{:S(2)}) %collective-permute-start) | collective-permute-done | bytes 65568 | tf_op jit(solution)/shard_map/ppermute | solution.py:177
  11.2 1.4 %collective-permute-done.1 = bf16[256,128]{1,0:T(8,128)(2,1)S(1)} collective-permute-done((bf16[256,128]{1,0:T(8,128)(2,1)S(1)}, bf16[256,128]{1,0:T(8,128)(2,1)S(1)}, u32[]{:S(2)}, u32[]{:S(2)}) %collective-permute-start.1) | collective-permute-done | bytes 65568 | tf_op jit(solution)/shard_map/ppermute | solution.py:177
  12.6 1.6 %collective-permute-start.2 = (bf16[512,128]{1,0:T(8,128)(2,1)S(1)}, bf16[512,128]{1,0:T(8,128)(2,1)S(1)}, u32[]{:S(2)}, u32[]{:S(2)}) collective-permute-start(bf16[512,128]{1,0:T(8,128)(2,1)S(1)} %constant_dynamic-update-slice_fusion.2.refs_2_), channel_id=1, source_target_pairs={{8,0},{9,1},{10,2},{11,3},{20,4},{21,5},{22,6},{23,7},{0,8},{1,9},... | collective-permute-start | bytes 393224 | tf_op jit(solution)/shard_map/ppermute | solution.py:177
  14.2 1.5 %collective-permute-start.6 = (bf16[512,128]{1,0:T(8,128)(2,1)S(1)}, bf16[512,128]{1,0:T(8,128)(2,1)S(1)}, u32[]{:S(2)}, u32[]{:S(2)}) collective-permute-start(bf16[512,128]{1,0:T(8,128)(2,1)S(1)} %constant_dynamic-update-slice_fusion.2.refs_2_), channel_id=1, source_target_pairs={{16,0},{17,1},{18,2},{19,3},{12,4},{13,5},{14,6},{15,7},{24,8},{25... | collective-permute-start | bytes 393224 | tf_op jit(solution)/shard_map/ppermute | solution.py:177
  15.7 0.5 %collective-permute-start.11 = (bf16[512,128]{1,0:T(8,128)(2,1)S(1)}, bf16[512,128]{1,0:T(8,128)(2,1)S(1)}, u32[]{:S(2)}, u32[]{:S(2)}) collective-permute-start(bf16[512,128]{1,0:T(8,128)(2,1)S(1)} %collective-permute-done.10.refs_2_), channel_id=1, source_target_pairs={{16,0},{17,1},{18,2},{19,3},{12,4},{13,5},{14,6},{15,7},{24,8},{25... | collective-permute-start | bytes 393224 | tf_op jit(solution)/shard_map/ppermute | solution.py:177
  16.2 0.5 %collective-permute-start.14 = (bf16[512,128]{1,0:T(8,128)(2,1)S(1)}, bf16[512,128]{1,0:T(8,128)(2,1)S(1)}, u32[]{:S(2)}, u32[]{:S(2)}) collective-permute-start(bf16[512,128]{1,0:T(8,128)(2,1)S(1)} %collective-permute-done.10.refs_2_), channel_id=1, source_target_pairs={{4,0},{5,1},{6,2},{7,3},{0,4},{1,5},{2,6},{3,7},{12,8},{13,9},{14,... | collective-permute-start | bytes 393224 | tf_op jit(solution)/shard_map/ppermute | solution.py:177
  16.7 2.2 %collective-permute-done.2.refs_2_ = bf16[512,128]{1,0:T(8,128)(2,1)S(1)} collective-permute-done((bf16[512,128]{1,0:T(8,128)(2,1)S(1)}, bf16[512,128]{1,0:T(8,128)(2,1)S(1)}, u32[]{:S(2)}, u32[]{:S(2)}) %collective-permute-start.2) | collective-permute-done | bytes 131104 | tf_op jit(solution)/shard_map/ppermute | solution.py:177
  18.9 0.2 collective-permute-done.6.refs_3_
  19.1 1.5 %collective-permute-start.3 = (bf16[512,128]{1,0:T(8,128)(2,1)S(1)}, bf16[512,128]{1,0:T(8,128)(2,1)S(1)}, u32[]{:S(2)}, u32[]{:S(2)}) collective-permute-start(bf16[512,128]{1,0:T(8,128)(2,1)S(1)} %collective-permute-done.2.refs_2_), channel_id=1, source_target_pairs={{16,0},{17,1},{18,2},{19,3},{12,4},{13,5},{14,6},{15,7},{24,8},{25... | collective-permute-start | bytes 393224 | tf_op jit(solution)/shard_map/ppermute | solution.py:177
  20.7 0.1 slice_reduce_fusion.refs_0_
  20.8 0.6 %shard_map.46 = (bf16[1024,128]{1,0:T(8,128)(2,1)S(1)}, f32[1024,128]{1,0:T(8,128)S(1)}, f32[1024,128]{1,0:T(8,128)S(1)}, f32[1024,128]{1,0:T(8,128)S(1)}) custom-call(bf16[128,1024]{1,0:T(8,128)(2,1)S(1)} %copy-done, bf16[256,128]{1,0:T(8,128)(2,1)S(1)} %get-tuple-element.46.own_ref), custom_call_target="tpu_custom_call" | custom-call | flops 100663296 | bytes 1048576 | tf_op jit(solution)/shard_map/pallas_call | solution.py:140
  21.4 1.4 %shard_map.47 = (f32[1024,128]{1,0:T(8,128)S(1)}, f32[1024,128]{1,0:T(8,128)S(1)}, f32[1024,128]{1,0:T(8,128)S(1)}) custom-call(s32[32]{0:T(128)S(1)} %slice_reduce_fusion.refs_0_, bf16[1024,128]{1,0:T(8,128)(2,1)S(1)} %get-tuple-element.25.refs_1_, ...), custom_call_target="tpu_custom_call", output_to_operand_aliasing={{0}: (4, {}), {1}: (5, {}), {2}: (6, {})} | custom-call | flops 402653184 | bytes 1048576 | tf_op jit(solution)/shard_map/pallas_call | solution.py:158
  23.0 0.5 %collective-permute-start.7 = (bf16[512,128]{1,0:T(8,128)(2,1)S(1)}, bf16[512,128]{1,0:T(8,128)(2,1)S(1)}, u32[]{:S(2)}, u32[]{:S(2)}) collective-permute-start(bf16[512,128]{1,0:T(8,128)(2,1)S(1)} %collective-permute-done.6.refs_3_), channel_id=1, source_target_pairs={{4,0},{5,1},{6,2},{7,3},{0,4},{1,5},{2,6},{3,7},{12,8},{13,9},{14,... | collective-permute-start | bytes 393224 | tf_op jit(solution)/shard_map/ppermute | solution.py:177
  23.5 0.6 %collective-permute-done.3.refs_4_ = bf16[512,128]{1,0:T(8,128)(2,1)S(1)} collective-permute-done((bf16[512,128]{1,0:T(8,128)(2,1)S(1)}, bf16[512,128]{1,0:T(8,128)(2,1)S(1)}, u32[]{:S(2)}, u32[]{:S(2)}) %collective-permute-start.3) | collective-permute-done | bytes 131104 | tf_op jit(solution)/shard_map/ppermute | solution.py:177
  24.1 3.5 %shard_map.48 = (f32[1024,128]{1,0:T(8,128)S(1)}, f32[1024,128]{1,0:T(8,128)S(1)}, f32[1024,128]{1,0:T(8,128)S(1)}) custom-call(s32[32]{0:T(128)S(1)} %slice_reduce_fusion.refs_0_, bf16[1024,128]{1,0:T(8,128)(2,1)S(1)} %get-tuple-element.25.refs_1_, ...), custom_call_target="tpu_custom_call", output_to_operand_aliasing={{0}: (6, {}), {1}: (7, {}), {2}: (8, {})} | custom-call | flops 805306368 | bytes 1048576 | tf_op jit(solution)/shard_map/pallas_call | solution.py:158
  27.7 3.4 %shard_map.49 = (f32[1024,128]{1,0:T(8,128)S(1)}, f32[1024,128]{1,0:T(8,128)S(1)}, f32[1024,128]{1,0:T(8,128)S(1)}) custom-call(s32[32]{0:T(128)S(1)} %slice_reduce_fusion.refs_0_, bf16[1024,128]{1,0:T(8,128)(2,1)S(1)} %get-tuple-element.25.refs_1_, ...), custom_call_target="tpu_custom_call", output_to_operand_aliasing={{0}: (6, {}), {1}: (7, {}), {2}: (8, {})} | custom-call | flops 805306368 | bytes 1048576 | tf_op jit(solution)/shard_map/pallas_call | solution.py:158
  31.0 2.2 %shard_map.50 = (f32[1024,128]{1,0:T(8,128)S(1)}, f32[1024,128]{1,0:T(8,128)S(1)}, f32[1024,128]{1,0:T(8,128)S(1)}) custom-call(s32[32]{0:T(128)S(1)} %slice_reduce_fusion.refs_0_, bf16[1024,128]{1,0:T(8,128)(2,1)S(1)} %get-tuple-element.25.refs_1_, ...), custom_call_target="tpu_custom_call", output_to_operand_aliasing={{0}: (4, {}), {1}: (5, {}), {2}: (6, {})} | custom-call | flops 402653184 | bytes 1048576 | tf_op jit(solution)/shard_map/pallas_call | solution.py:158
  33.2 2.0 %shard_map.51 = (f32[1024,128]{1,0:T(8,128)S(1)}, f32[1024,128]{1,0:T(8,128)S(1)}, f32[1024,128]{1,0:T(8,128)S(1)}) custom-call(s32[32]{0:T(128)S(1)} %slice_reduce_fusion.refs_0_, bf16[1024,128]{1,0:T(8,128)(2,1)S(1)} %get-tuple-element.25.refs_1_, ...), custom_call_target="tpu_custom_call", output_to_operand_aliasing={{0}: (5, {}), {1}: (6, {}), {2}: (7, {})} | custom-call | flops 603979776 | bytes 1048576 | tf_op jit(solution)/shard_map/pallas_call | solution.py:158
  35.2 2.4 %shard_map.52 = (f32[1024,128]{1,0:T(8,128)S(1)}, f32[1024,128]{1,0:T(8,128)S(1)}, f32[1024,128]{1,0:T(8,128)S(1)}, f32[128,1024]{1,0:T(8,128)}) custom-call(s32[32]{0:T(128)S(1)} %slice_reduce_fusion.refs_0_, bf16[1024,128]{1,0:T(8,128)(2,1)S(1)} %get-tuple-element.25.refs_1_, ...), custom_call_target="tpu_custom_call", output_to_operand_aliasing={{0}: (3, {}), {1}: (4, {}), {2}: (5, {})} | custom-call | flops 201326592 | bytes 1048576 | tf_op jit(solution)/shard_map/pallas_call | solution.py:158
  (29 shorter events, 0.3 us)
Async XLA Ops:
  0.0 0.8 %copy-start.1 = (bf16[128,128]{1,0:T(8,128)(2,1)S(1)}, bf16[128,128]{1,0:T(8,128)(2,1)}, u32[]{:S(2)}) copy-start(bf16[128,128]{1,0:T(8,128)(2,1)} %param.6) | copy-start | bytes 98308
  0.8 20.0 %copy-start = (bf16[128,1024]{1,0:T(8,128)(2,1)S(1)}, bf16[128,1024]{1,0:T(8,128)(2,1)}, u32[]{:S(2)}) copy-start(bf16[128,1024]{1,0:T(8,128)(2,1)} %queries_ref.1) | copy-start | bytes 786436
  0.8 5.7 %collective-permute-start.9 = (bf16[256,128]{1,0:T(8,128)(2,1)S(1)}, bf16[256,128]{1,0:T(8,128)(2,1)S(1)}, u32[]{:S(2)}, u32[]{:S(2)}) collective-permute-start(bf16[256,128]{1,0:T(8,128)(2,1)S(1)} %get-tuple-element.46.own_ref), channel_id=1, source_target_pairs={{1,0},{0,1},{3,2},{2,3},{5,4},{4,5},{7,6},{6,7},{9,8},{8,9},{11,10... | collective-permute-start | bytes 196616 | tf_op jit(solution)/shard_map/ppermute | solution.py:177
  3.9 7.3 %collective-permute-start = (bf16[256,128]{1,0:T(8,128)(2,1)S(1)}, bf16[256,128]{1,0:T(8,128)(2,1)S(1)}, u32[]{:S(2)}, u32[]{:S(2)}) collective-permute-start(bf16[256,128]{1,0:T(8,128)(2,1)S(1)} %get-tuple-element.46.own_ref), channel_id=1, source_target_pairs={{2,0},{3,1},{0,2},{1,3},{6,4},{7,5},{4,6},{5,7},{10,8},{11,9},{8,1... | collective-permute-start | bytes 196616 | tf_op jit(solution)/shard_map/ppermute | solution.py:177
  6.5 6.1 %collective-permute-start.1 = (bf16[256,128]{1,0:T(8,128)(2,1)S(1)}, bf16[256,128]{1,0:T(8,128)(2,1)S(1)}, u32[]{:S(2)}, u32[]{:S(2)}) collective-permute-start(bf16[256,128]{1,0:T(8,128)(2,1)S(1)} %get-tuple-element.46.own_ref), channel_id=1, source_target_pairs={{3,0},{2,1},{1,2},{0,3},{7,4},{6,5},{5,6},{4,7},{11,8},{10,9},{9,1... | collective-permute-start | bytes 196616 | tf_op jit(solution)/shard_map/ppermute | solution.py:177
  6.5 9.7 %collective-permute-start.16 = (bf16[512,128]{1,0:T(8,128)(2,1)S(1)}, bf16[512,128]{1,0:T(8,128)(2,1)S(1)}, u32[]{:S(2)}, u32[]{:S(2)}) collective-permute-start(bf16[512,128]{1,0:T(8,128)(2,1)S(1)} %constant_dynamic-update-slice_fusion.4.refs_2_), channel_id=1, source_target_pairs={{4,0},{5,1},{6,2},{7,3},{0,4},{1,5},{2,6},{3,7},{12,8},{13,9},{14,... | collective-permute-start | bytes 393224 | tf_op jit(solution)/shard_map/ppermute | solution.py:177
  6.6 9.1 %collective-permute-start.10 = (bf16[512,128]{1,0:T(8,128)(2,1)S(1)}, bf16[512,128]{1,0:T(8,128)(2,1)S(1)}, u32[]{:S(2)}, u32[]{:S(2)}) collective-permute-start(bf16[512,128]{1,0:T(8,128)(2,1)S(1)} %constant_dynamic-update-slice_fusion.4.refs_2_), channel_id=1, source_target_pairs={{8,0},{9,1},{10,2},{11,3},{20,4},{21,5},{22,6},{23,7},{0,8},{1,9},... | collective-permute-start | bytes 393224 | tf_op jit(solution)/shard_map/ppermute | solution.py:177
  8.4 7.8 %collective-permute-start.13 = (bf16[512,128]{1,0:T(8,128)(2,1)S(1)}, bf16[512,128]{1,0:T(8,128)(2,1)S(1)}, u32[]{:S(2)}, u32[]{:S(2)}) collective-permute-start(bf16[512,128]{1,0:T(8,128)(2,1)S(1)} %constant_dynamic-update-slice_fusion.4.refs_2_), channel_id=1, source_target_pairs={{16,0},{17,1},{18,2},{19,3},{12,4},{13,5},{14,6},{15,7},{24,8},{25... | collective-permute-start | bytes 393224 | tf_op jit(solution)/shard_map/ppermute | solution.py:177
  11.2 9.5 %copy-start.2 = (s32[4096]{0:T(1024)S(1)}, s32[4096]{0:T(1024)}, u32[]{:S(2)}) copy-start(s32[4096]{0:T(1024)} %param.7) | copy-start | bytes 49156
  12.6 6.3 %collective-permute-start.2 = (bf16[512,128]{1,0:T(8,128)(2,1)S(1)}, bf16[512,128]{1,0:T(8,128)(2,1)S(1)}, u32[]{:S(2)}, u32[]{:S(2)}) collective-permute-start(bf16[512,128]{1,0:T(8,128)(2,1)S(1)} %constant_dynamic-update-slice_fusion.2.refs_2_), channel_id=1, source_target_pairs={{8,0},{9,1},{10,2},{11,3},{20,4},{21,5},{22,6},{23,7},{0,8},{1,9},... | collective-permute-start | bytes 393224 | tf_op jit(solution)/shard_map/ppermute | solution.py:177
  14.2 5.0 %collective-permute-start.6 = (bf16[512,128]{1,0:T(8,128)(2,1)S(1)}, bf16[512,128]{1,0:T(8,128)(2,1)S(1)}, u32[]{:S(2)}, u32[]{:S(2)}) collective-permute-start(bf16[512,128]{1,0:T(8,128)(2,1)S(1)} %constant_dynamic-update-slice_fusion.2.refs_2_), channel_id=1, source_target_pairs={{16,0},{17,1},{18,2},{19,3},{12,4},{13,5},{14,6},{15,7},{24,8},{25... | collective-permute-start | bytes 393224 | tf_op jit(solution)/shard_map/ppermute | solution.py:177
  15.7 5.0 %collective-permute-start.11 = (bf16[512,128]{1,0:T(8,128)(2,1)S(1)}, bf16[512,128]{1,0:T(8,128)(2,1)S(1)}, u32[]{:S(2)}, u32[]{:S(2)}) collective-permute-start(bf16[512,128]{1,0:T(8,128)(2,1)S(1)} %collective-permute-done.10.refs_2_), channel_id=1, source_target_pairs={{16,0},{17,1},{18,2},{19,3},{12,4},{13,5},{14,6},{15,7},{24,8},{25... | collective-permute-start | bytes 393224 | tf_op jit(solution)/shard_map/ppermute | solution.py:177
  16.2 11.5 %collective-permute-start.8 = (bf16[512,128]{1,0:T(8,128)(2,1)S(1)}, bf16[512,128]{1,0:T(8,128)(2,1)S(1)}, u32[]{:S(2)}, u32[]{:S(2)}) collective-permute-start(bf16[512,128]{1,0:T(8,128)(2,1)S(1)} %constant_dynamic-update-slice_fusion.2.refs_2_), channel_id=1, source_target_pairs={{4,0},{5,1},{6,2},{7,3},{0,4},{1,5},{2,6},{3,7},{12,8},{13,9},{14,... | collective-permute-start | bytes 393224 | tf_op jit(solution)/shard_map/ppermute | solution.py:177
  16.2 6.7 %collective-permute-start.14 = (bf16[512,128]{1,0:T(8,128)(2,1)S(1)}, bf16[512,128]{1,0:T(8,128)(2,1)S(1)}, u32[]{:S(2)}, u32[]{:S(2)}) collective-permute-start(bf16[512,128]{1,0:T(8,128)(2,1)S(1)} %collective-permute-done.10.refs_2_), channel_id=1, source_target_pairs={{4,0},{5,1},{6,2},{7,3},{0,4},{1,5},{2,6},{3,7},{12,8},{13,9},{14,... | collective-permute-start | bytes 393224 | tf_op jit(solution)/shard_map/ppermute | solution.py:177
  18.9 4.0 %collective-permute-start.15 = (bf16[512,128]{1,0:T(8,128)(2,1)S(1)}, bf16[512,128]{1,0:T(8,128)(2,1)S(1)}, u32[]{:S(2)}, u32[]{:S(2)}) collective-permute-start(bf16[512,128]{1,0:T(8,128)(2,1)S(1)} %collective-permute-done.13.refs_3_), channel_id=1, source_target_pairs={{4,0},{5,1},{6,2},{7,3},{0,4},{1,5},{2,6},{3,7},{12,8},{13,9},{14,... | collective-permute-start | bytes 393224 | tf_op jit(solution)/shard_map/ppermute | solution.py:177
  19.1 5.0 %collective-permute-start.3 = (bf16[512,128]{1,0:T(8,128)(2,1)S(1)}, bf16[512,128]{1,0:T(8,128)(2,1)S(1)}, u32[]{:S(2)}, u32[]{:S(2)}) collective-permute-start(bf16[512,128]{1,0:T(8,128)(2,1)S(1)} %collective-permute-done.2.refs_2_), channel_id=1, source_target_pairs={{16,0},{17,1},{18,2},{19,3},{12,4},{13,5},{14,6},{15,7},{24,8},{25... | collective-permute-start | bytes 393224 | tf_op jit(solution)/shard_map/ppermute | solution.py:177
  20.7 7.0 %collective-permute-start.12 = (bf16[512,128]{1,0:T(8,128)(2,1)S(1)}, bf16[512,128]{1,0:T(8,128)(2,1)S(1)}, u32[]{:S(2)}, u32[]{:S(2)}) collective-permute-start(bf16[512,128]{1,0:T(8,128)(2,1)S(1)} %collective-permute-done.11.refs_4_), channel_id=1, source_target_pairs={{4,0},{5,1},{6,2},{7,3},{0,4},{1,5},{2,6},{3,7},{12,8},{13,9},{14,... | collective-permute-start | bytes 393224 | tf_op jit(solution)/shard_map/ppermute | solution.py:177
  22.9 10.3 %collective-permute-start.5 = (bf16[512,128]{1,0:T(8,128)(2,1)S(1)}, bf16[512,128]{1,0:T(8,128)(2,1)S(1)}, u32[]{:S(2)}, u32[]{:S(2)}) collective-permute-start(bf16[512,128]{1,0:T(8,128)(2,1)S(1)} %collective-permute-done.2.refs_2_), channel_id=1, source_target_pairs={{4,0},{5,1},{6,2},{7,3},{0,4},{1,5},{2,6},{3,7},{12,8},{13,9},{14,... | collective-permute-start | bytes 393224 | tf_op jit(solution)/shard_map/ppermute | solution.py:177
  23.0 10.2 %collective-permute-start.7 = (bf16[512,128]{1,0:T(8,128)(2,1)S(1)}, bf16[512,128]{1,0:T(8,128)(2,1)S(1)}, u32[]{:S(2)}, u32[]{:S(2)}) collective-permute-start(bf16[512,128]{1,0:T(8,128)(2,1)S(1)} %collective-permute-done.6.refs_3_), channel_id=1, source_target_pairs={{4,0},{5,1},{6,2},{7,3},{0,4},{1,5},{2,6},{3,7},{12,8},{13,9},{14,... | collective-permute-start | bytes 393224 | tf_op jit(solution)/shard_map/ppermute | solution.py:177
  24.1 11.1 %collective-permute-start.4 = (bf16[512,128]{1,0:T(8,128)(2,1)S(1)}, bf16[512,128]{1,0:T(8,128)(2,1)S(1)}, u32[]{:S(2)}, u32[]{:S(2)}) collective-permute-start(bf16[512,128]{1,0:T(8,128)(2,1)S(1)} %collective-permute-done.3.refs_4_), channel_id=1, source_target_pairs={{4,0},{5,1},{6,2},{7,3},{0,4},{1,5},{2,6},{3,7},{12,8},{13,9},{14,... | collective-permute-start | bytes 393224 | tf_op jit(solution)/shard_map/ppermute | solution.py:177

commit v2 on v1

v2 whole, which is shorter than its diff:
```python
import functools
import math

import jax
import jax.numpy as jnp
from jax import lax
from jax.experimental import pallas as pl
from jax.experimental.pallas import tpu as pltpu
from jax.sharding import PartitionSpec as P


HD = 128
AXES = ("pb", "ka")
BIG = -1e30
STEP = 4
LIMIT = 24 << 20

VMEM = pl.BlockSpec(memory_space=pltpu.VMEM)
SMEM = pl.BlockSpec(memory_space=pltpu.SMEM)


def combine(rows, keys, values, sums, to_log2, mask=None):
    score = lax.dot_general(
        rows, keys, (((1,), (1,)), ((), ())), preferred_element_type=jnp.float32
    )
    if mask is not None:
        score = jnp.where(mask, score, BIG)
    parts = [score[:, at : at + HD] for at in range(0, keys.shape[0], HD)]
    top = jnp.max(functools.reduce(jnp.maximum, parts), axis=1, keepdims=True)
    if sums is None:
        top = jnp.broadcast_to(top, (rows.shape[0], HD))
    else:
        top = jnp.maximum(sums[0], top)
    weights = [jnp.exp2((part - top) * to_log2) for part in parts]
    if mask is not None:
        weights = [jnp.where(mask, weight, 0.0) for weight in weights]
    total = functools.reduce(jnp.add, weights)
    weight = jnp.concatenate(weights, axis=1) if len(weights) > 1 else weights[0]
    high = weight.astype(jnp.bfloat16)
    low = (weight - high.astype(jnp.float32)).astype(jnp.bfloat16)
    over = (((1,), (0,)), ((), ()))
    result = lax.dot_general(high, values, over, preferred_element_type=jnp.float32)
    result += lax.dot_general(low, values, over, preferred_element_type=jnp.float32)
    if sums is None:
        return top, total, result
    largest, totals, summed = sums
    factor = jnp.exp2((largest - top) * to_log2)
    return top, totals * factor + total, summed * factor + result


TO_LOG2 = math.log2(math.e) / HD**0.5


def own_kernel(queries_ref, own_ref, rows_ref, largest_ref, totals_ref, summed_ref):
    token, width = queries_ref.shape
    heads = width // HD
    for head in range(heads):
        rows_ref[head * token : (head + 1) * token, :] = queries_ref[:, head * HD : (head + 1) * HD]
    shape = (heads, token, token)
    causal = lax.broadcasted_iota(jnp.int32, shape, 2) <= lax.broadcasted_iota(jnp.int32, shape, 1)
    keys, values = own_ref[:token, :], own_ref[token:, :]
    mask = causal.reshape(heads * token, token)
    new = combine(rows_ref[...], keys, values, None, TO_LOG2, mask)
    for held, value in zip((largest_ref, totals_ref, summed_ref), new):
        held[...] = value


def attend_kernel(pieces, groups, fresh, pack, size_key, token, *refs):
    refs = list(refs)
    take = lambda number: [refs.pop(0) for _ in range(number)]
    (starts_ref,) = take(1)
    rows_refs = take(len(groups))
    block_refs = take(len(pieces))
    take(3 * (len(groups) - len(fresh)))
    states = [take(3) for _ in groups]
    packed_refs = take(1 if pack else 0)
    keys_ref, values_ref = take(2)

    own_pb, own_ka = lax.axis_index("pb"), lax.axis_index("ka")
    core = own_pb % 2
    bounds = [starts_ref[(own_pb ^ group) * size_key + own_ka] for group in groups]
    low = functools.reduce(jnp.minimum, bounds)
    high = functools.reduce(jnp.maximum, bounds)

    def compact(seen, inside):
        for ref, parts in zip(block_refs, pieces):
            for offset, number, base, mask_even, mask_odd in parts:
                source = (own_pb ^ jnp.where(core == 0, mask_even, mask_odd)) * size_key
                for at in range(number):
                    visible = inside(starts_ref[source + (own_ka ^ (base + at))])
                    row = (offset + at) * 2 * token

                    @pl.when(visible)
                    def _():
                        target = pl.ds(pl.multiple_of(seen * token, token), token)
                        keys_ref[target, :] = ref[row : row + token, :]
                        values_ref[target, :] = ref[row + token : row + 2 * token, :]

                    seen = seen + visible.astype(jnp.int32)
        return seen

    both = compact(jnp.int32(0), lambda start: start < low)
    some = both
    if len(groups) > 1:
        some = compact(both, lambda start: (start >= low) & (start < high))

    def attend_group(rows_ref, state, seen):
        def update(first, number):
            part = pl.ds(pl.multiple_of(first * token, token), number * token)
            sums = [held[...] for held in state]
            new = combine(rows_ref[...], keys_ref[part, :], values_ref[part, :], sums, TO_LOG2)
            for held, value in zip(state, new):
                held[...] = value

        def many(index, _):
            update(index * STEP, STEP)
            return 0

        lax.fori_loop(0, seen // STEP, many, 0)
        left = seen % STEP
        done = seen - left
        number = STEP // 2
        while number:
            pl.when((left & number) != 0)(
                functools.partial(update, done + (left & ~(2 * number - 1)), number)
            )
            number //= 2

    for group, bound, rows_ref, state in zip(groups, bounds, rows_refs, states):
        if group in fresh:
            state[0][...] = jnp.full_like(state[0], BIG)
            state[1][...] = jnp.zeros_like(state[1])
            state[2][...] = jnp.zeros_like(state[2])
        attend_group(rows_ref, state, jnp.where(bound == high, some, both))

    if pack:
        largest_ref, totals_ref, summed_ref = states[0]
        count = summed_ref.shape[0]
        lane = lax.broadcasted_iota(jnp.int32, (count, HD), 1)
        total = jnp.sum(totals_ref[...], axis=1, keepdims=True)
        packed_refs[0][:count, :] = summed_ref[...]
        packed_refs[0][count:, :] = jnp.where(lane < HD // 2, largest_ref[...], total)


def finish_kernel(heads, largest_ref, totals_ref, summed_ref, packed_ref, out_ref):
    token = out_ref.shape[0]
    count = summed_ref.shape[0]
    for at in range(heads):
        first = (pl.program_id(0) * heads + at) * token
        rows = pl.ds(pl.multiple_of(first, token), token)
        packed = packed_ref[pl.ds(pl.multiple_of(count + first, token), token), :]
        largest = largest_ref[rows, :]
        other = packed[:, :1]
        top = jnp.maximum(largest, other)
        mine, theirs = jnp.exp2((largest - top) * TO_LOG2), jnp.exp2((other - top) * TO_LOG2)
        total = jnp.sum(totals_ref[rows, :], axis=1, keepdims=True) * mine
        total += packed[:, HD // 2 : HD // 2 + 1] * theirs
        summed = summed_ref[rows, :] * mine + packed_ref[rows, :] * theirs
        out_ref[:, at * HD : (at + 1) * HD] = summed / total


def params(rows, token, blocks):
    return dict(
        compiler_params=pltpu.CompilerParams(vmem_limit_bytes=LIMIT),
        cost_estimate=pl.CostEstimate(
            flops=6 * rows * HD * token * blocks,
            transcendentals=rows * token * blocks,
            bytes_accessed=1 << 20,
        ),
    )


def attend_own(queries, own):
    token, width = queries.shape
    rows = width // HD * token
    sums = jax.ShapeDtypeStruct((rows, HD), jnp.float32)
    result = pl.pallas_call(
        own_kernel,
        out_shape=[jax.ShapeDtypeStruct((rows, HD), jnp.bfloat16), sums, sums, sums],
        in_specs=[VMEM] * 2,
        out_specs=[VMEM] * 4,
        **params(rows, token, 1),
    )(queries, own)
    return result[0], tuple(result[1:])


def attend(starts, rows, states, items, groups, size_key, token, pack=False):
    count = rows[0].shape[0]
    arrays, pieces = zip(*items)
    blocks = sum(array.shape[0] for array in arrays) // (2 * token)
    fresh = tuple(group for group in groups if states[group] is None)
    sums = [jax.ShapeDtypeStruct((count, HD), jnp.float32)] * 3
    outs = sums * len(groups)
    if pack:
        outs.append(jax.ShapeDtypeStruct((2 * count, HD), jnp.float32))
    operands = [starts, *(rows[group] for group in groups), *arrays]
    aliases = {}
    for at, group in enumerate(groups):
        if group not in fresh:
            aliases.update({len(operands) + index: 3 * at + index for index in range(3)})
            operands += states[group]
    kernel = functools.partial(attend_kernel, pieces, groups, fresh, pack, size_key, token)
    result = pl.pallas_call(
        kernel,
        out_shape=outs,
        in_specs=[SMEM] + [VMEM] * (len(operands) - 1),
        out_specs=[VMEM] * len(outs),
        input_output_aliases=aliases,
        scratch_shapes=[pltpu.VMEM((blocks * token, HD), jnp.bfloat16)] * 2,
        **params(count * len(groups), token, blocks),
    )(*operands)
    states = list(states)
    for at, group in enumerate(groups):
        states[group] = tuple(result[3 * at : 3 * at + 3])
    return states, result[-1]


def finish(sums, packed, shape):
    token, width = shape
    heads = 2 if width % (2 * HD) == 0 else 1
    return pl.pallas_call(
        functools.partial(finish_kernel, heads),
        grid=(width // (heads * HD),),
        out_shape=jax.ShapeDtypeStruct(shape, jnp.float32),
        in_specs=[VMEM] * 4,
        out_specs=pl.BlockSpec((token, heads * HD), lambda step: (0, step)),
        **params(width // HD * token, token, 1),
    )(*sums, packed)


def move(array, mask_even, mask_odd, place):
    size_query, size_key = lax.axis_size("pb"), lax.axis_size("ka")
    pairs = []
    for query in range(size_query):
        source = query ^ (mask_odd if query % 2 else mask_even)
        for key in range(size_key):
            pairs.append((source * size_key + (key ^ place), query * size_key + key))
    return lax.ppermute(array, AXES, pairs)


def stages(size_query):
    bits = [1 << at for at in range(1, size_query.bit_length() - 1)]
    return [bits[at : at + 2] for at in range(0, len(bits), 2)]


def paired(size_query, size_key):
    plan = stages(size_query)
    return len(plan) == 1 and len(plan[0]) == 2 and size_key > 1


def spread(item, bits):
    array, parts = item
    one, two = bits[0], bits[-1]
    near = (move(array, one, two, 0), shifted(parts, one, two))
    if one == two:
        return near, None, None
    side = (move(array, two, one, 0), shifted(parts, two, one))
    far = (move(near[0], two, one, 0), shifted(near[1], two, one))
    return near, side, far


def shifted(parts, even, odd):
    return tuple((at, number, base, one ^ even, two ^ odd) for at, number, base, one, two in parts)


def joined(first, second):
    (one, parts), (two, more) = first, second
    skip = sum(number for _, number, *_ in parts)
    more = tuple((at + skip, *rest) for at, *rest in more)
    return jnp.concatenate([one, two], axis=0), parts + more


def gathered_attention(queries, keys, values, positions):
    token = queries.shape[0]
    size_query, size_key = lax.axis_size("pb"), lax.axis_size("ka")
    assert size_query & (size_query - 1) == 0 and size_key & (size_key - 1) == 0 and size_query > 1
    starts = positions.reshape(-1, token)[:, 0]
    own = jnp.concatenate([keys, values], axis=0)
    column = [own] + [move(own, 0, 0, place) for place in range(1, size_key)]
    half = max(size_key // 2, 1)
    held = [
        (jnp.concatenate(column[base : base + half], axis=0), ((0, half, base, 0, 0),))
        for base in range(0, size_key, half)
    ]

    rows, sums = attend_own(queries, own)
    rows = (rows, move(rows, 1, 1, 0))
    plan = stages(size_query)
    if paired(size_query, size_key):
        (lower, upper), (one, two) = held, plan[0]
        array, parts = lower
        near = (move(array, one, two, 0), shifted(parts, one, two))
        side = (move(array, two, one, 0), shifted(parts, two, one))
        array, parts = upper
        near_up = (move(array, one, two, 0), shifted(parts, one, two))
        array, parts = joined(near, upper)
        mixed = (move(array, two, one, 0), shifted(parts, two, one))
        array, parts = near_up
        far_up = (move(array, two, one, 0), shifted(parts, two, one))
        early = [[lower], [near, side]]
        late = [[upper, near_up, mixed], [far_up]]
    else:
        early = [held]
        for bits in plan:
            more = [item for piece in held for item in spread(piece, bits) if item is not None]
            early.append(more)
            held = held + more
        early, late = early[:-1], early[-1:]

    states = [sums, None]
    attend_to = functools.partial(attend, size_key=size_key, token=token)
    number = 0
    steps = [(group, (0, 1)) for group in early] + [(group, (1,)) for group in late]
    for number, (group, who) in enumerate(steps):
        pack = number == len(steps) - 1
        states, packed = attend_to(starts, rows, states, group, who, pack=pack)
    packed = move(packed, 1, 1, 0)
    rest = [item for group in late for item in group]
    states, _ = attend_to(starts, rows, states, rest, (0,))
    return finish(states[0], packed, queries.shape)


def solution(mesh):
    return jax.shard_map(
        gathered_attention,
        mesh=mesh,
        in_specs=(P(AXES, None), P(AXES, None), P(AXES, None), P()),
        out_specs=P(AXES, None),
        check_vma=False,
    )
```

time: 37.9 us -> 39.2 us (1.034)
  the two profiles are of different devices: /device:TPU:0 before, /device:TPU:29 now
where the time goes in v2:
time: 39.2 us; the launch traced here: 39.1 us
  starting transfers between devices  17.1 us (44%)
  Pallas kernels  15.3 us (39%)
  waiting for transfers between devices  5.59 us (14%)
  local copies, waits for them, and re-layouts  0.98 us (2%)
    ppermute x10, starting transfers between devices, move(): return lax.ppermute(array, AXES, pairs)  17.1 us
    pallas_call x5, Pallas kernels, attend(): pl.pallas_call(kernel, out_shape=outs, in_specs=[SMEM] + [VMEM] * (len(op...  12.6 us
    ppermute x10, waiting for transfers between devices, move(): return lax.ppermute(array, AXES, pairs)  5.59 us
    pallas_call x1, Pallas kernels, finish(): pl.pallas_call(functools.partial(finish_kernel, heads), grid=(width // (h...  2.07 us
    unnamed x9, local copies, waits for them, and re-layouts  0.84 us
  transfers between devices with their start and end apart: 10, of which 3 were waited for; matrix products, arithmetic and copies ran while one was open for 0% of the time, Pallas kernels for 30%

profile of v2, /device:TPU:29, one launch (start us, length us, event | category | flops | bytes accessed | tf_op | source)
XLA Modules:
  0.0 39.1 jit_solution(5354188931664376037)
XLA Ops:
  0.0 0.8 %constant_dynamic-update-slice_fusion.6 = (bf16[512,128]{1,0:T(8,128)(2,1)S(1)}, bf16[256,128]{1,0:T(8,128)(2,1)S(1)}) fusion(bf16[128,128]{1,0:T(8,128)(2,1)} %param.5), kind=kLoop, calls=%fused_computation.8 | loop fusion | bytes 98304
  0.8 0.2 collective-permute-start.3
  1.1 0.1 collective-permute-start
  1.1 2.9 %collective-permute-done.3 = bf16[256,128]{1,0:T(8,128)(2,1)S(1)} collective-permute-done((bf16[256,128]{1,0:T(8,128)(2,1)S(1)}, bf16[256,128]{1,0:T(8,128)(2,1)S(1)}, u32[]{:S(2)}, u32[]{:S(2)}) %collective-permute-start.3) | collective-permute-done | bytes 65568 | tf_op jit(solution)/shard_map/ppermute | solution.py:238
  4.0 0.3 collective-permute-start.4
  4.3 0.4 %collective-permute-start.1 = (bf16[256,128]{1,0:T(8,128)(2,1)S(1)}, bf16[256,128]{1,0:T(8,128)(2,1)S(1)}, u32[]{:S(2)}, u32[]{:S(2)}) collective-permute-start(bf16[256,128]{1,0:T(8,128)(2,1)S(1)} %get-tuple-element.52.own_ref), channel_id=1, source_target_pairs={{3,0},{2,1},{1,2},{0,3},{7,4},{6,5},{5,6},{4,7},{11,8},{10,9},{9,1... | collective-permute-start | bytes 196616 | tf_op jit(solution)/shard_map/ppermute | solution.py:238
  4.8 0.6 %shard_map.46 = (bf16[1024,128]{1,0:T(8,128)(2,1)S(1)}, f32[1024,128]{1,0:T(8,128)S(1)}, f32[1024,128]{1,0:T(8,128)S(1)}, f32[1024,128]{1,0:T(8,128)S(1)}) custom-call(bf16[128,1024]{1,0:T(8,128)(2,1)S(1)} %copy-done, bf16[256,128]{1,0:T(8,128)(2,1)S(1)} %get-tuple-element.52.own_ref), custom_call_target="tpu_custom_call" | custom-call | flops 100663296 | bytes 1048576 | tf_op jit(solution)/shard_map/pallas_call | solution.py:177
  5.4 3.4 %collective-permute-start.7 = (bf16[1024,128]{1,0:T(8,128)(2,1)S(1)}, bf16[1024,128]{1,0:T(8,128)(2,1)S(1)}, u32[]{:S(2)}, u32[]{:S(2)}) collective-permute-start(bf16[1024,128]{1,0:T(8,128)(2,1)S(1)} %get-tuple-element.28.refs_1_), channel_id=1, source_target_pairs={{4,0},{5,1},{6,2},{7,3},{0,4},{1,5},{2,6},{3,7},{12,8},{13,9},{14,... | collective-permute-start | bytes 786440 | tf_op jit(solution)/shard_map/ppermute | solution.py:238
  8.8 0.0 collective-permute-done
  8.8 0.5 %collective-permute-done.1 = bf16[256,128]{1,0:T(8,128)(2,1)S(1)} collective-permute-done((bf16[256,128]{1,0:T(8,128)(2,1)S(1)}, bf16[256,128]{1,0:T(8,128)(2,1)S(1)}, u32[]{:S(2)}, u32[]{:S(2)}) %collective-permute-start.1) | collective-permute-done | bytes 65568 | tf_op jit(solution)/shard_map/ppermute | solution.py:238
  9.3 0.0 copy-start.2
  9.3 1.3 %collective-permute-start.5 = (bf16[1024,128]{1,0:T(8,128)(2,1)S(1)}, bf16[1024,128]{1,0:T(8,128)(2,1)S(1)}, u32[]{:S(2)}, u32[]{:S(2)}) collective-permute-start(bf16[1024,128]{1,0:T(8,128)(2,1)S(1)} %pad_maximum_fusion), channel_id=1, source_target_pairs={{16,0},{17,1},{18,2},{19,3},{12,4},{13,5},{14,6},{15,7},{24,8},{25... | collective-permute-start | bytes 786440 | tf_op jit(solution)/shard_map/ppermute | solution.py:238
  10.6 1.4 %collective-permute-start.2 = (bf16[512,128]{1,0:T(8,128)(2,1)S(1)}, bf16[512,128]{1,0:T(8,128)(2,1)S(1)}, u32[]{:S(2)}, u32[]{:S(2)}) collective-permute-start(bf16[512,128]{1,0:T(8,128)(2,1)S(1)} %constant_dynamic-update-slice_fusion.2.refs_2_), channel_id=1, source_target_pairs={{8,0},{9,1},{10,2},{11,3},{20,4},{21,5},{22,6},{23,7},{0,8},{1,9},... | collective-permute-start | bytes 393224 | tf_op jit(solution)/shard_map/ppermute | solution.py:238
  12.0 0.2 collective-permute-start.8
  12.1 0.1 slice_reduce_fusion.refs_0_
  12.3 2.2 %collective-permute-done.2.refs_3_ = bf16[512,128]{1,0:T(8,128)(2,1)S(1)} collective-permute-done((bf16[512,128]{1,0:T(8,128)(2,1)S(1)}, bf16[512,128]{1,0:T(8,128)(2,1)S(1)}, u32[]{:S(2)}, u32[]{:S(2)}) %collective-permute-start.2) | collective-permute-done | bytes 131104 | tf_op jit(solution)/shard_map/ppermute | solution.py:238
  14.5 0.3 collective-permute-start.6
  14.7 1.4 %shard_map.47 = (f32[1024,128]{1,0:T(8,128)S(1)}, f32[1024,128]{1,0:T(8,128)S(1)}, f32[1024,128]{1,0:T(8,128)S(1)}, f32[1024,128]{1,0:T(8,128)S(1)}, f32[1024,128]{1,0:T(8,128)S(1)}, /*index=5*/f32[1024,128]{1,0:T(8,128)S(1)}) custom-call(s32[32]{0:T(128)S(1)} %slice_reduce_fusion.refs_0_, ...), custom_call_target="tpu_custom_call", output_to_operand_aliasing={{0}: (4, {}), {1}: (5, {}), {2}: (6, {})} | custom-call | flops 402653184 | bytes 1048576 | tf_op jit(solution)/shard_map/pallas_call | solution.py:203
  16.2 3.3 %shard_map.48 = (f32[1024,128]{1,0:T(8,128)S(1)}, f32[1024,128]{1,0:T(8,128)S(1)}, f32[1024,128]{1,0:T(8,128)S(1)}, f32[1024,128]{1,0:T(8,128)S(1)}, f32[1024,128]{1,0:T(8,128)S(1)}, /*index=5*/f32[1024,128]{1,0:T(8,128)S(1)}) custom-call(s32[32]{0:T(128)S(1)} %slice_reduce_fusion.refs_0_, ...), custom_call_target="tpu_custom_call", output_to_operand_aliasing={{0}: (5, {}), {1}: (6, {}), {2}: (7, {}), {3}: (8, {}), {4}... | custom-call | flops 805306368 | bytes 1048576 | tf_op jit(solution)/shard_map/pallas_call | solution.py:203
  19.5 2.2 %shard_map.50 = (f32[1024,128]{1,0:T(8,128)S(1)}, f32[1024,128]{1,0:T(8,128)S(1)}, f32[1024,128]{1,0:T(8,128)S(1)}) custom-call(s32[32]{0:T(128)S(1)} %slice_reduce_fusion.refs_0_, bf16[1024,128]{1,0:T(8,128)(2,1)S(1)} %collective-permute-done.7.refs_2_.refs_1_, ...), custom_call_target="tpu_custom_call", output_to_operand_aliasing={{0}: (5, {}), {1}: (6, {}), {2}: (7, {})} | custom-call | flops 805306368 | bytes 1048576 | tf_op jit(solution)/shard_map/pallas_call | solution.py:203
  21.7 1.6 %shard_map.51 = (f32[1024,128]{1,0:T(8,128)S(1)}, f32[1024,128]{1,0:T(8,128)S(1)}, f32[1024,128]{1,0:T(8,128)S(1)}, f32[2048,128]{1,0:T(8,128)S(1)}) custom-call(s32[32]{0:T(128)S(1)} %slice_reduce_fusion.refs_0_, bf16[1024,128]{1,0:T(8,128)(2,1)S(1)} %collective-permute-done.7.refs_2_.refs_1_, ...), custom_call_target="tpu_custom_call", output_to_operand_aliasing={{0}: (3, {}), {1}: (4, {}), {2}: (5, {})} | custom-call | flops 201326592 | bytes 1048576 | tf_op jit(solution)/shard_map/pallas_call | solution.py:203
  23.3 9.7 %collective-permute-start.9 = (f32[2048,128]{1,0:T(8,128)S(1)}, f32[2048,128]{1,0:T(8,128)S(1)}, u32[]{:S(2)}, u32[]{:S(2)}) collective-permute-start(f32[2048,128]{1,0:T(8,128)S(1)} %get-tuple-element.50), channel_id=1, source_target_pairs={{4,0},{5,1},{6,2},{7,3},{0,4},{1,5},{2,6},{3,7},{12,8},{13,9},{14,... | collective-permute-start | bytes 3145736 | tf_op jit(solution)/shard_map/ppermute | solution.py:238
  33.0 4.0 %shard_map.49 = (f32[1024,128]{1,0:T(8,128)S(1)}, f32[1024,128]{1,0:T(8,128)S(1)}, f32[1024,128]{1,0:T(8,128)S(1)}) custom-call(s32[32]{0:T(128)S(1)} %slice_reduce_fusion.refs_0_, bf16[1024,128]{1,0:T(8,128)(2,1)S(1)} %get-tuple-element.28.refs_1_, ...), custom_call_target="tpu_custom_call", output_to_operand_aliasing={{0}: (6, {}), {1}: (7, {}), {2}: (8, {})} | custom-call | flops 1006632960 | bytes 1048576 | tf_op jit(solution)/shard_map/pallas_call | solution.py:203
  37.0 2.1 %shard_map.52 = f32[128,1024]{1,0:T(8,128)} custom-call(f32[1024,128]{1,0:T(8,128)S(1)} %get-tuple-element.41.largest_ref, f32[1024,128]{1,0:T(8,128)S(1)} %get-tuple-element.42.totals_ref, f32[1024,128]{1,0:T(8,128)S(1)} %get-tuple-element.43.summed_ref, f32[2048,128]{1,0:T(8,128)S(1)} %collective-permute-done.9.packed_ref), custom_call_target="tpu_custom_call" | custom-call | flops 100663296 | bytes 1048576 | tf_op jit(solution)/shard_map/pallas_call | solution.py:221
  (16 shorter events, 0.1 us)
Async XLA Ops:
  0.0 0.8 %copy-start.1 = (bf16[128,128]{1,0:T(8,128)(2,1)S(1)}, bf16[128,128]{1,0:T(8,128)(2,1)}, u32[]{:S(2)}) copy-start(bf16[128,128]{1,0:T(8,128)(2,1)} %param.6) | copy-start | bytes 98308
  0.0 4.8 %copy-start = (bf16[128,1024]{1,0:T(8,128)(2,1)S(1)}, bf16[128,1024]{1,0:T(8,128)(2,1)}, u32[]{:S(2)}) copy-start(bf16[128,1024]{1,0:T(8,128)(2,1)} %queries_ref.1) | copy-start | bytes 786436
  0.8 3.2 %collective-permute-start.3 = (bf16[256,128]{1,0:T(8,128)(2,1)S(1)}, bf16[256,128]{1,0:T(8,128)(2,1)S(1)}, u32[]{:S(2)}, u32[]{:S(2)}) collective-permute-start(bf16[256,128]{1,0:T(8,128)(2,1)S(1)} %get-tuple-element.52.own_ref), channel_id=1, source_target_pairs={{1,0},{0,1},{3,2},{2,3},{5,4},{4,5},{7,6},{6,7},{9,8},{8,9},{11,10... | collective-permute-start | bytes 196616 | tf_op jit(solution)/shard_map/ppermute | solution.py:238
  1.1 7.7 %collective-permute-start = (bf16[256,128]{1,0:T(8,128)(2,1)S(1)}, bf16[256,128]{1,0:T(8,128)(2,1)S(1)}, u32[]{:S(2)}, u32[]{:S(2)}) collective-permute-start(bf16[256,128]{1,0:T(8,128)(2,1)S(1)} %get-tuple-element.52.own_ref), channel_id=1, source_target_pairs={{2,0},{3,1},{0,2},{1,3},{6,4},{7,5},{4,6},{5,7},{10,8},{11,9},{8,1... | collective-permute-start | bytes 196616 | tf_op jit(solution)/shard_map/ppermute | solution.py:238
  4.0 5.2 %collective-permute-start.4 = (bf16[512,128]{1,0:T(8,128)(2,1)S(1)}, bf16[512,128]{1,0:T(8,128)(2,1)S(1)}, u32[]{:S(2)}, u32[]{:S(2)}) collective-permute-start(bf16[512,128]{1,0:T(8,128)(2,1)S(1)} %constant_dynamic-update-slice_fusion.4.refs_3_), channel_id=1, source_target_pairs={{8,0},{9,1},{10,2},{11,3},{20,4},{21,5},{22,6},{23,7},{0,8},{1,9},... | collective-permute-start | bytes 393224 | tf_op jit(solution)/shard_map/ppermute | solution.py:238
  4.3 4.9 %collective-permute-start.1 = (bf16[256,128]{1,0:T(8,128)(2,1)S(1)}, bf16[256,128]{1,0:T(8,128)(2,1)S(1)}, u32[]{:S(2)}, u32[]{:S(2)}) collective-permute-start(bf16[256,128]{1,0:T(8,128)(2,1)S(1)} %get-tuple-element.52.own_ref), channel_id=1, source_target_pairs={{3,0},{2,1},{1,2},{0,3},{7,4},{6,5},{5,6},{4,7},{11,8},{10,9},{9,1... | collective-permute-start | bytes 196616 | tf_op jit(solution)/shard_map/ppermute | solution.py:238
  5.4 9.3 %collective-permute-start.7 = (bf16[1024,128]{1,0:T(8,128)(2,1)S(1)}, bf16[1024,128]{1,0:T(8,128)(2,1)S(1)}, u32[]{:S(2)}, u32[]{:S(2)}) collective-permute-start(bf16[1024,128]{1,0:T(8,128)(2,1)S(1)} %get-tuple-element.28.refs_1_), channel_id=1, source_target_pairs={{4,0},{5,1},{6,2},{7,3},{0,4},{1,5},{2,6},{3,7},{12,8},{13,9},{14,... | collective-permute-start | bytes 786440 | tf_op jit(solution)/shard_map/ppermute | solution.py:238
  9.3 2.9 %copy-start.2 = (s32[4096]{0:T(1024)S(1)}, s32[4096]{0:T(1024)}, u32[]{:S(2)}) copy-start(s32[4096]{0:T(1024)} %param.7) | copy-start | bytes 49156
  9.3 10.2 %collective-permute-start.5 = (bf16[1024,128]{1,0:T(8,128)(2,1)S(1)}, bf16[1024,128]{1,0:T(8,128)(2,1)S(1)}, u32[]{:S(2)}, u32[]{:S(2)}) collective-permute-start(bf16[1024,128]{1,0:T(8,128)(2,1)S(1)} %pad_maximum_fusion), channel_id=1, source_target_pairs={{16,0},{17,1},{18,2},{19,3},{12,4},{13,5},{14,6},{15,7},{24,8},{25... | collective-permute-start | bytes 786440 | tf_op jit(solution)/shard_map/ppermute | solution.py:238
  10.6 3.9 %collective-permute-start.2 = (bf16[512,128]{1,0:T(8,128)(2,1)S(1)}, bf16[512,128]{1,0:T(8,128)(2,1)S(1)}, u32[]{:S(2)}, u32[]{:S(2)}) collective-permute-start(bf16[512,128]{1,0:T(8,128)(2,1)S(1)} %constant_dynamic-update-slice_fusion.2.refs_2_), channel_id=1, source_target_pairs={{8,0},{9,1},{10,2},{11,3},{20,4},{21,5},{22,6},{23,7},{0,8},{1,9},... | collective-permute-start | bytes 393224 | tf_op jit(solution)/shard_map/ppermute | solution.py:238
  12.0 4.2 %collective-permute-start.8 = (bf16[512,128]{1,0:T(8,128)(2,1)S(1)}, bf16[512,128]{1,0:T(8,128)(2,1)S(1)}, u32[]{:S(2)}, u32[]{:S(2)}) collective-permute-start(bf16[512,128]{1,0:T(8,128)(2,1)S(1)} %constant_dynamic-update-slice_fusion.4.refs_3_), channel_id=1, source_target_pairs={{16,0},{17,1},{18,2},{19,3},{12,4},{13,5},{14,6},{15,7},{24,8},{25... | collective-permute-start | bytes 393224 | tf_op jit(solution)/shard_map/ppermute | solution.py:238
  14.5 7.2 %collective-permute-start.6 = (bf16[512,128]{1,0:T(8,128)(2,1)S(1)}, bf16[512,128]{1,0:T(8,128)(2,1)S(1)}, u32[]{:S(2)}, u32[]{:S(2)}) collective-permute-start(bf16[512,128]{1,0:T(8,128)(2,1)S(1)} %collective-permute-done.2.refs_3_), channel_id=1, source_target_pairs={{16,0},{17,1},{18,2},{19,3},{12,4},{13,5},{14,6},{15,7},{24,8},{25... | collective-permute-start | bytes 393224 | tf_op jit(solution)/shard_map/ppermute | solution.py:238
  23.3 13.7 %collective-permute-start.9 = (f32[2048,128]{1,0:T(8,128)S(1)}, f32[2048,128]{1,0:T(8,128)S(1)}, u32[]{:S(2)}, u32[]{:S(2)}) collective-permute-start(f32[2048,128]{1,0:T(8,128)S(1)} %get-tuple-element.50), channel_id=1, source_target_pairs={{4,0},{5,1},{6,2},{7,3},{0,4},{1,5},{2,6},{3,7},{12,8},{13,9},{14,... | collective-permute-start | bytes 3145736 | tf_op jit(solution)/shard_map/ppermute | solution.py:238

commit v3 on v2

--- a/solution.py
+++ b/solution.py
@@ -51,11 +51,15 @@
 TO_LOG2 = math.log2(math.e) / HD**0.5
 
 
-def own_kernel(queries_ref, own_ref, rows_ref, largest_ref, totals_ref, summed_ref):
+def own_kernel(
+    queries_ref, other_ref, own_ref, rows_ref, other_rows_ref, largest_ref, totals_ref, summed_ref
+):
     token, width = queries_ref.shape
     heads = width // HD
     for head in range(heads):
-        rows_ref[head * token : (head + 1) * token, :] = queries_ref[:, head * HD : (head + 1) * HD]
+        rows, columns = slice(head * token, (head + 1) * token), slice(head * HD, (head + 1) * HD)
+        rows_ref[rows, :] = queries_ref[:, columns]
+        other_rows_ref[rows, :] = other_ref[:, columns]
     shape = (heads, token, token)
     causal = lax.broadcasted_iota(jnp.int32, shape, 2) <= lax.broadcasted_iota(jnp.int32, shape, 1)
     keys, values = own_ref[:token, :], own_ref[token:, :]
@@ -142,13 +146,12 @@
         packed_refs[0][count:, :] = jnp.where(lane < HD // 2, largest_ref[...], total)
 
 
-def finish_kernel(heads, largest_ref, totals_ref, summed_ref, packed_ref, out_ref):
-    token = out_ref.shape[0]
+def finish_kernel(largest_ref, totals_ref, summed_ref, packed_ref, out_ref):
+    token, width = out_ref.shape
     count = summed_ref.shape[0]
-    for at in range(heads):
-        first = (pl.program_id(0) * heads + at) * token
-        rows = pl.ds(pl.multiple_of(first, token), token)
-        packed = packed_ref[pl.ds(pl.multiple_of(count + first, token), token), :]
+    for head in range(width // HD):
+        rows = slice(head * token, (head + 1) * token)
+        packed = packed_ref[count + head * token : count + (head + 1) * token, :]
         largest = largest_ref[rows, :]
         other = packed[:, :1]
         top = jnp.maximum(largest, other)
@@ -156,7 +159,7 @@
         total = jnp.sum(totals_ref[rows, :], axis=1, keepdims=True) * mine
         total += packed[:, HD // 2 : HD // 2 + 1] * theirs
         summed = summed_ref[rows, :] * mine + packed_ref[rows, :] * theirs
-        out_ref[:, at * HD : (at + 1) * HD] = summed / total
+        out_ref[:, head * HD : (head + 1) * HD] = summed / total
 
 
 def params(rows, token, blocks):
@@ -170,18 +173,19 @@
     )
 
 
-def attend_own(queries, own):
+def attend_own(queries, other, own):
     token, width = queries.shape
-    rows = width // HD * token
-    sums = jax.ShapeDtypeStruct((rows, HD), jnp.float32)
+    count = width // HD * token
+    rows = jax.ShapeDtypeStruct((count, HD), jnp.bfloat16)
+    sums = jax.ShapeDtypeStruct((count, HD), jnp.float32)
     result = pl.pallas_call(
         own_kernel,
-        out_shape=[jax.ShapeDtypeStruct((rows, HD), jnp.bfloat16), sums, sums, sums],
-        in_specs=[VMEM] * 2,
-        out_specs=[VMEM] * 4,
-        **params(rows, token, 1),
-    )(queries, own)
-    return result[0], tuple(result[1:])
+        out_shape=[rows, rows, sums, sums, sums],
+        in_specs=[VMEM] * 3,
+        out_specs=[VMEM] * 5,
+        **params(count, token, 1),
+    )(queries, other, own)
+    return tuple(result[:2]), tuple(result[2:])
 
 
 def attend(starts, rows, states, items, groups, size_key, token, pack=False):
@@ -217,13 +221,11 @@
 
 def finish(sums, packed, shape):
     token, width = shape
-    heads = 2 if width % (2 * HD) == 0 else 1
     return pl.pallas_call(
-        functools.partial(finish_kernel, heads),
-        grid=(width // (heads * HD),),
+        finish_kernel,
         out_shape=jax.ShapeDtypeStruct(shape, jnp.float32),
         in_specs=[VMEM] * 4,
-        out_specs=pl.BlockSpec((token, heads * HD), lambda step: (0, step)),
+        out_specs=VMEM,
         **params(width // HD * token, token, 1),
     )(*sums, packed)
 
@@ -276,6 +278,7 @@
     assert size_query & (size_query - 1) == 0 and size_key & (size_key - 1) == 0 and size_query > 1
     starts = positions.reshape(-1, token)[:, 0]
     own = jnp.concatenate([keys, values], axis=0)
+    other = move(queries, 1, 1, 0)
     column = [own] + [move(own, 0, 0, place) for place in range(1, size_key)]
     half = max(size_key // 2, 1)
     held = [
@@ -283,8 +286,7 @@
         for base in range(0, size_key, half)
     ]
 
-    rows, sums = attend_own(queries, own)
-    rows = (rows, move(rows, 1, 1, 0))
+    rows, sums = attend_own(queries, other, own)
     plan = stages(size_query)
     if paired(size_query, size_key):
         (lower, upper), (one, two) = held, plan[0]
@@ -297,7 +299,7 @@
         mixed = (move(array, two, one, 0), shifted(parts, two, one))
         array, parts = near_up
         far_up = (move(array, two, one, 0), shifted(parts, two, one))
-        early = [[lower], [near, side]]
+        early = [[lower, near, side]]
         late = [[upper, near_up, mixed], [far_up]]
     else:
         early = [held]

time: 39.2 us -> 37.8 us (0.964)
  starting transfers between devices: 17.1 us -> 15.6 us
  waiting for transfers between devices: 5.59 us -> 6.87 us
  Pallas kernels: 15.3 us -> 14.1 us
    ppermute x10, starting transfers between devices: 17.1 us -> 15.6 us  [move(): return lax.ppermute(array, AXES, pairs)]
    ppermute x10, waiting for transfers between devices: 5.59 us -> 6.87 us  [move(): return lax.ppermute(array, AXES, pairs)]
    pallas_call x2, Pallas kernels: 2.7 us -> 2.11 us  [the longest x1 1.44 us: finish(): pl.pallas_call(finish_kernel, out_shape=jax.ShapeDtypeStruct(shape, jnp.f...]
    pallas_call x5 -> x4, Pallas kernels: 12.6 us -> 12 us  [attend(): pl.pallas_call(kernel, out_shape=outs, in_specs=[SMEM] + [VMEM] * (len(op...]
  transfers between devices with their start and end apart: 10 -> 10, of which waited for: 3 -> 4; matrix products, arithmetic and copies ran while one was open for 0% -> 0% of each run, Pallas kernels for 30% -> 29%
where the time goes in v3:
time: 37.8 us; the launch traced here: 37.7 us
  starting transfers between devices  15.6 us (41%)
  Pallas kernels  14.1 us (37%)
  waiting for transfers between devices  6.87 us (18%)
  local copies, waits for them, and re-layouts  0.98 us (3%)
    ppermute x10, starting transfers between devices, move(): return lax.ppermute(array, AXES, pairs)  15.6 us
    pallas_call x4, Pallas kernels, attend(): pl.pallas_call(kernel, out_shape=outs, in_specs=[SMEM] + [VMEM] * (len(op...  12 us
    ppermute x10, waiting for transfers between devices, move(): return lax.ppermute(array, AXES, pairs)  6.87 us
    pallas_call x1, Pallas kernels, finish(): pl.pallas_call(finish_kernel, out_shape=jax.ShapeDtypeStruct(shape, jnp.f...  1.44 us
    unnamed x9, local copies, waits for them, and re-layouts  0.84 us
  transfers between devices with their start and end apart: 10, of which 4 were waited for; matrix products, arithmetic and copies ran while one was open for 0% of the time, Pallas kernels for 29%

profile of v3, /device:TPU:29, one launch (start us, length us, event | category | flops | bytes accessed | tf_op | source)
XLA Modules:
  0.0 37.7 jit_solution(13797193842025429488)
XLA Ops:
  0.0 0.8 %constant_dynamic-update-slice_fusion.6 = (bf16[512,128]{1,0:T(8,128)(2,1)S(1)}, bf16[256,128]{1,0:T(8,128)(2,1)S(1)}) fusion(bf16[128,128]{1,0:T(8,128)(2,1)} %param.5), kind=kLoop, calls=%fused_computation.8 | loop fusion | bytes 98304
  0.8 0.2 collective-permute-start.4
  1.1 0.1 collective-permute-start.1
  1.1 2.9 %collective-permute-done.4 = bf16[256,128]{1,0:T(8,128)(2,1)S(1)} collective-permute-done((bf16[256,128]{1,0:T(8,128)(2,1)S(1)}, bf16[256,128]{1,0:T(8,128)(2,1)S(1)}, u32[]{:S(2)}, u32[]{:S(2)}) %collective-permute-start.4) | collective-permute-done | bytes 65568 | tf_op jit(solution)/shard_map/ppermute | solution.py:240
  4.0 0.3 collective-permute-start.5
  4.3 0.4 %collective-permute-start.2 = (bf16[256,128]{1,0:T(8,128)(2,1)S(1)}, bf16[256,128]{1,0:T(8,128)(2,1)S(1)}, u32[]{:S(2)}, u32[]{:S(2)}) collective-permute-start(bf16[256,128]{1,0:T(8,128)(2,1)S(1)} %get-tuple-element.42.own_ref), channel_id=1, source_target_pairs={{3,0},{2,1},{1,2},{0,3},{7,4},{6,5},{5,6},{4,7},{11,8},{10,9},{9,1... | collective-permute-start | bytes 196616 | tf_op jit(solution)/shard_map/ppermute | solution.py:240
  4.8 3.3 %collective-permute-start = (bf16[128,1024]{1,0:T(8,128)(2,1)S(1)}, bf16[128,1024]{1,0:T(8,128)(2,1)S(1)}, u32[]{:S(2)}, u32[]{:S(2)}) collective-permute-start(bf16[128,1024]{1,0:T(8,128)(2,1)S(1)} %copy-done), channel_id=1, source_target_pairs={{4,0},{5,1},{6,2},{7,3},{0,4},{1,5},{2,6},{3,7},{12,8},{13,9},{14,... | collective-permute-start | bytes 786440 | tf_op jit(solution)/shard_map/ppermute | solution.py:240
  8.1 0.0 collective-permute-done.1
  8.1 1.2 %collective-permute-done.2 = bf16[256,128]{1,0:T(8,128)(2,1)S(1)} collective-permute-done((bf16[256,128]{1,0:T(8,128)(2,1)S(1)}, bf16[256,128]{1,0:T(8,128)(2,1)S(1)}, u32[]{:S(2)}, u32[]{:S(2)}) %collective-permute-start.2) | collective-permute-done | bytes 65568 | tf_op jit(solution)/shard_map/ppermute | solution.py:240
  9.3 0.0 copy-start.2
  9.3 1.3 %collective-permute-start.6 = (bf16[1024,128]{1,0:T(8,128)(2,1)S(1)}, bf16[1024,128]{1,0:T(8,128)(2,1)S(1)}, u32[]{:S(2)}, u32[]{:S(2)}) collective-permute-start(bf16[1024,128]{1,0:T(8,128)(2,1)S(1)} %pad_maximum_fusion), channel_id=1, source_target_pairs={{16,0},{17,1},{18,2},{19,3},{12,4},{13,5},{14,6},{15,7},{24,8},{25... | collective-permute-start | bytes 786440 | tf_op jit(solution)/shard_map/ppermute | solution.py:240
  10.6 1.4 %collective-permute-start.3 = (bf16[512,128]{1,0:T(8,128)(2,1)S(1)}, bf16[512,128]{1,0:T(8,128)(2,1)S(1)}, u32[]{:S(2)}, u32[]{:S(2)}) collective-permute-start(bf16[512,128]{1,0:T(8,128)(2,1)S(1)} %constant_dynamic-update-slice_fusion.2.refs_2_), channel_id=1, source_target_pairs={{8,0},{9,1},{10,2},{11,3},{20,4},{21,5},{22,6},{23,7},{0,8},{1,9},... | collective-permute-start | bytes 393224 | tf_op jit(solution)/shard_map/ppermute | solution.py:240
  12.0 0.2 collective-permute-start.8
  12.1 0.1 slice_reduce_fusion.refs_0_
  12.3 2.2 %collective-permute-done.3.refs_3_ = bf16[512,128]{1,0:T(8,128)(2,1)S(1)} collective-permute-done((bf16[512,128]{1,0:T(8,128)(2,1)S(1)}, bf16[512,128]{1,0:T(8,128)(2,1)S(1)}, u32[]{:S(2)}, u32[]{:S(2)}) %collective-permute-start.3) | collective-permute-done | bytes 131104 | tf_op jit(solution)/shard_map/ppermute | solution.py:240
  14.5 0.3 collective-permute-start.7
  14.7 0.7 %shard_map.46 = (bf16[1024,128]{1,0:T(8,128)(2,1)S(1)}, bf16[1024,128]{1,0:T(8,128)(2,1)S(1)}, f32[1024,128]{1,0:T(8,128)S(1)}, f32[1024,128]{1,0:T(8,128)S(1)}, f32[1024,128]{1,0:T(8,128)S(1)}) custom-call(bf16[128,1024]{1,0:T(8,128)(2,1)S(1)} %copy-done, bf16[128,1024]{1,0:T(8,128)(2,1)S(1)} %collective-permute-done.other_ref, ...), custom_call_target="tpu_custom_call" | custom-call | flops 100663296 | bytes 1048576 | tf_op jit(solution)/shard_map/pallas_call | solution.py:181
  15.4 0.6 %collective-permute-done.8.refs_5_ = bf16[512,128]{1,0:T(8,128)(2,1)S(1)} collective-permute-done((bf16[512,128]{1,0:T(8,128)(2,1)S(1)}, bf16[512,128]{1,0:T(8,128)(2,1)S(1)}, u32[]{:S(2)}, u32[]{:S(2)}) %collective-permute-start.8) | collective-permute-done | bytes 131104 | tf_op jit(solution)/shard_map/ppermute | solution.py:240
  16.0 4.2 %shard_map.47 = (f32[1024,128]{1,0:T(8,128)S(1)}, f32[1024,128]{1,0:T(8,128)S(1)}, f32[1024,128]{1,0:T(8,128)S(1)}, f32[1024,128]{1,0:T(8,128)S(1)}, f32[1024,128]{1,0:T(8,128)S(1)}, /*index=5*/f32[1024,128]{1,0:T(8,128)S(1)}) custom-call(s32[32]{0:T(128)S(1)} %slice_reduce_fusion.refs_0_, ...), custom_call_target="tpu_custom_call", output_to_operand_aliasing={{0}: (6, {}), {1}: (7, {}), {2}: (8, {})} | custom-call | flops 1207959552 | bytes 1048576 | tf_op jit(solution)/shard_map/pallas_call | solution.py:207
  20.2 2.0 %shard_map.49 = (f32[1024,128]{1,0:T(8,128)S(1)}, f32[1024,128]{1,0:T(8,128)S(1)}, f32[1024,128]{1,0:T(8,128)S(1)}) custom-call(s32[32]{0:T(128)S(1)} %slice_reduce_fusion.refs_0_, bf16[1024,128]{1,0:T(8,128)(2,1)S(1)} %get-tuple-element.24.refs_2_.refs_1_, ...), custom_call_target="tpu_custom_call", output_to_operand_aliasing={{0}: (5, {}), {1}: (6, {}), {2}: (7, {})} | custom-call | flops 805306368 | bytes 1048576 | tf_op jit(solution)/shard_map/pallas_call | solution.py:207
  22.2 1.6 %shard_map.50 = (f32[1024,128]{1,0:T(8,128)S(1)}, f32[1024,128]{1,0:T(8,128)S(1)}, f32[1024,128]{1,0:T(8,128)S(1)}, f32[2048,128]{1,0:T(8,128)S(1)}) custom-call(s32[32]{0:T(128)S(1)} %slice_reduce_fusion.refs_0_, bf16[1024,128]{1,0:T(8,128)(2,1)S(1)} %get-tuple-element.24.refs_2_.refs_1_, ...), custom_call_target="tpu_custom_call", output_to_operand_aliasing={{0}: (3, {}), {1}: (4, {}), {2}: (5, {})} | custom-call | flops 201326592 | bytes 1048576 | tf_op jit(solution)/shard_map/pallas_call | solution.py:207
  23.8 8.2 %collective-permute-start.9 = (f32[2048,128]{1,0:T(8,128)S(1)}, f32[2048,128]{1,0:T(8,128)S(1)}, u32[]{:S(2)}, u32[]{:S(2)}) collective-permute-start(f32[2048,128]{1,0:T(8,128)S(1)} %get-tuple-element.40), channel_id=1, source_target_pairs={{4,0},{5,1},{6,2},{7,3},{0,4},{1,5},{2,6},{3,7},{12,8},{13,9},{14,... | collective-permute-start | bytes 3145736 | tf_op jit(solution)/shard_map/ppermute | solution.py:240
  32.0 4.2 %shard_map.48 = (f32[1024,128]{1,0:T(8,128)S(1)}, f32[1024,128]{1,0:T(8,128)S(1)}, f32[1024,128]{1,0:T(8,128)S(1)}) custom-call(s32[32]{0:T(128)S(1)} %slice_reduce_fusion.refs_0_, bf16[1024,128]{1,0:T(8,128)(2,1)S(1)} %get-tuple-element.23.refs_1_, ...), custom_call_target="tpu_custom_call", output_to_operand_aliasing={{0}: (6, {}), {1}: (7, {}), {2}: (8, {})} | custom-call | flops 1006632960 | bytes 1048576 | tf_op jit(solution)/shard_map/pallas_call | solution.py:207
  36.3 1.4 %shard_map.51 = f32[128,1024]{1,0:T(8,128)} custom-call(f32[1024,128]{1,0:T(8,128)S(1)} %get-tuple-element.31.largest_ref, f32[1024,128]{1,0:T(8,128)S(1)} %get-tuple-element.32.totals_ref, f32[1024,128]{1,0:T(8,128)S(1)} %get-tuple-element.33.summed_ref, f32[2048,128]{1,0:T(8,128)S(1)} %collective-permute-done.9.packed_ref), custom_call_target="tpu_custom_call" | custom-call | flops 100663296 | bytes 1048576 | tf_op jit(solution)/shard_map/pallas_call | solution.py:224
  (15 shorter events, 0.1 us)
Async XLA Ops:
  0.0 0.8 %copy-start.1 = (bf16[128,128]{1,0:T(8,128)(2,1)S(1)}, bf16[128,128]{1,0:T(8,128)(2,1)}, u32[]{:S(2)}) copy-start(bf16[128,128]{1,0:T(8,128)(2,1)} %param.6) | copy-start | bytes 98308
  0.0 4.8 %copy-start = (bf16[128,1024]{1,0:T(8,128)(2,1)S(1)}, bf16[128,1024]{1,0:T(8,128)(2,1)}, u32[]{:S(2)}) copy-start(bf16[128,1024]{1,0:T(8,128)(2,1)} %queries_ref.1) | copy-start | bytes 786436
  0.8 3.2 %collective-permute-start.4 = (bf16[256,128]{1,0:T(8,128)(2,1)S(1)}, bf16[256,128]{1,0:T(8,128)(2,1)S(1)}, u32[]{:S(2)}, u32[]{:S(2)}) collective-permute-start(bf16[256,128]{1,0:T(8,128)(2,1)S(1)} %get-tuple-element.42.own_ref), channel_id=1, source_target_pairs={{1,0},{0,1},{3,2},{2,3},{5,4},{4,5},{7,6},{6,7},{9,8},{8,9},{11,10... | collective-permute-start | bytes 196616 | tf_op jit(solution)/shard_map/ppermute | solution.py:240
  1.1 7.0 %collective-permute-start.1 = (bf16[256,128]{1,0:T(8,128)(2,1)S(1)}, bf16[256,128]{1,0:T(8,128)(2,1)S(1)}, u32[]{:S(2)}, u32[]{:S(2)}) collective-permute-start(bf16[256,128]{1,0:T(8,128)(2,1)S(1)} %get-tuple-element.42.own_ref), channel_id=1, source_target_pairs={{2,0},{3,1},{0,2},{1,3},{6,4},{7,5},{4,6},{5,7},{10,8},{11,9},{8,1... | collective-permute-start | bytes 196616 | tf_op jit(solution)/shard_map/ppermute | solution.py:240
  4.0 5.2 %collective-permute-start.5 = (bf16[512,128]{1,0:T(8,128)(2,1)S(1)}, bf16[512,128]{1,0:T(8,128)(2,1)S(1)}, u32[]{:S(2)}, u32[]{:S(2)}) collective-permute-start(bf16[512,128]{1,0:T(8,128)(2,1)S(1)} %constant_dynamic-update-slice_fusion.4.refs_3_), channel_id=1, source_target_pairs={{8,0},{9,1},{10,2},{11,3},{20,4},{21,5},{22,6},{23,7},{0,8},{1,9},... | collective-permute-start | bytes 393224 | tf_op jit(solution)/shard_map/ppermute | solution.py:240
  4.3 4.9 %collective-permute-start.2 = (bf16[256,128]{1,0:T(8,128)(2,1)S(1)}, bf16[256,128]{1,0:T(8,128)(2,1)S(1)}, u32[]{:S(2)}, u32[]{:S(2)}) collective-permute-start(bf16[256,128]{1,0:T(8,128)(2,1)S(1)} %get-tuple-element.42.own_ref), channel_id=1, source_target_pairs={{3,0},{2,1},{1,2},{0,3},{7,4},{6,5},{5,6},{4,7},{11,8},{10,9},{9,1... | collective-permute-start | bytes 196616 | tf_op jit(solution)/shard_map/ppermute | solution.py:240
  4.8 9.9 %collective-permute-start = (bf16[128,1024]{1,0:T(8,128)(2,1)S(1)}, bf16[128,1024]{1,0:T(8,128)(2,1)S(1)}, u32[]{:S(2)}, u32[]{:S(2)}) collective-permute-start(bf16[128,1024]{1,0:T(8,128)(2,1)S(1)} %copy-done), channel_id=1, source_target_pairs={{4,0},{5,1},{6,2},{7,3},{0,4},{1,5},{2,6},{3,7},{12,8},{13,9},{14,... | collective-permute-start | bytes 786440 | tf_op jit(solution)/shard_map/ppermute | solution.py:240
  9.3 2.9 %copy-start.2 = (s32[4096]{0:T(1024)S(1)}, s32[4096]{0:T(1024)}, u32[]{:S(2)}) copy-start(s32[4096]{0:T(1024)} %param.7) | copy-start | bytes 49156
  9.3 10.9 %collective-permute-start.6 = (bf16[1024,128]{1,0:T(8,128)(2,1)S(1)}, bf16[1024,128]{1,0:T(8,128)(2,1)S(1)}, u32[]{:S(2)}, u32[]{:S(2)}) collective-permute-start(bf16[1024,128]{1,0:T(8,128)(2,1)S(1)} %pad_maximum_fusion), channel_id=1, source_target_pairs={{16,0},{17,1},{18,2},{19,3},{12,4},{13,5},{14,6},{15,7},{24,8},{25... | collective-permute-start | bytes 786440 | tf_op jit(solution)/shard_map/ppermute | solution.py:240
  10.6 3.9 %collective-permute-start.3 = (bf16[512,128]{1,0:T(8,128)(2,1)S(1)}, bf16[512,128]{1,0:T(8,128)(2,1)S(1)}, u32[]{:S(2)}, u32[]{:S(2)}) collective-permute-start(bf16[512,128]{1,0:T(8,128)(2,1)S(1)} %constant_dynamic-update-slice_fusion.2.refs_2_), channel_id=1, source_target_pairs={{8,0},{9,1},{10,2},{11,3},{20,4},{21,5},{22,6},{23,7},{0,8},{1,9},... | collective-permute-start | bytes 393224 | tf_op jit(solution)/shard_map/ppermute | solution.py:240
  12.0 4.0 %collective-permute-start.8 = (bf16[512,128]{1,0:T(8,128)(2,1)S(1)}, bf16[512,128]{1,0:T(8,128)(2,1)S(1)}, u32[]{:S(2)}, u32[]{:S(2)}) collective-permute-start(bf16[512,128]{1,0:T(8,128)(2,1)S(1)} %constant_dynamic-update-slice_fusion.4.refs_3_), channel_id=1, source_target_pairs={{16,0},{17,1},{18,2},{19,3},{12,4},{13,5},{14,6},{15,7},{24,8},{25... | collective-permute-start | bytes 393224 | tf_op jit(solution)/shard_map/ppermute | solution.py:240
  14.5 7.7 %collective-permute-start.7 = (bf16[512,128]{1,0:T(8,128)(2,1)S(1)}, bf16[512,128]{1,0:T(8,128)(2,1)S(1)}, u32[]{:S(2)}, u32[]{:S(2)}) collective-permute-start(bf16[512,128]{1,0:T(8,128)(2,1)S(1)} %collective-permute-done.3.refs_3_), channel_id=1, source_target_pairs={{16,0},{17,1},{18,2},{19,3},{12,4},{13,5},{14,6},{15,7},{24,8},{25... | collective-permute-start | bytes 393224 | tf_op jit(solution)/shard_map/ppermute | solution.py:240
  23.8 12.5 %collective-permute-start.9 = (f32[2048,128]{1,0:T(8,128)S(1)}, f32[2048,128]{1,0:T(8,128)S(1)}, u32[]{:S(2)}, u32[]{:S(2)}) collective-permute-start(f32[2048,128]{1,0:T(8,128)S(1)} %get-tuple-element.40), channel_id=1, source_target_pairs={{4,0},{5,1},{6,2},{7,3},{0,4},{1,5},{2,6},{3,7},{12,8},{13,9},{14,... | collective-permute-start | bytes 3145736 | tf_op jit(solution)/shard_map/ppermute | solution.py:240

commit v4 on v3

--- a/solution.py
+++ b/solution.py
@@ -51,6 +51,18 @@
 TO_LOG2 = math.log2(math.e) / HD**0.5
 
 
+def pack_kernel(keys_ref, values_ref, out_ref, done):
+    token = keys_ref.shape[0]
+    copies = [
+        pltpu.make_async_copy(keys_ref, out_ref.at[:token, :], done.at[0]),
+        pltpu.make_async_copy(values_ref, out_ref.at[token:, :], done.at[1]),
+    ]
+    for copy in copies:
+        copy.start()
+    for copy in copies:
+        copy.wait()
+
+
 def own_kernel(
     queries_ref, other_ref, own_ref, rows_ref, other_rows_ref, largest_ref, totals_ref, summed_ref
 ):
@@ -171,6 +183,18 @@
             bytes_accessed=1 << 20,
         ),
     )
+
+
+def packed_blocks(keys, values):
+    token, width = keys.shape
+    return pl.pallas_call(
+        pack_kernel,
+        out_shape=jax.ShapeDtypeStruct((2 * token, width), keys.dtype),
+        in_specs=[pl.BlockSpec(memory_space=pltpu.HBM)] * 2,
+        out_specs=VMEM,
+        scratch_shapes=[pltpu.SemaphoreType.DMA((2,))],
+        compiler_params=pltpu.CompilerParams(vmem_limit_bytes=LIMIT),
+    )(*(pltpu.with_memory_space_constraint(array, pltpu.HBM) for array in (keys, values)))
 
 
 def attend_own(queries, other, own):
@@ -265,19 +289,12 @@
     return tuple((at, number, base, one ^ even, two ^ odd) for at, number, base, one, two in parts)
 
 
-def joined(first, second):
-    (one, parts), (two, more) = first, second
-    skip = sum(number for _, number, *_ in parts)
-    more = tuple((at + skip, *rest) for at, *rest in more)
-    return jnp.concatenate([one, two], axis=0), parts + more
-
-
 def gathered_attention(queries, keys, values, positions):
     token = queries.shape[0]
     size_query, size_key = lax.axis_size("pb"), lax.axis_size("ka")
     assert size_query & (size_query - 1) == 0 and size_key & (size_key - 1) == 0 and size_query > 1
     starts = positions.reshape(-1, token)[:, 0]
-    own = jnp.concatenate([keys, values], axis=0)
+    own = packed_blocks(keys, values)
     other = move(queries, 1, 1, 0)
     column = [own] + [move(own, 0, 0, place) for place in range(1, size_key)]
     half = max(size_key // 2, 1)
@@ -290,17 +307,10 @@
     plan = stages(size_query)
     if paired(size_query, size_key):
         (lower, upper), (one, two) = held, plan[0]
-        array, parts = lower
-        near = (move(array, one, two, 0), shifted(parts, one, two))
-        side = (move(array, two, one, 0), shifted(parts, two, one))
-        array, parts = upper
-        near_up = (move(array, one, two, 0), shifted(parts, one, two))
-        array, parts = joined(near, upper)
-        mixed = (move(array, two, one, 0), shifted(parts, two, one))
-        array, parts = near_up
-        far_up = (move(array, two, one, 0), shifted(parts, two, one))
-        early = [[lower, near, side]]
-        late = [[upper, near_up, mixed], [far_up]]
+        near, side, far = spread(lower, (one, two))
+        near_up, side_up, far_up = spread(upper, (one, two))
+        early = [[lower], [near, side], [far, upper]]
+        late = [[near_up, side_up, far_up]]
     else:
         early = [held]
         for bits in plan:

time: 37.8 us -> 35.4 us (0.937)
  the two profiles are of different devices: /device:TPU:29 before, /device:TPU:0 now
where the time goes in v4:
time: 35.4 us; the launch traced here: 35.2 us
  Pallas kernels  15.2 us (43%)
  starting transfers between devices  14.2 us (40%)
  waiting for transfers between devices  5.44 us (15%)
    ppermute x11, starting transfers between devices, move(): return lax.ppermute(array, AXES, pairs)  14.2 us
    pallas_call x5, Pallas kernels, attend(): pl.pallas_call(kernel, out_shape=outs, in_specs=[SMEM] + [VMEM] * (len(op...  12.3 us
    ppermute x11, waiting for transfers between devices, move(): return lax.ppermute(array, AXES, pairs)  5.44 us
    pallas_call x1, Pallas kernels, finish(): pl.pallas_call(finish_kernel, out_shape=jax.ShapeDtypeStruct(shape, jnp.f...  1.44 us
    pallas_call x1, Pallas kernels, packed_blocks(): pl.pallas_call(pack_kernel, out_shape=jax.ShapeDtypeStruct((2 * token, wi...  0.79 us
  transfers between devices with their start and end apart: 11, of which 3 were waited for; matrix products, arithmetic and copies ran while one was open for 0% of the time, Pallas kernels for 31%

profile of v4, /device:TPU:0, one launch (start us, length us, event | category | flops | bytes accessed | tf_op | source)
XLA Modules:
  0.0 35.2 jit_solution(15173220155591567972)
XLA Ops:
  0.0 0.8 %shard_map.46.own_ref = bf16[256,128]{1,0:T(8,128)(2,1)S(1)} custom-call(bf16[128,128]{1,0:T(8,128)(2,1)} %keys_ref.1, bf16[128,128]{1,0:T(8,128)(2,1)} %values_ref.1), custom_call_target="tpu_custom_call" | custom-call | tf_op jit(solution)/shard_map/pallas_call | solution.py:190
  0.8 0.0 copy-start
  0.8 3.1 %collective-permute-start.6 = (bf16[256,128]{1,0:T(8,128)(2,1)S(1)}, bf16[256,128]{1,0:T(8,128)(2,1)S(1)}, u32[]{:S(2)}, u32[]{:S(2)}) collective-permute-start(bf16[256,128]{1,0:T(8,128)(2,1)S(1)} %shard_map.46.own_ref), channel_id=1, source_target_pairs={{1,0},{0,1},{3,2},{2,3},{5,4},{4,5},{7,6},{6,7},{9,8},{8,9},{11,10... | collective-permute-start | bytes 196616 | tf_op jit(solution)/shard_map/ppermute | solution.py:264
  3.9 2.6 %collective-permute-start.1 = (bf16[256,128]{1,0:T(8,128)(2,1)S(1)}, bf16[256,128]{1,0:T(8,128)(2,1)S(1)}, u32[]{:S(2)}, u32[]{:S(2)}) collective-permute-start(bf16[256,128]{1,0:T(8,128)(2,1)S(1)} %shard_map.46.own_ref), channel_id=1, source_target_pairs={{2,0},{3,1},{0,2},{1,3},{6,4},{7,5},{4,6},{5,7},{10,8},{11,9},{8,1... | collective-permute-start | bytes 196616 | tf_op jit(solution)/shard_map/ppermute | solution.py:264
  6.5 1.8 %collective-permute-start.7 = (bf16[512,128]{1,0:T(8,128)(2,1)S(1)}, bf16[512,128]{1,0:T(8,128)(2,1)S(1)}, u32[]{:S(2)}, u32[]{:S(2)}) collective-permute-start(bf16[512,128]{1,0:T(8,128)(2,1)S(1)} %pad_maximum_fusion.refs_3_), channel_id=1, source_target_pairs={{8,0},{9,1},{10,2},{11,3},{20,4},{21,5},{22,6},{23,7},{0,8},{1,9},... | collective-permute-start | bytes 393224 | tf_op jit(solution)/shard_map/ppermute | solution.py:264
  8.3 2.9 %collective-permute-done.1 = bf16[256,128]{1,0:T(8,128)(2,1)S(1)} collective-permute-done((bf16[256,128]{1,0:T(8,128)(2,1)S(1)}, bf16[256,128]{1,0:T(8,128)(2,1)S(1)}, u32[]{:S(2)}, u32[]{:S(2)}) %collective-permute-start.1) | collective-permute-done | bytes 65568 | tf_op jit(solution)/shard_map/ppermute | solution.py:264
  11.2 1.4 %collective-permute-done.2 = bf16[256,128]{1,0:T(8,128)(2,1)S(1)} collective-permute-done((bf16[256,128]{1,0:T(8,128)(2,1)S(1)}, bf16[256,128]{1,0:T(8,128)(2,1)S(1)}, u32[]{:S(2)}, u32[]{:S(2)}) %collective-permute-start.2) | collective-permute-done | bytes 65568 | tf_op jit(solution)/shard_map/ppermute | solution.py:264
  12.6 1.6 %collective-permute-start.3 = (bf16[512,128]{1,0:T(8,128)(2,1)S(1)}, bf16[512,128]{1,0:T(8,128)(2,1)S(1)}, u32[]{:S(2)}, u32[]{:S(2)}) collective-permute-start(bf16[512,128]{1,0:T(8,128)(2,1)S(1)} %constant_dynamic-update-slice_fusion.refs_4_), channel_id=1, source_target_pairs={{8,0},{9,1},{10,2},{11,3},{20,4},{21,5},{22,6},{23,7},{0,8},{1,9},... | collective-permute-start | bytes 393224 | tf_op jit(solution)/shard_map/ppermute | solution.py:264
  14.2 1.5 %collective-permute-start.9 = (bf16[512,128]{1,0:T(8,128)(2,1)S(1)}, bf16[512,128]{1,0:T(8,128)(2,1)S(1)}, u32[]{:S(2)}, u32[]{:S(2)}) collective-permute-start(bf16[512,128]{1,0:T(8,128)(2,1)S(1)} %pad_maximum_fusion.refs_3_), channel_id=1, source_target_pairs={{16,0},{17,1},{18,2},{19,3},{12,4},{13,5},{14,6},{15,7},{24,8},{25... | collective-permute-start | bytes 393224 | tf_op jit(solution)/shard_map/ppermute | solution.py:264
  15.7 0.0 collective-permute-done.7.refs_3_
  15.7 0.5 %collective-permute-start.8 = (bf16[512,128]{1,0:T(8,128)(2,1)S(1)}, bf16[512,128]{1,0:T(8,128)(2,1)S(1)}, u32[]{:S(2)}, u32[]{:S(2)}) collective-permute-start(bf16[512,128]{1,0:T(8,128)(2,1)S(1)} %collective-permute-done.7.refs_3_), channel_id=1, source_target_pairs={{16,0},{17,1},{18,2},{19,3},{12,4},{13,5},{14,6},{15,7},{24,8},{25... | collective-permute-start | bytes 393224 | tf_op jit(solution)/shard_map/ppermute | solution.py:264
  16.2 0.1 slice_reduce_fusion.refs_0_
  16.3 1.6 %collective-permute-start.4 = (bf16[512,128]{1,0:T(8,128)(2,1)S(1)}, bf16[512,128]{1,0:T(8,128)(2,1)S(1)}, u32[]{:S(2)}, u32[]{:S(2)}) collective-permute-start(bf16[512,128]{1,0:T(8,128)(2,1)S(1)} %constant_dynamic-update-slice_fusion.refs_4_), channel_id=1, source_target_pairs={{16,0},{17,1},{18,2},{19,3},{12,4},{13,5},{14,6},{15,7},{24,8},{25... | collective-permute-start | bytes 393224 | tf_op jit(solution)/shard_map/ppermute | solution.py:264
  17.9 1.2 %collective-permute-done.3.refs_2_ = bf16[512,128]{1,0:T(8,128)(2,1)S(1)} collective-permute-done((bf16[512,128]{1,0:T(8,128)(2,1)S(1)}, bf16[512,128]{1,0:T(8,128)(2,1)S(1)}, u32[]{:S(2)}, u32[]{:S(2)}) %collective-permute-start.3) | collective-permute-done | bytes 131104 | tf_op jit(solution)/shard_map/ppermute | solution.py:264
  19.0 1.5 %collective-permute-start.5 = (bf16[512,128]{1,0:T(8,128)(2,1)S(1)}, bf16[512,128]{1,0:T(8,128)(2,1)S(1)}, u32[]{:S(2)}, u32[]{:S(2)}) collective-permute-start(bf16[512,128]{1,0:T(8,128)(2,1)S(1)} %collective-permute-done.3.refs_2_), channel_id=1, source_target_pairs={{16,0},{17,1},{18,2},{19,3},{12,4},{13,5},{14,6},{15,7},{24,8},{25... | collective-permute-start | bytes 393224 | tf_op jit(solution)/shard_map/ppermute | solution.py:264
  20.6 0.7 %shard_map.47 = (bf16[1024,128]{1,0:T(8,128)(2,1)S(1)}, bf16[1024,128]{1,0:T(8,128)(2,1)S(1)}, f32[1024,128]{1,0:T(8,128)S(1)}, f32[1024,128]{1,0:T(8,128)S(1)}, f32[1024,128]{1,0:T(8,128)S(1)}) custom-call(bf16[128,1024]{1,0:T(8,128)(2,1)S(1)} %copy-done, bf16[128,1024]{1,0:T(8,128)(2,1)S(1)} %collective-permute-done.other_ref, ...), custom_call_target="tpu_custom_call" | custom-call | flops 100663296 | bytes 1048576 | tf_op jit(solution)/shard_map/pallas_call | solution.py:205
  21.2 1.4 %shard_map.48 = (f32[1024,128]{1,0:T(8,128)S(1)}, f32[1024,128]{1,0:T(8,128)S(1)}, f32[1024,128]{1,0:T(8,128)S(1)}, f32[1024,128]{1,0:T(8,128)S(1)}, f32[1024,128]{1,0:T(8,128)S(1)}, /*index=5*/f32[1024,128]{1,0:T(8,128)S(1)}) custom-call(s32[32]{0:T(128)S(1)} %slice_reduce_fusion.refs_0_, ...), custom_call_target="tpu_custom_call", output_to_operand_aliasing={{0}: (4, {}), {1}: (5, {}), {2}: (6, {})} | custom-call | flops 402653184 | bytes 1048576 | tf_op jit(solution)/shard_map/pallas_call | solution.py:231
  22.7 3.0 %shard_map.49 = (f32[1024,128]{1,0:T(8,128)S(1)}, f32[1024,128]{1,0:T(8,128)S(1)}, f32[1024,128]{1,0:T(8,128)S(1)}, f32[1024,128]{1,0:T(8,128)S(1)}, f32[1024,128]{1,0:T(8,128)S(1)}, /*index=5*/f32[1024,128]{1,0:T(8,128)S(1)}) custom-call(s32[32]{0:T(128)S(1)} %slice_reduce_fusion.refs_0_, ...), custom_call_target="tpu_custom_call", output_to_operand_aliasing={{0}: (5, {}), {1}: (6, {}), {2}: (7, {}), {3}: (8, {}), {4}... | custom-call | flops 805306368 | bytes 1048576 | tf_op jit(solution)/shard_map/pallas_call | solution.py:231
  25.7 0.0 collective-permute-done.8.refs_3_
  25.8 3.0 %shard_map.50 = (f32[1024,128]{1,0:T(8,128)S(1)}, f32[1024,128]{1,0:T(8,128)S(1)}, f32[1024,128]{1,0:T(8,128)S(1)}, f32[1024,128]{1,0:T(8,128)S(1)}, f32[1024,128]{1,0:T(8,128)S(1)}, /*index=5*/f32[1024,128]{1,0:T(8,128)S(1)}) custom-call(s32[32]{0:T(128)S(1)} %slice_reduce_fusion.refs_0_, ...), custom_call_target="tpu_custom_call", output_to_operand_aliasing={{0}: (5, {}), {1}: (6, {}), {2}: (7, {}), {3}: (8, {}), {4}... | custom-call | flops 805306368 | bytes 1048576 | tf_op jit(solution)/shard_map/pallas_call | solution.py:231
  28.8 2.2 %shard_map.52 = (f32[1024,128]{1,0:T(8,128)S(1)}, f32[1024,128]{1,0:T(8,128)S(1)}, f32[1024,128]{1,0:T(8,128)S(1)}, f32[2048,128]{1,0:T(8,128)S(1)}) custom-call(s32[32]{0:T(128)S(1)} %slice_reduce_fusion.refs_0_, bf16[1024,128]{1,0:T(8,128)(2,1)S(1)} %get-tuple-element.33.refs_2_.refs_1_, ...), custom_call_target="tpu_custom_call", output_to_operand_aliasing={{0}: (5, {}), {1}: (6, {}), {2}: (7, {})} | custom-call | flops 603979776 | bytes 1048576 | tf_op jit(solution)/shard_map/pallas_call | solution.py:231
  31.0 0.1 collective-permute-start.10
  31.1 2.7 %shard_map.51 = (f32[1024,128]{1,0:T(8,128)S(1)}, f32[1024,128]{1,0:T(8,128)S(1)}, f32[1024,128]{1,0:T(8,128)S(1)}) custom-call(s32[32]{0:T(128)S(1)} %slice_reduce_fusion.refs_0_, bf16[1024,128]{1,0:T(8,128)(2,1)S(1)} %get-tuple-element.32.refs_1_, ...), custom_call_target="tpu_custom_call", output_to_operand_aliasing={{0}: (5, {}), {1}: (6, {}), {2}: (7, {})} | custom-call | flops 603979776 | bytes 1048576 | tf_op jit(solution)/shard_map/pallas_call | solution.py:231
  33.7 1.4 %shard_map.53 = f32[128,1024]{1,0:T(8,128)} custom-call(f32[1024,128]{1,0:T(8,128)S(1)} %get-tuple-element.52.largest_ref, f32[1024,128]{1,0:T(8,128)S(1)} %get-tuple-element.53.totals_ref, f32[1024,128]{1,0:T(8,128)S(1)} %get-tuple-element.54.summed_ref, f32[2048,128]{1,0:T(8,128)S(1)} %collective-permute-done.10.packed_ref), custom_call_target="tpu_custom_call" | custom-call | flops 100663296 | bytes 1048576 | tf_op jit(solution)/shard_map/pallas_call | solution.py:248
  (14 shorter events, 0.1 us)
Async XLA Ops:
  0.8 19.8 %copy-start = (bf16[128,1024]{1,0:T(8,128)(2,1)S(1)}, bf16[128,1024]{1,0:T(8,128)(2,1)}, u32[]{:S(2)}) copy-start(bf16[128,1024]{1,0:T(8,128)(2,1)} %queries_ref.1) | copy-start | bytes 786436
  0.8 5.7 %collective-permute-start.6 = (bf16[256,128]{1,0:T(8,128)(2,1)S(1)}, bf16[256,128]{1,0:T(8,128)(2,1)S(1)}, u32[]{:S(2)}, u32[]{:S(2)}) collective-permute-start(bf16[256,128]{1,0:T(8,128)(2,1)S(1)} %shard_map.46.own_ref), channel_id=1, source_target_pairs={{1,0},{0,1},{3,2},{2,3},{5,4},{4,5},{7,6},{6,7},{9,8},{8,9},{11,10... | collective-permute-start | bytes 196616 | tf_op jit(solution)/shard_map/ppermute | solution.py:264
  3.9 7.3 %collective-permute-start.1 = (bf16[256,128]{1,0:T(8,128)(2,1)S(1)}, bf16[256,128]{1,0:T(8,128)(2,1)S(1)}, u32[]{:S(2)}, u32[]{:S(2)}) collective-permute-start(bf16[256,128]{1,0:T(8,128)(2,1)S(1)} %shard_map.46.own_ref), channel_id=1, source_target_pairs={{2,0},{3,1},{0,2},{1,3},{6,4},{7,5},{4,6},{5,7},{10,8},{11,9},{8,1... | collective-permute-start | bytes 196616 | tf_op jit(solution)/shard_map/ppermute | solution.py:264
  6.5 6.1 %collective-permute-start.2 = (bf16[256,128]{1,0:T(8,128)(2,1)S(1)}, bf16[256,128]{1,0:T(8,128)(2,1)S(1)}, u32[]{:S(2)}, u32[]{:S(2)}) collective-permute-start(bf16[256,128]{1,0:T(8,128)(2,1)S(1)} %shard_map.46.own_ref), channel_id=1, source_target_pairs={{3,0},{2,1},{1,2},{0,3},{7,4},{6,5},{5,6},{4,7},{11,8},{10,9},{9,1... | collective-permute-start | bytes 196616 | tf_op jit(solution)/shard_map/ppermute | solution.py:264
  6.5 14.0 %collective-permute-start = (bf16[128,1024]{1,0:T(8,128)(2,1)}, bf16[128,1024]{1,0:T(8,128)(2,1)S(1)}, u32[]{:S(2)}, u32[]{:S(2)}) collective-permute-start(bf16[128,1024]{1,0:T(8,128)(2,1)} %queries_ref.1), channel_id=1, source_target_pairs={{4,0},{5,1},{6,2},{7,3},{0,4},{1,5},{2,6},{3,7},{12,8},{13,9},{14,... | collective-permute-start | bytes 786440 | tf_op jit(solution)/shard_map/ppermute | solution.py:264
  6.5 9.1 %collective-permute-start.7 = (bf16[512,128]{1,0:T(8,128)(2,1)S(1)}, bf16[512,128]{1,0:T(8,128)(2,1)S(1)}, u32[]{:S(2)}, u32[]{:S(2)}) collective-permute-start(bf16[512,128]{1,0:T(8,128)(2,1)S(1)} %pad_maximum_fusion.refs_3_), channel_id=1, source_target_pairs={{8,0},{9,1},{10,2},{11,3},{20,4},{21,5},{22,6},{23,7},{0,8},{1,9},... | collective-permute-start | bytes 393224 | tf_op jit(solution)/shard_map/ppermute | solution.py:264
  11.2 5.0 %copy-start.1 = (s32[4096]{0:T(1024)S(1)}, s32[4096]{0:T(1024)}, u32[]{:S(2)}) copy-start(s32[4096]{0:T(1024)} %param.7) | copy-start | bytes 49156
  12.6 6.4 %collective-permute-start.3 = (bf16[512,128]{1,0:T(8,128)(2,1)S(1)}, bf16[512,128]{1,0:T(8,128)(2,1)S(1)}, u32[]{:S(2)}, u32[]{:S(2)}) collective-permute-start(bf16[512,128]{1,0:T(8,128)(2,1)S(1)} %constant_dynamic-update-slice_fusion.refs_4_), channel_id=1, source_target_pairs={{8,0},{9,1},{10,2},{11,3},{20,4},{21,5},{22,6},{23,7},{0,8},{1,9},... | collective-permute-start | bytes 393224 | tf_op jit(solution)/shard_map/ppermute | solution.py:264
  14.2 8.5 %collective-permute-start.9 = (bf16[512,128]{1,0:T(8,128)(2,1)S(1)}, bf16[512,128]{1,0:T(8,128)(2,1)S(1)}, u32[]{:S(2)}, u32[]{:S(2)}) collective-permute-start(bf16[512,128]{1,0:T(8,128)(2,1)S(1)} %pad_maximum_fusion.refs_3_), channel_id=1, source_target_pairs={{16,0},{17,1},{18,2},{19,3},{12,4},{13,5},{14,6},{15,7},{24,8},{25... | collective-permute-start | bytes 393224 | tf_op jit(solution)/shard_map/ppermute | solution.py:264
  15.7 10.1 %collective-permute-start.8 = (bf16[512,128]{1,0:T(8,128)(2,1)S(1)}, bf16[512,128]{1,0:T(8,128)(2,1)S(1)}, u32[]{:S(2)}, u32[]{:S(2)}) collective-permute-start(bf16[512,128]{1,0:T(8,128)(2,1)S(1)} %collective-permute-done.7.refs_3_), channel_id=1, source_target_pairs={{16,0},{17,1},{18,2},{19,3},{12,4},{13,5},{14,6},{15,7},{24,8},{25... | collective-permute-start | bytes 393224 | tf_op jit(solution)/shard_map/ppermute | solution.py:264
  16.3 12.5 %collective-permute-start.4 = (bf16[512,128]{1,0:T(8,128)(2,1)S(1)}, bf16[512,128]{1,0:T(8,128)(2,1)S(1)}, u32[]{:S(2)}, u32[]{:S(2)}) collective-permute-start(bf16[512,128]{1,0:T(8,128)(2,1)S(1)} %constant_dynamic-update-slice_fusion.refs_4_), channel_id=1, source_target_pairs={{16,0},{17,1},{18,2},{19,3},{12,4},{13,5},{14,6},{15,7},{24,8},{25... | collective-permute-start | bytes 393224 | tf_op jit(solution)/shard_map/ppermute | solution.py:264
  19.0 9.8 %collective-permute-start.5 = (bf16[512,128]{1,0:T(8,128)(2,1)S(1)}, bf16[512,128]{1,0:T(8,128)(2,1)S(1)}, u32[]{:S(2)}, u32[]{:S(2)}) collective-permute-start(bf16[512,128]{1,0:T(8,128)(2,1)S(1)} %collective-permute-done.3.refs_2_), channel_id=1, source_target_pairs={{16,0},{17,1},{18,2},{19,3},{12,4},{13,5},{14,6},{15,7},{24,8},{25... | collective-permute-start | bytes 393224 | tf_op jit(solution)/shard_map/ppermute | solution.py:264
  31.0 2.8 %collective-permute-start.10 = (f32[2048,128]{1,0:T(8,128)S(1)}, f32[2048,128]{1,0:T(8,128)S(1)}, u32[]{:S(2)}, u32[]{:S(2)}) collective-permute-start(f32[2048,128]{1,0:T(8,128)S(1)} %get-tuple-element.58), channel_id=1, source_target_pairs={{4,0},{5,1},{6,2},{7,3},{0,4},{1,5},{2,6},{3,7},{12,8},{13,9},{14,... | collective-permute-start | bytes 3145736 | tf_op jit(solution)/shard_map/ppermute | solution.py:264

commit v5 on v4

--- a/solution.py
+++ b/solution.py
@@ -19,13 +19,15 @@
 SMEM = pl.BlockSpec(memory_space=pltpu.SMEM)
 
 
-def combine(rows, keys, values, sums, to_log2, mask=None):
+def combine(rows, keys, values, sums, to_log2, mask=None, last_counts=None):
     score = lax.dot_general(
         rows, keys, (((1,), (1,)), ((), ())), preferred_element_type=jnp.float32
     )
     if mask is not None:
         score = jnp.where(mask, score, BIG)
     parts = [score[:, at : at + HD] for at in range(0, keys.shape[0], HD)]
+    if last_counts is not None:
+        parts[-1] = jnp.where(last_counts, parts[-1], BIG)
     top = jnp.max(functools.reduce(jnp.maximum, parts), axis=1, keepdims=True)
     if sums is None:
         top = jnp.broadcast_to(top, (rows.shape[0], HD))
@@ -35,12 +37,19 @@
     if mask is not None:
         weights = [jnp.where(mask, weight, 0.0) for weight in weights]
     total = functools.reduce(jnp.add, weights)
-    weight = jnp.concatenate(weights, axis=1) if len(weights) > 1 else weights[0]
-    high = weight.astype(jnp.bfloat16)
-    low = (weight - high.astype(jnp.float32)).astype(jnp.bfloat16)
-    over = (((1,), (0,)), ((), ()))
-    result = lax.dot_general(high, values, over, preferred_element_type=jnp.float32)
-    result += lax.dot_general(low, values, over, preferred_element_type=jnp.float32)
+    highs = [weight.astype(jnp.bfloat16) for weight in weights]
+    lows = [
+        (weight - high.astype(jnp.float32)).astype(jnp.bfloat16)
+        for weight, high in zip(weights, highs)
+    ]
+    halves = [jnp.concatenate(half, axis=1) if len(half) > 1 else half[0] for half in (highs, lows)]
+    result = lax.dot_general(
+        jnp.concatenate(halves, axis=0),
+        values,
+        (((1,), (0,)), ((), ())),
+        preferred_element_type=jnp.float32,
+    )
+    result = result[: rows.shape[0]] + result[rows.shape[0] :]
     if sums is None:
         return top, total, result
     largest, totals, summed = sums
@@ -120,27 +129,38 @@
     if len(groups) > 1:
         some = compact(both, lambda start: (start >= low) & (start < high))
 
+    @pl.when(some % STEP == STEP - 1)
+    def _():
+        target = pl.ds(pl.multiple_of(some * token, token), token)
+        keys_ref[target, :] = jnp.zeros((token, HD), keys_ref.dtype)
+        values_ref[target, :] = jnp.zeros((token, HD), values_ref.dtype)
+
     def attend_group(rows_ref, state, seen):
-        def update(first, number):
+        def update(first, number, last_counts=None):
             part = pl.ds(pl.multiple_of(first * token, token), number * token)
             sums = [held[...] for held in state]
-            new = combine(rows_ref[...], keys_ref[part, :], values_ref[part, :], sums, TO_LOG2)
+            new = combine(
+                rows_ref[...],
+                keys_ref[part, :],
+                values_ref[part, :],
+                sums,
+                TO_LOG2,
+                last_counts=last_counts,
+            )
             for held, value in zip(state, new):
                 held[...] = value
 
         def many(index, _):
-            update(index * STEP, STEP)
+            first = index * STEP
+            update(first, STEP, first + STEP <= seen)
             return 0
 
-        lax.fori_loop(0, seen // STEP, many, 0)
         left = seen % STEP
-        done = seen - left
-        number = STEP // 2
-        while number:
-            pl.when((left & number) != 0)(
-                functools.partial(update, done + (left & ~(2 * number - 1)), number)
-            )
-            number //= 2
+        full = (seen + 1) // STEP
+        lax.fori_loop(0, full, many, 0)
+        done = full * STEP
+        pl.when(left == 1)(functools.partial(update, done, 1))
+        pl.when(left == 2)(functools.partial(update, done, 2))
 
     for group, bound, rows_ref, state in zip(groups, bounds, rows_refs, states):
         if group in fresh:
@@ -216,6 +236,7 @@
     count = rows[0].shape[0]
     arrays, pieces = zip(*items)
     blocks = sum(array.shape[0] for array in arrays) // (2 * token)
+    room = -(-blocks // STEP) * STEP * token
     fresh = tuple(group for group in groups if states[group] is None)
     sums = [jax.ShapeDtypeStruct((count, HD), jnp.float32)] * 3
     outs = sums * len(groups)
@@ -234,7 +255,7 @@
         in_specs=[SMEM] + [VMEM] * (len(operands) - 1),
         out_specs=[VMEM] * len(outs),
         input_output_aliases=aliases,
-        scratch_shapes=[pltpu.VMEM((blocks * token, HD), jnp.bfloat16)] * 2,
+        scratch_shapes=[pltpu.VMEM((room, HD), jnp.bfloat16)] * 2,
         **params(count * len(groups), token, blocks),
     )(*operands)
     states = list(states)
@@ -309,8 +330,8 @@
         (lower, upper), (one, two) = held, plan[0]
         near, side, far = spread(lower, (one, two))
         near_up, side_up, far_up = spread(upper, (one, two))
-        early = [[lower], [near, side], [far, upper]]
-        late = [[near_up, side_up, far_up]]
+        early = [[lower], [near, side], [far, upper, near_up]]
+        late = [[side_up, far_up]]
     else:
         early = [held]
         for bits in plan:

time: 35.4 us -> 36.2 us (1.023)
  waiting for transfers between devices: 5.44 us -> 6.2 us
    ppermute x11, waiting for transfers between devices: 5.44 us -> 6.2 us  [move(): return lax.ppermute(array, AXES, pairs)]
  transfers between devices with their start and end apart: 11 -> 11, of which waited for: 3 -> 4; matrix products, arithmetic and copies ran while one was open for 0% -> 0% of each run, Pallas kernels for 31% -> 31%
where the time goes in v5:
time: 36.2 us; the launch traced here: 36.1 us
  Pallas kernels  15.4 us (43%)
  starting transfers between devices  14.2 us (39%)
  waiting for transfers between devices  6.2 us (17%)
    ppermute x11, starting transfers between devices, move(): return lax.ppermute(array, AXES, pairs)  14.2 us
    pallas_call x5, Pallas kernels, attend(): pl.pallas_call(kernel, out_shape=outs, in_specs=[SMEM] + [VMEM] * (len(op...  12.5 us
    ppermute x11, waiting for transfers between devices, move(): return lax.ppermute(array, AXES, pairs)  6.2 us
    pallas_call x1, Pallas kernels, finish(): pl.pallas_call(finish_kernel, out_shape=jax.ShapeDtypeStruct(shape, jnp.f...  1.43 us
    pallas_call x1, Pallas kernels, packed_blocks(): pl.pallas_call(pack_kernel, out_shape=jax.ShapeDtypeStruct((2 * token, wi...  0.79 us
  transfers between devices with their start and end apart: 11, of which 4 were waited for; matrix products, arithmetic and copies ran while one was open for 0% of the time, Pallas kernels for 31%

profile of v5, /device:TPU:0, one launch (start us, length us, event | category | flops | bytes accessed | tf_op | source)
XLA Modules:
  0.0 36.1 jit_solution(3964470710580562257)
XLA Ops:
  0.0 0.8 %shard_map.46.own_ref = bf16[256,128]{1,0:T(8,128)(2,1)S(1)} custom-call(bf16[128,128]{1,0:T(8,128)(2,1)} %keys_ref.1, bf16[128,128]{1,0:T(8,128)(2,1)} %values_ref.1), custom_call_target="tpu_custom_call" | custom-call | tf_op jit(solution)/shard_map/pallas_call | solution.py:210
  0.8 0.0 copy-start
  0.8 3.1 %collective-permute-start.6 = (bf16[256,128]{1,0:T(8,128)(2,1)S(1)}, bf16[256,128]{1,0:T(8,128)(2,1)S(1)}, u32[]{:S(2)}, u32[]{:S(2)}) collective-permute-start(bf16[256,128]{1,0:T(8,128)(2,1)S(1)} %shard_map.46.own_ref), channel_id=1, source_target_pairs={{1,0},{0,1},{3,2},{2,3},{5,4},{4,5},{7,6},{6,7},{9,8},{8,9},{11,10... | collective-permute-start | bytes 196616 | tf_op jit(solution)/shard_map/ppermute | solution.py:285
  3.9 2.6 %collective-permute-start.1 = (bf16[256,128]{1,0:T(8,128)(2,1)S(1)}, bf16[256,128]{1,0:T(8,128)(2,1)S(1)}, u32[]{:S(2)}, u32[]{:S(2)}) collective-permute-start(bf16[256,128]{1,0:T(8,128)(2,1)S(1)} %shard_map.46.own_ref), channel_id=1, source_target_pairs={{2,0},{3,1},{0,2},{1,3},{6,4},{7,5},{4,6},{5,7},{10,8},{11,9},{8,1... | collective-permute-start | bytes 196616 | tf_op jit(solution)/shard_map/ppermute | solution.py:285
  6.5 1.8 %collective-permute-start.7 = (bf16[512,128]{1,0:T(8,128)(2,1)S(1)}, bf16[512,128]{1,0:T(8,128)(2,1)S(1)}, u32[]{:S(2)}, u32[]{:S(2)}) collective-permute-start(bf16[512,128]{1,0:T(8,128)(2,1)S(1)} %pad_maximum_fusion.refs_3_), channel_id=1, source_target_pairs={{8,0},{9,1},{10,2},{11,3},{20,4},{21,5},{22,6},{23,7},{0,8},{1,9},... | collective-permute-start | bytes 393224 | tf_op jit(solution)/shard_map/ppermute | solution.py:285
  8.3 2.9 %collective-permute-done.1 = bf16[256,128]{1,0:T(8,128)(2,1)S(1)} collective-permute-done((bf16[256,128]{1,0:T(8,128)(2,1)S(1)}, bf16[256,128]{1,0:T(8,128)(2,1)S(1)}, u32[]{:S(2)}, u32[]{:S(2)}) %collective-permute-start.1) | collective-permute-done | bytes 65568 | tf_op jit(solution)/shard_map/ppermute | solution.py:285
  11.2 1.4 %collective-permute-done.2 = bf16[256,128]{1,0:T(8,128)(2,1)S(1)} collective-permute-done((bf16[256,128]{1,0:T(8,128)(2,1)S(1)}, bf16[256,128]{1,0:T(8,128)(2,1)S(1)}, u32[]{:S(2)}, u32[]{:S(2)}) %collective-permute-start.2) | collective-permute-done | bytes 65568 | tf_op jit(solution)/shard_map/ppermute | solution.py:285
  12.6 1.6 %collective-permute-start.4 = (bf16[512,128]{1,0:T(8,128)(2,1)S(1)}, bf16[512,128]{1,0:T(8,128)(2,1)S(1)}, u32[]{:S(2)}, u32[]{:S(2)}) collective-permute-start(bf16[512,128]{1,0:T(8,128)(2,1)S(1)} %constant_dynamic-update-slice_fusion.refs_4_), channel_id=1, source_target_pairs={{8,0},{9,1},{10,2},{11,3},{20,4},{21,5},{22,6},{23,7},{0,8},{1,9},... | collective-permute-start | bytes 393224 | tf_op jit(solution)/shard_map/ppermute | solution.py:285
  14.2 1.5 %collective-permute-start.9 = (bf16[512,128]{1,0:T(8,128)(2,1)S(1)}, bf16[512,128]{1,0:T(8,128)(2,1)S(1)}, u32[]{:S(2)}, u32[]{:S(2)}) collective-permute-start(bf16[512,128]{1,0:T(8,128)(2,1)S(1)} %pad_maximum_fusion.refs_3_), channel_id=1, source_target_pairs={{16,0},{17,1},{18,2},{19,3},{12,4},{13,5},{14,6},{15,7},{24,8},{25... | collective-permute-start | bytes 393224 | tf_op jit(solution)/shard_map/ppermute | solution.py:285
  15.7 0.0 collective-permute-done.7.refs_3_
  15.7 0.5 %collective-permute-start.8 = (bf16[512,128]{1,0:T(8,128)(2,1)S(1)}, bf16[512,128]{1,0:T(8,128)(2,1)S(1)}, u32[]{:S(2)}, u32[]{:S(2)}) collective-permute-start(bf16[512,128]{1,0:T(8,128)(2,1)S(1)} %collective-permute-done.7.refs_3_), channel_id=1, source_target_pairs={{16,0},{17,1},{18,2},{19,3},{12,4},{13,5},{14,6},{15,7},{24,8},{25... | collective-permute-start | bytes 393224 | tf_op jit(solution)/shard_map/ppermute | solution.py:285
  16.2 0.1 slice_reduce_fusion.refs_0_
  16.3 1.6 %collective-permute-start.3 = (bf16[512,128]{1,0:T(8,128)(2,1)S(1)}, bf16[512,128]{1,0:T(8,128)(2,1)S(1)}, u32[]{:S(2)}, u32[]{:S(2)}) collective-permute-start(bf16[512,128]{1,0:T(8,128)(2,1)S(1)} %constant_dynamic-update-slice_fusion.refs_4_), channel_id=1, source_target_pairs={{16,0},{17,1},{18,2},{19,3},{12,4},{13,5},{14,6},{15,7},{24,8},{25... | collective-permute-start | bytes 393224 | tf_op jit(solution)/shard_map/ppermute | solution.py:285
  17.9 1.2 %collective-permute-done.4.refs_5_ = bf16[512,128]{1,0:T(8,128)(2,1)S(1)} collective-permute-done((bf16[512,128]{1,0:T(8,128)(2,1)S(1)}, bf16[512,128]{1,0:T(8,128)(2,1)S(1)}, u32[]{:S(2)}, u32[]{:S(2)}) %collective-permute-start.4) | collective-permute-done | bytes 131104 | tf_op jit(solution)/shard_map/ppermute | solution.py:285
  19.0 1.5 %collective-permute-start.5 = (bf16[512,128]{1,0:T(8,128)(2,1)S(1)}, bf16[512,128]{1,0:T(8,128)(2,1)S(1)}, u32[]{:S(2)}, u32[]{:S(2)}) collective-permute-start(bf16[512,128]{1,0:T(8,128)(2,1)S(1)} %collective-permute-done.4.refs_5_), channel_id=1, source_target_pairs={{16,0},{17,1},{18,2},{19,3},{12,4},{13,5},{14,6},{15,7},{24,8},{25... | collective-permute-start | bytes 393224 | tf_op jit(solution)/shard_map/ppermute | solution.py:285
  20.6 0.7 %shard_map.47 = (bf16[1024,128]{1,0:T(8,128)(2,1)S(1)}, bf16[1024,128]{1,0:T(8,128)(2,1)S(1)}, f32[1024,128]{1,0:T(8,128)S(1)}, f32[1024,128]{1,0:T(8,128)S(1)}, f32[1024,128]{1,0:T(8,128)S(1)}) custom-call(bf16[128,1024]{1,0:T(8,128)(2,1)S(1)} %copy-done, bf16[128,1024]{1,0:T(8,128)(2,1)S(1)} %collective-permute-done.other_ref, ...), custom_call_target="tpu_custom_call" | custom-call | flops 100663296 | bytes 1048576 | tf_op jit(solution)/shard_map/pallas_call | solution.py:225
  21.2 1.4 %shard_map.48 = (f32[1024,128]{1,0:T(8,128)S(1)}, f32[1024,128]{1,0:T(8,128)S(1)}, f32[1024,128]{1,0:T(8,128)S(1)}, f32[1024,128]{1,0:T(8,128)S(1)}, f32[1024,128]{1,0:T(8,128)S(1)}, /*index=5*/f32[1024,128]{1,0:T(8,128)S(1)}) custom-call(s32[32]{0:T(128)S(1)} %slice_reduce_fusion.refs_0_, ...), custom_call_target="tpu_custom_call", output_to_operand_aliasing={{0}: (4, {}), {1}: (5, {}), {2}: (6, {})} | custom-call | flops 402653184 | bytes 1048576 | tf_op jit(solution)/shard_map/pallas_call | solution.py:252
  22.7 3.1 %shard_map.49 = (f32[1024,128]{1,0:T(8,128)S(1)}, f32[1024,128]{1,0:T(8,128)S(1)}, f32[1024,128]{1,0:T(8,128)S(1)}, f32[1024,128]{1,0:T(8,128)S(1)}, f32[1024,128]{1,0:T(8,128)S(1)}, /*index=5*/f32[1024,128]{1,0:T(8,128)S(1)}) custom-call(s32[32]{0:T(128)S(1)} %slice_reduce_fusion.refs_0_, ...), custom_call_target="tpu_custom_call", output_to_operand_aliasing={{0}: (5, {}), {1}: (6, {}), {2}: (7, {}), {3}: (8, {}), {4}... | custom-call | flops 805306368 | bytes 1048576 | tf_op jit(solution)/shard_map/pallas_call | solution.py:252
  25.8 4.2 %shard_map.50 = (f32[1024,128]{1,0:T(8,128)S(1)}, f32[1024,128]{1,0:T(8,128)S(1)}, f32[1024,128]{1,0:T(8,128)S(1)}, f32[1024,128]{1,0:T(8,128)S(1)}, f32[1024,128]{1,0:T(8,128)S(1)}, /*index=5*/f32[1024,128]{1,0:T(8,128)S(1)}) custom-call(s32[32]{0:T(128)S(1)} %slice_reduce_fusion.refs_0_, ...), custom_call_target="tpu_custom_call", output_to_operand_aliasing={{0}: (6, {}), {1}: (7, {}), {2}: (8, {}), {3}: (9, {}), {4}... | custom-call | flops 1207959552 | bytes 1048576 | tf_op jit(solution)/shard_map/pallas_call | solution.py:252
  30.1 1.8 %shard_map.52 = (f32[1024,128]{1,0:T(8,128)S(1)}, f32[1024,128]{1,0:T(8,128)S(1)}, f32[1024,128]{1,0:T(8,128)S(1)}, f32[2048,128]{1,0:T(8,128)S(1)}) custom-call(s32[32]{0:T(128)S(1)} %slice_reduce_fusion.refs_0_, bf16[1024,128]{1,0:T(8,128)(2,1)S(1)} %get-tuple-element.33.refs_2_.refs_1_, ...), custom_call_target="tpu_custom_call", output_to_operand_aliasing={{0}: (4, {}), {1}: (5, {}), {2}: (6, {})} | custom-call | flops 402653184 | bytes 1048576 | tf_op jit(solution)/shard_map/pallas_call | solution.py:252
  31.9 0.1 collective-permute-start.10
  32.0 1.9 %shard_map.51 = (f32[1024,128]{1,0:T(8,128)S(1)}, f32[1024,128]{1,0:T(8,128)S(1)}, f32[1024,128]{1,0:T(8,128)S(1)}) custom-call(s32[32]{0:T(128)S(1)} %slice_reduce_fusion.refs_0_, bf16[1024,128]{1,0:T(8,128)(2,1)S(1)} %get-tuple-element.32.refs_1_, ...), custom_call_target="tpu_custom_call", output_to_operand_aliasing={{0}: (4, {}), {1}: (5, {}), {2}: (6, {})} | custom-call | flops 402653184 | bytes 1048576 | tf_op jit(solution)/shard_map/pallas_call | solution.py:252
  33.9 0.8 %collective-permute-done.10.packed_ref = f32[2048,128]{1,0:T(8,128)S(1)} collective-permute-done((f32[2048,128]{1,0:T(8,128)S(1)}, f32[2048,128]{1,0:T(8,128)S(1)}, u32[]{:S(2)}, u32[]{:S(2)}) %collective-permute-start.10) | collective-permute-done | bytes 1048608 | tf_op jit(solution)/shard_map/ppermute | solution.py:285
  34.6 1.4 %shard_map.53 = f32[128,1024]{1,0:T(8,128)} custom-call(f32[1024,128]{1,0:T(8,128)S(1)} %get-tuple-element.52.largest_ref, f32[1024,128]{1,0:T(8,128)S(1)} %get-tuple-element.53.totals_ref, f32[1024,128]{1,0:T(8,128)S(1)} %get-tuple-element.54.summed_ref, f32[2048,128]{1,0:T(8,128)S(1)} %collective-permute-done.10.packed_ref), custom_call_target="tpu_custom_call" | custom-call | flops 100663296 | bytes 1048576 | tf_op jit(solution)/shard_map/pallas_call | solution.py:269
  (14 shorter events, 0.1 us)
Async XLA Ops:
  0.8 19.8 %copy-start = (bf16[128,1024]{1,0:T(8,128)(2,1)S(1)}, bf16[128,1024]{1,0:T(8,128)(2,1)}, u32[]{:S(2)}) copy-start(bf16[128,1024]{1,0:T(8,128)(2,1)} %queries_ref.1) | copy-start | bytes 786436
  0.8 5.7 %collective-permute-start.6 = (bf16[256,128]{1,0:T(8,128)(2,1)S(1)}, bf16[256,128]{1,0:T(8,128)(2,1)S(1)}, u32[]{:S(2)}, u32[]{:S(2)}) collective-permute-start(bf16[256,128]{1,0:T(8,128)(2,1)S(1)} %shard_map.46.own_ref), channel_id=1, source_target_pairs={{1,0},{0,1},{3,2},{2,3},{5,4},{4,5},{7,6},{6,7},{9,8},{8,9},{11,10... | collective-permute-start | bytes 196616 | tf_op jit(solution)/shard_map/ppermute | solution.py:285
  3.9 7.3 %collective-permute-start.1 = (bf16[256,128]{1,0:T(8,128)(2,1)S(1)}, bf16[256,128]{1,0:T(8,128)(2,1)S(1)}, u32[]{:S(2)}, u32[]{:S(2)}) collective-permute-start(bf16[256,128]{1,0:T(8,128)(2,1)S(1)} %shard_map.46.own_ref), channel_id=1, source_target_pairs={{2,0},{3,1},{0,2},{1,3},{6,4},{7,5},{4,6},{5,7},{10,8},{11,9},{8,1... | collective-permute-start | bytes 196616 | tf_op jit(solution)/shard_map/ppermute | solution.py:285
  6.5 6.1 %collective-permute-start.2 = (bf16[256,128]{1,0:T(8,128)(2,1)S(1)}, bf16[256,128]{1,0:T(8,128)(2,1)S(1)}, u32[]{:S(2)}, u32[]{:S(2)}) collective-permute-start(bf16[256,128]{1,0:T(8,128)(2,1)S(1)} %shard_map.46.own_ref), channel_id=1, source_target_pairs={{3,0},{2,1},{1,2},{0,3},{7,4},{6,5},{5,6},{4,7},{11,8},{10,9},{9,1... | collective-permute-start | bytes 196616 | tf_op jit(solution)/shard_map/ppermute | solution.py:285
  6.5 14.0 %collective-permute-start = (bf16[128,1024]{1,0:T(8,128)(2,1)}, bf16[128,1024]{1,0:T(8,128)(2,1)S(1)}, u32[]{:S(2)}, u32[]{:S(2)}) collective-permute-start(bf16[128,1024]{1,0:T(8,128)(2,1)} %queries_ref.1), channel_id=1, source_target_pairs={{4,0},{5,1},{6,2},{7,3},{0,4},{1,5},{2,6},{3,7},{12,8},{13,9},{14,... | collective-permute-start | bytes 786440 | tf_op jit(solution)/shard_map/ppermute | solution.py:285
  6.5 9.1 %collective-permute-start.7 = (bf16[512,128]{1,0:T(8,128)(2,1)S(1)}, bf16[512,128]{1,0:T(8,128)(2,1)S(1)}, u32[]{:S(2)}, u32[]{:S(2)}) collective-permute-start(bf16[512,128]{1,0:T(8,128)(2,1)S(1)} %pad_maximum_fusion.refs_3_), channel_id=1, source_target_pairs={{8,0},{9,1},{10,2},{11,3},{20,4},{21,5},{22,6},{23,7},{0,8},{1,9},... | collective-permute-start | bytes 393224 | tf_op jit(solution)/shard_map/ppermute | solution.py:285
  11.2 5.0 %copy-start.1 = (s32[4096]{0:T(1024)S(1)}, s32[4096]{0:T(1024)}, u32[]{:S(2)}) copy-start(s32[4096]{0:T(1024)} %param.7) | copy-start | bytes 49156
  12.6 6.4 %collective-permute-start.4 = (bf16[512,128]{1,0:T(8,128)(2,1)S(1)}, bf16[512,128]{1,0:T(8,128)(2,1)S(1)}, u32[]{:S(2)}, u32[]{:S(2)}) collective-permute-start(bf16[512,128]{1,0:T(8,128)(2,1)S(1)} %constant_dynamic-update-slice_fusion.refs_4_), channel_id=1, source_target_pairs={{8,0},{9,1},{10,2},{11,3},{20,4},{21,5},{22,6},{23,7},{0,8},{1,9},... | collective-permute-start | bytes 393224 | tf_op jit(solution)/shard_map/ppermute | solution.py:285
  14.2 8.5 %collective-permute-start.9 = (bf16[512,128]{1,0:T(8,128)(2,1)S(1)}, bf16[512,128]{1,0:T(8,128)(2,1)S(1)}, u32[]{:S(2)}, u32[]{:S(2)}) collective-permute-start(bf16[512,128]{1,0:T(8,128)(2,1)S(1)} %pad_maximum_fusion.refs_3_), channel_id=1, source_target_pairs={{16,0},{17,1},{18,2},{19,3},{12,4},{13,5},{14,6},{15,7},{24,8},{25... | collective-permute-start | bytes 393224 | tf_op jit(solution)/shard_map/ppermute | solution.py:285
  15.7 10.1 %collective-permute-start.8 = (bf16[512,128]{1,0:T(8,128)(2,1)S(1)}, bf16[512,128]{1,0:T(8,128)(2,1)S(1)}, u32[]{:S(2)}, u32[]{:S(2)}) collective-permute-start(bf16[512,128]{1,0:T(8,128)(2,1)S(1)} %collective-permute-done.7.refs_3_), channel_id=1, source_target_pairs={{16,0},{17,1},{18,2},{19,3},{12,4},{13,5},{14,6},{15,7},{24,8},{25... | collective-permute-start | bytes 393224 | tf_op jit(solution)/shard_map/ppermute | solution.py:285
  16.3 13.7 %collective-permute-start.3 = (bf16[512,128]{1,0:T(8,128)(2,1)S(1)}, bf16[512,128]{1,0:T(8,128)(2,1)S(1)}, u32[]{:S(2)}, u32[]{:S(2)}) collective-permute-start(bf16[512,128]{1,0:T(8,128)(2,1)S(1)} %constant_dynamic-update-slice_fusion.refs_4_), channel_id=1, source_target_pairs={{16,0},{17,1},{18,2},{19,3},{12,4},{13,5},{14,6},{15,7},{24,8},{25... | collective-permute-start | bytes 393224 | tf_op jit(solution)/shard_map/ppermute | solution.py:285
  19.0 11.0 %collective-permute-start.5 = (bf16[512,128]{1,0:T(8,128)(2,1)S(1)}, bf16[512,128]{1,0:T(8,128)(2,1)S(1)}, u32[]{:S(2)}, u32[]{:S(2)}) collective-permute-start(bf16[512,128]{1,0:T(8,128)(2,1)S(1)} %collective-permute-done.4.refs_5_), channel_id=1, source_target_pairs={{16,0},{17,1},{18,2},{19,3},{12,4},{13,5},{14,6},{15,7},{24,8},{25... | collective-permute-start | bytes 393224 | tf_op jit(solution)/shard_map/ppermute | solution.py:285
  31.9 2.7 %collective-permute-start.10 = (f32[2048,128]{1,0:T(8,128)S(1)}, f32[2048,128]{1,0:T(8,128)S(1)}, u32[]{:S(2)}, u32[]{:S(2)}) collective-permute-start(f32[2048,128]{1,0:T(8,128)S(1)} %get-tuple-element.58), channel_id=1, source_target_pairs={{4,0},{5,1},{6,2},{7,3},{0,4},{1,5},{2,6},{3,7},{12,8},{13,9},{14,... | collective-permute-start | bytes 3145736 | tf_op jit(solution)/shard_map/ppermute | solution.py:285

commit v6 on v5

--- a/solution.py
+++ b/solution.py
@@ -43,13 +43,16 @@
         for weight, high in zip(weights, highs)
     ]
     halves = [jnp.concatenate(half, axis=1) if len(half) > 1 else half[0] for half in (highs, lows)]
-    result = lax.dot_general(
-        jnp.concatenate(halves, axis=0),
-        values,
-        (((1,), (0,)), ((), ())),
-        preferred_element_type=jnp.float32,
-    )
-    result = result[: rows.shape[0]] + result[rows.shape[0] :]
+    over = (((1,), (0,)), ((), ()))
+    if len(parts) < STEP:
+        result = sum(
+            lax.dot_general(half, values, over, preferred_element_type=jnp.float32)
+            for half in halves
+        )
+    else:
+        both = jnp.concatenate(halves, axis=0)
+        result = lax.dot_general(both, values, over, preferred_element_type=jnp.float32)
+        result = result[: rows.shape[0]] + result[rows.shape[0] :]
     if sums is None:
         return top, total, result
     largest, totals, summed = sums
@@ -103,16 +106,15 @@
 
     own_pb, own_ka = lax.axis_index("pb"), lax.axis_index("ka")
     core = own_pb % 2
-    bounds = [starts_ref[(own_pb ^ group) * size_key + own_ka] for group in groups]
-    low = functools.reduce(jnp.minimum, bounds)
-    high = functools.reduce(jnp.maximum, bounds)
-
-    def compact(seen, inside):
-        for ref, parts in zip(block_refs, pieces):
-            for offset, number, base, mask_even, mask_odd in parts:
+
+    def compact(bound, places):
+        seen = jnp.int32(0)
+        for place in places:
+            ref = block_refs[place]
+            for offset, number, base, mask_even, mask_odd in pieces[place]:
                 source = (own_pb ^ jnp.where(core == 0, mask_even, mask_odd)) * size_key
                 for at in range(number):
-                    visible = inside(starts_ref[source + (own_ka ^ (base + at))])
+                    visible = starts_ref[source + (own_ka ^ (base + at))] < bound
                     row = (offset + at) * 2 * token
 
                     @pl.when(visible)
@@ -122,18 +124,14 @@
                         values_ref[target, :] = ref[row + token : row + 2 * token, :]
 
                     seen = seen + visible.astype(jnp.int32)
+
+        @pl.when(seen % STEP == STEP - 1)
+        def _():
+            target = pl.ds(pl.multiple_of(seen * token, token), token)
+            keys_ref[target, :] = jnp.zeros((token, HD), keys_ref.dtype)
+            values_ref[target, :] = jnp.zeros((token, HD), values_ref.dtype)
+
         return seen
-
-    both = compact(jnp.int32(0), lambda start: start < low)
-    some = both
-    if len(groups) > 1:
-        some = compact(both, lambda start: (start >= low) & (start < high))
-
-    @pl.when(some % STEP == STEP - 1)
-    def _():
-        target = pl.ds(pl.multiple_of(some * token, token), token)
-        keys_ref[target, :] = jnp.zeros((token, HD), keys_ref.dtype)
-        values_ref[target, :] = jnp.zeros((token, HD), values_ref.dtype)
 
     def attend_group(rows_ref, state, seen):
         def update(first, number, last_counts=None):
@@ -162,12 +160,13 @@
         pl.when(left == 1)(functools.partial(update, done, 1))
         pl.when(left == 2)(functools.partial(update, done, 2))
 
-    for group, bound, rows_ref, state in zip(groups, bounds, rows_refs, states):
+    for (group, places), rows_ref, state in zip(groups, rows_refs, states):
         if group in fresh:
             state[0][...] = jnp.full_like(state[0], BIG)
             state[1][...] = jnp.zeros_like(state[1])
             state[2][...] = jnp.zeros_like(state[2])
-        attend_group(rows_ref, state, jnp.where(bound == high, some, both))
+        bound = starts_ref[(own_pb ^ group) * size_key + own_ka]
+        attend_group(rows_ref, state, compact(bound, places))
 
     if pack:
         largest_ref, totals_ref, summed_ref = states[0]
@@ -232,23 +231,30 @@
     return tuple(result[:2]), tuple(result[2:])
 
 
-def attend(starts, rows, states, items, groups, size_key, token, pack=False):
+def attend(starts, rows, states, wanted, size_key, token, pack=False):
     count = rows[0].shape[0]
+    items = []
+    for _, mine in wanted:
+        items += [item for item in mine if not any(item is other for other in items)]
+    places = [
+        (group, tuple(at for item in mine for at, other in enumerate(items) if other is item))
+        for group, mine in wanted
+    ]
     arrays, pieces = zip(*items)
     blocks = sum(array.shape[0] for array in arrays) // (2 * token)
     room = -(-blocks // STEP) * STEP * token
-    fresh = tuple(group for group in groups if states[group] is None)
+    fresh = tuple(group for group, _ in wanted if states[group] is None)
     sums = [jax.ShapeDtypeStruct((count, HD), jnp.float32)] * 3
-    outs = sums * len(groups)
+    outs = sums * len(wanted)
     if pack:
         outs.append(jax.ShapeDtypeStruct((2 * count, HD), jnp.float32))
-    operands = [starts, *(rows[group] for group in groups), *arrays]
+    operands = [starts, *(rows[group] for group, _ in wanted), *arrays]
     aliases = {}
-    for at, group in enumerate(groups):
+    for at, (group, _) in enumerate(wanted):
         if group not in fresh:
             aliases.update({len(operands) + index: 3 * at + index for index in range(3)})
             operands += states[group]
-    kernel = functools.partial(attend_kernel, pieces, groups, fresh, pack, size_key, token)
+    kernel = functools.partial(attend_kernel, pieces, places, fresh, pack, size_key, token)
     result = pl.pallas_call(
         kernel,
         out_shape=outs,
@@ -256,10 +262,10 @@
         out_specs=[VMEM] * len(outs),
         input_output_aliases=aliases,
         scratch_shapes=[pltpu.VMEM((room, HD), jnp.bfloat16)] * 2,
-        **params(count * len(groups), token, blocks),
+        **params(count * len(wanted), token, blocks),
     )(*operands)
     states = list(states)
-    for at, group in enumerate(groups):
+    for at, (group, _) in enumerate(wanted):
         states[group] = tuple(result[3 * at : 3 * at + 3])
     return states, result[-1]
 
@@ -293,6 +299,14 @@
 def paired(size_query, size_key):
     plan = stages(size_query)
     return len(plan) == 1 and len(plan[0]) == 2 and size_key > 1
+
+
+def spread_near(item, bits):
+    array, parts = item
+    one, two = bits
+    near = (move(array, one, two, 0), shifted(parts, one, two))
+    side = (move(array, two, one, 0), shifted(parts, two, one))
+    return near, side
 
 
 def spread(item, bits):
@@ -328,28 +342,29 @@
     plan = stages(size_query)
     if paired(size_query, size_key):
         (lower, upper), (one, two) = held, plan[0]
-        near, side, far = spread(lower, (one, two))
-        near_up, side_up, far_up = spread(upper, (one, two))
-        early = [[lower], [near, side], [far, upper, near_up]]
-        late = [[side_up, far_up]]
+        near, side = spread_near(lower, (one, two))
+        both = one ^ two
+        far = (move(lower[0], both, both, 0), shifted(lower[1], both, both))
+        near_up, side_up = spread_near(upper, (one, two))
+        far_up = (move(upper[0], both, both, 0), shifted(upper[1], both, both))
+        steps = [[(0, [lower]), (1, [lower])], [(0, [near, side, far, upper]), (1, [near, side, far, upper])], [(1, [near_up, side_up, far_up])]]
+        rest = [near_up, side_up, far_up]
     else:
-        early = [held]
+        shared = [held]
         for bits in plan:
             more = [item for piece in held for item in spread(piece, bits) if item is not None]
-            early.append(more)
+            shared.append(more)
             held = held + more
-        early, late = early[:-1], early[-1:]
+        rest = shared.pop()
+        steps = [[(0, group), (1, group)] for group in shared] + [[(1, rest)]]
 
     states = [sums, None]
     attend_to = functools.partial(attend, size_key=size_key, token=token)
-    number = 0
-    steps = [(group, (0, 1)) for group in early] + [(group, (1,)) for group in late]
-    for number, (group, who) in enumerate(steps):
+    for number, wanted in enumerate(steps):
         pack = number == len(steps) - 1
-        states, packed = attend_to(starts, rows, states, group, who, pack=pack)
+        states, packed = attend_to(starts, rows, states, wanted, pack=pack)
     packed = move(packed, 1, 1, 0)
-    rest = [item for group in late for item in group]
-    states, _ = attend_to(starts, rows, states, rest, (0,))
+    states, _ = attend_to(starts, rows, states, [(0, rest)])
     return finish(states[0], packed, queries.shape)
 
 

time: 36.2 us -> 31.5 us (0.87)
  the two profiles are of different devices: /device:TPU:0 before, /device:TPU:9 now
where the time goes in v6:
time: 31.5 us; the launch traced here: 31.3 us
  Pallas kernels  16.5 us (52%)
  starting transfers between devices  14.1 us (45%)
  waiting for transfers between devices  0.51 us (2%)
    ppermute x11, starting transfers between devices, move(): return lax.ppermute(array, AXES, pairs)  14.1 us
    pallas_call x4, Pallas kernels, attend(): pl.pallas_call(kernel, out_shape=outs, in_specs=[SMEM] + [VMEM] * (len(op...  13.5 us
    pallas_call x1, Pallas kernels, finish(): pl.pallas_call(finish_kernel, out_shape=jax.ShapeDtypeStruct(shape, jnp.f...  1.44 us
    pallas_call x1, Pallas kernels, packed_blocks(): pl.pallas_call(pack_kernel, out_shape=jax.ShapeDtypeStruct((2 * token, wi...  0.8 us
    pallas_call x1, Pallas kernels, attend_own(): pl.pallas_call(own_kernel, out_shape=[rows, rows, sums, sums, sums], in_s...  0.67 us
  transfers between devices with their start and end apart: 11, of which 1 were waited for; matrix products, arithmetic and copies ran while one was open for 0% of the time, Pallas kernels for 36%

profile of v6, /device:TPU:9, one launch (start us, length us, event | category | flops | bytes accessed | tf_op | source)
XLA Modules:
  0.0 31.3 jit_solution(17237398492819509942)
XLA Ops:
  0.0 0.8 %shard_map.46.own_ref = bf16[256,128]{1,0:T(8,128)(2,1)S(1)} custom-call(bf16[128,128]{1,0:T(8,128)(2,1)} %keys_ref.1, bf16[128,128]{1,0:T(8,128)(2,1)} %values_ref.1), custom_call_target="tpu_custom_call" | custom-call | tf_op jit(solution)/shard_map/pallas_call | solution.py:209
  0.8 0.1 collective-permute-start.6
  0.9 2.5 %collective-permute-start.1 = (bf16[256,128]{1,0:T(8,128)(2,1)S(1)}, bf16[256,128]{1,0:T(8,128)(2,1)S(1)}, u32[]{:S(2)}, u32[]{:S(2)}) collective-permute-start(bf16[256,128]{1,0:T(8,128)(2,1)S(1)} %shard_map.46.own_ref), channel_id=1, source_target_pairs={{2,0},{3,1},{0,2},{1,3},{6,4},{7,5},{4,6},{5,7},{10,8},{11,9},{8,1... | collective-permute-start | bytes 196616 | tf_op jit(solution)/shard_map/ppermute | solution.py:291
  3.4 0.2 collective-permute-start.2
  3.5 1.5 %collective-permute-start = (bf16[128,1024]{1,0:T(8,128)(2,1)}, bf16[128,1024]{1,0:T(8,128)(2,1)S(1)}, u32[]{:S(2)}, u32[]{:S(2)}) collective-permute-start(bf16[128,1024]{1,0:T(8,128)(2,1)} %queries_ref.1), channel_id=1, source_target_pairs={{4,0},{5,1},{6,2},{7,3},{0,4},{1,5},{2,6},{3,7},{12,8},{13,9},{14,... | collective-permute-start | bytes 786440 | tf_op jit(solution)/shard_map/ppermute | solution.py:291
  5.0 0.1 slice_reduce_fusion.refs_0_
  5.2 0.0 collective-permute-done.6
  5.2 1.3 %collective-permute-start.7 = (bf16[512,128]{1,0:T(8,128)(2,1)S(1)}, bf16[512,128]{1,0:T(8,128)(2,1)S(1)}, u32[]{:S(2)}, u32[]{:S(2)}) collective-permute-start(bf16[512,128]{1,0:T(8,128)(2,1)S(1)} %pad_maximum_fusion.refs_3_), channel_id=1, source_target_pairs={{8,0},{9,1},{10,2},{11,3},{20,4},{21,5},{22,6},{23,7},{0,8},{1,9},... | collective-permute-start | bytes 393224 | tf_op jit(solution)/shard_map/ppermute | solution.py:291
  6.5 1.2 %collective-permute-start.8 = (bf16[512,128]{1,0:T(8,128)(2,1)S(1)}, bf16[512,128]{1,0:T(8,128)(2,1)S(1)}, u32[]{:S(2)}, u32[]{:S(2)}) collective-permute-start(bf16[512,128]{1,0:T(8,128)(2,1)S(1)} %pad_maximum_fusion.refs_3_), channel_id=1, source_target_pairs={{16,0},{17,1},{18,2},{19,3},{12,4},{13,5},{14,6},{15,7},{24,8},{25... | collective-permute-start | bytes 393224 | tf_op jit(solution)/shard_map/ppermute | solution.py:291
  7.7 0.4 %collective-permute-start.9 = (bf16[512,128]{1,0:T(8,128)(2,1)S(1)}, bf16[512,128]{1,0:T(8,128)(2,1)S(1)}, u32[]{:S(2)}, u32[]{:S(2)}) collective-permute-start(bf16[512,128]{1,0:T(8,128)(2,1)S(1)} %pad_maximum_fusion.refs_3_), channel_id=1, source_target_pairs={{24,0},{25,1},{26,2},{27,3},{28,4},{29,5},{30,6},{31,7},{16,8},{17... | collective-permute-start | bytes 393224 | tf_op jit(solution)/shard_map/ppermute | solution.py:291
  8.1 0.5 %collective-permute-done.2 = bf16[256,128]{1,0:T(8,128)(2,1)S(1)} collective-permute-done((bf16[256,128]{1,0:T(8,128)(2,1)S(1)}, bf16[256,128]{1,0:T(8,128)(2,1)S(1)}, u32[]{:S(2)}, u32[]{:S(2)}) %collective-permute-start.2) | collective-permute-done | bytes 65568 | tf_op jit(solution)/shard_map/ppermute | solution.py:291
  8.6 1.3 %collective-permute-start.3 = (bf16[512,128]{1,0:T(8,128)(2,1)S(1)}, bf16[512,128]{1,0:T(8,128)(2,1)S(1)}, u32[]{:S(2)}, u32[]{:S(2)}) collective-permute-start(bf16[512,128]{1,0:T(8,128)(2,1)S(1)} %constant_dynamic-update-slice_fusion.refs_6_), channel_id=1, source_target_pairs={{8,0},{9,1},{10,2},{11,3},{20,4},{21,5},{22,6},{23,7},{0,8},{1,9},... | collective-permute-start | bytes 393224 | tf_op jit(solution)/shard_map/ppermute | solution.py:291
  10.0 1.2 %collective-permute-start.4 = (bf16[512,128]{1,0:T(8,128)(2,1)S(1)}, bf16[512,128]{1,0:T(8,128)(2,1)S(1)}, u32[]{:S(2)}, u32[]{:S(2)}) collective-permute-start(bf16[512,128]{1,0:T(8,128)(2,1)S(1)} %constant_dynamic-update-slice_fusion.refs_6_), channel_id=1, source_target_pairs={{16,0},{17,1},{18,2},{19,3},{12,4},{13,5},{14,6},{15,7},{24,8},{25... | collective-permute-start | bytes 393224 | tf_op jit(solution)/shard_map/ppermute | solution.py:291
  11.2 0.7 %shard_map.47 = (bf16[1024,128]{1,0:T(8,128)(2,1)S(1)}, bf16[1024,128]{1,0:T(8,128)(2,1)S(1)}, f32[1024,128]{1,0:T(8,128)S(1)}, f32[1024,128]{1,0:T(8,128)S(1)}, f32[1024,128]{1,0:T(8,128)S(1)}) custom-call(bf16[128,1024]{1,0:T(8,128)(2,1)S(1)} %copy-done, bf16[128,1024]{1,0:T(8,128)(2,1)S(1)} %collective-permute-done.other_ref, ...), custom_call_target="tpu_custom_call" | custom-call | flops 100663296 | bytes 1048576 | tf_op jit(solution)/shard_map/pallas_call | solution.py:224
  11.8 2.1 %shard_map.48 = (f32[1024,128]{1,0:T(8,128)S(1)}, f32[1024,128]{1,0:T(8,128)S(1)}, f32[1024,128]{1,0:T(8,128)S(1)}, f32[1024,128]{1,0:T(8,128)S(1)}, f32[1024,128]{1,0:T(8,128)S(1)}, /*index=5*/f32[1024,128]{1,0:T(8,128)S(1)}) custom-call(s32[32]{0:T(128)S(1)} %slice_reduce_fusion.refs_0_, ...), custom_call_target="tpu_custom_call", output_to_operand_aliasing={{0}: (4, {}), {1}: (5, {}), {2}: (6, {})} | custom-call | flops 402653184 | bytes 1048576 | tf_op jit(solution)/shard_map/pallas_call | solution.py:258
  14.0 0.0 collective-permute-done.7.refs_3_
  14.0 0.3 collective-permute-start.5
  14.2 0.0 collective-permute-done.8.refs_4_
  14.3 5.7 %shard_map.49 = (f32[1024,128]{1,0:T(8,128)S(1)}, f32[1024,128]{1,0:T(8,128)S(1)}, f32[1024,128]{1,0:T(8,128)S(1)}, f32[1024,128]{1,0:T(8,128)S(1)}, f32[1024,128]{1,0:T(8,128)S(1)}, /*index=5*/f32[1024,128]{1,0:T(8,128)S(1)}) custom-call(s32[32]{0:T(128)S(1)} %slice_reduce_fusion.refs_0_, ...), custom_call_target="tpu_custom_call", output_to_operand_aliasing={{0}: (7, {}), {1}: (8, {}), {2}: (9, {}), {3}: (10, {}), {4... | custom-call | flops 1610612736 | bytes 1048576 | tf_op jit(solution)/shard_map/pallas_call | solution.py:258
  20.0 0.0 collective-permute-done.5.refs_4_
  20.0 3.0 %shard_map.51 = (f32[1024,128]{1,0:T(8,128)S(1)}, f32[1024,128]{1,0:T(8,128)S(1)}, f32[1024,128]{1,0:T(8,128)S(1)}, f32[2048,128]{1,0:T(8,128)S(1)}) custom-call(s32[32]{0:T(128)S(1)} %slice_reduce_fusion.refs_0_, bf16[1024,128]{1,0:T(8,128)(2,1)S(1)} %get-tuple-element.27.refs_2_.refs_1_, ...), custom_call_target="tpu_custom_call", output_to_operand_aliasing={{0}: (5, {}), {1}: (6, {}), {2}: (7, {})} | custom-call | flops 603979776 | bytes 1048576 | tf_op jit(solution)/shard_map/pallas_call | solution.py:258
  23.0 4.2 %collective-permute-start.10 = (f32[2048,128]{1,0:T(8,128)S(1)}, f32[2048,128]{1,0:T(8,128)S(1)}, u32[]{:S(2)}, u32[]{:S(2)}) collective-permute-start(f32[2048,128]{1,0:T(8,128)S(1)} %get-tuple-element.46), channel_id=1, source_target_pairs={{4,0},{5,1},{6,2},{7,3},{0,4},{1,5},{2,6},{3,7},{12,8},{13,9},{14,... | collective-permute-start | bytes 3145736 | tf_op jit(solution)/shard_map/ppermute | solution.py:291
  27.2 2.7 %shard_map.50 = (f32[1024,128]{1,0:T(8,128)S(1)}, f32[1024,128]{1,0:T(8,128)S(1)}, f32[1024,128]{1,0:T(8,128)S(1)}) custom-call(s32[32]{0:T(128)S(1)} %slice_reduce_fusion.refs_0_, bf16[1024,128]{1,0:T(8,128)(2,1)S(1)} %get-tuple-element.26.refs_1_, ...), custom_call_target="tpu_custom_call", output_to_operand_aliasing={{0}: (5, {}), {1}: (6, {}), {2}: (7, {})} | custom-call | flops 603979776 | bytes 1048576 | tf_op jit(solution)/shard_map/pallas_call | solution.py:258
  29.9 1.4 %shard_map.52 = f32[128,1024]{1,0:T(8,128)} custom-call(f32[1024,128]{1,0:T(8,128)S(1)} %get-tuple-element.40.largest_ref, f32[1024,128]{1,0:T(8,128)S(1)} %get-tuple-element.41.totals_ref, f32[1024,128]{1,0:T(8,128)S(1)} %get-tuple-element.42.summed_ref, f32[2048,128]{1,0:T(8,128)S(1)} %collective-permute-done.10.packed_ref), custom_call_target="tpu_custom_call" | custom-call | flops 100663296 | bytes 1048576 | tf_op jit(solution)/shard_map/pallas_call | solution.py:275
  (13 shorter events, 0.1 us)
Async XLA Ops:
  0.0 5.0 %copy-start.1 = (s32[4096]{0:T(1024)S(1)}, s32[4096]{0:T(1024)}, u32[]{:S(2)}) copy-start(s32[4096]{0:T(1024)} %param.7) | copy-start | bytes 49156
  0.8 4.4 %collective-permute-start.6 = (bf16[256,128]{1,0:T(8,128)(2,1)S(1)}, bf16[256,128]{1,0:T(8,128)(2,1)S(1)}, u32[]{:S(2)}, u32[]{:S(2)}) collective-permute-start(bf16[256,128]{1,0:T(8,128)(2,1)S(1)} %shard_map.46.own_ref), channel_id=1, source_target_pairs={{1,0},{0,1},{3,2},{2,3},{5,4},{4,5},{7,6},{6,7},{9,8},{8,9},{11,10... | collective-permute-start | bytes 196616 | tf_op jit(solution)/shard_map/ppermute | solution.py:291
  0.9 6.8 %collective-permute-start.1 = (bf16[256,128]{1,0:T(8,128)(2,1)S(1)}, bf16[256,128]{1,0:T(8,128)(2,1)S(1)}, u32[]{:S(2)}, u32[]{:S(2)}) collective-permute-start(bf16[256,128]{1,0:T(8,128)(2,1)S(1)} %shard_map.46.own_ref), channel_id=1, source_target_pairs={{2,0},{3,1},{0,2},{1,3},{6,4},{7,5},{4,6},{5,7},{10,8},{11,9},{8,1... | collective-permute-start | bytes 196616 | tf_op jit(solution)/shard_map/ppermute | solution.py:291
  3.4 5.3 %collective-permute-start.2 = (bf16[256,128]{1,0:T(8,128)(2,1)S(1)}, bf16[256,128]{1,0:T(8,128)(2,1)S(1)}, u32[]{:S(2)}, u32[]{:S(2)}) collective-permute-start(bf16[256,128]{1,0:T(8,128)(2,1)S(1)} %shard_map.46.own_ref), channel_id=1, source_target_pairs={{3,0},{2,1},{1,2},{0,3},{7,4},{6,5},{5,6},{4,7},{11,8},{10,9},{9,1... | collective-permute-start | bytes 196616 | tf_op jit(solution)/shard_map/ppermute | solution.py:291
  3.5 6.4 %collective-permute-start = (bf16[128,1024]{1,0:T(8,128)(2,1)}, bf16[128,1024]{1,0:T(8,128)(2,1)S(1)}, u32[]{:S(2)}, u32[]{:S(2)}) collective-permute-start(bf16[128,1024]{1,0:T(8,128)(2,1)} %queries_ref.1), channel_id=1, source_target_pairs={{4,0},{5,1},{6,2},{7,3},{0,4},{1,5},{2,6},{3,7},{12,8},{13,9},{14,... | collective-permute-start | bytes 786440 | tf_op jit(solution)/shard_map/ppermute | solution.py:291
  5.2 6.0 %copy-start = (bf16[128,1024]{1,0:T(8,128)(2,1)S(1)}, bf16[128,1024]{1,0:T(8,128)(2,1)}, u32[]{:S(2)}) copy-start(bf16[128,1024]{1,0:T(8,128)(2,1)} %queries_ref.1) | copy-start | bytes 786436
  5.2 8.8 %collective-permute-start.7 = (bf16[512,128]{1,0:T(8,128)(2,1)S(1)}, bf16[512,128]{1,0:T(8,128)(2,1)S(1)}, u32[]{:S(2)}, u32[]{:S(2)}) collective-permute-start(bf16[512,128]{1,0:T(8,128)(2,1)S(1)} %pad_maximum_fusion.refs_3_), channel_id=1, source_target_pairs={{8,0},{9,1},{10,2},{11,3},{20,4},{21,5},{22,6},{23,7},{0,8},{1,9},... | collective-permute-start | bytes 393224 | tf_op jit(solution)/shard_map/ppermute | solution.py:291
  6.5 7.8 %collective-permute-start.8 = (bf16[512,128]{1,0:T(8,128)(2,1)S(1)}, bf16[512,128]{1,0:T(8,128)(2,1)S(1)}, u32[]{:S(2)}, u32[]{:S(2)}) collective-permute-start(bf16[512,128]{1,0:T(8,128)(2,1)S(1)} %pad_maximum_fusion.refs_3_), channel_id=1, source_target_pairs={{16,0},{17,1},{18,2},{19,3},{12,4},{13,5},{14,6},{15,7},{24,8},{25... | collective-permute-start | bytes 393224 | tf_op jit(solution)/shard_map/ppermute | solution.py:291
  7.7 6.5 %collective-permute-start.9 = (bf16[512,128]{1,0:T(8,128)(2,1)S(1)}, bf16[512,128]{1,0:T(8,128)(2,1)S(1)}, u32[]{:S(2)}, u32[]{:S(2)}) collective-permute-start(bf16[512,128]{1,0:T(8,128)(2,1)S(1)} %pad_maximum_fusion.refs_3_), channel_id=1, source_target_pairs={{24,0},{25,1},{26,2},{27,3},{28,4},{29,5},{30,6},{31,7},{16,8},{17... | collective-permute-start | bytes 393224 | tf_op jit(solution)/shard_map/ppermute | solution.py:291
  8.6 11.4 %collective-permute-start.3 = (bf16[512,128]{1,0:T(8,128)(2,1)S(1)}, bf16[512,128]{1,0:T(8,128)(2,1)S(1)}, u32[]{:S(2)}, u32[]{:S(2)}) collective-permute-start(bf16[512,128]{1,0:T(8,128)(2,1)S(1)} %constant_dynamic-update-slice_fusion.refs_6_), channel_id=1, source_target_pairs={{8,0},{9,1},{10,2},{11,3},{20,4},{21,5},{22,6},{23,7},{0,8},{1,9},... | collective-permute-start | bytes 393224 | tf_op jit(solution)/shard_map/ppermute | solution.py:291
  10.0 10.1 %collective-permute-start.4 = (bf16[512,128]{1,0:T(8,128)(2,1)S(1)}, bf16[512,128]{1,0:T(8,128)(2,1)S(1)}, u32[]{:S(2)}, u32[]{:S(2)}) collective-permute-start(bf16[512,128]{1,0:T(8,128)(2,1)S(1)} %constant_dynamic-update-slice_fusion.refs_6_), channel_id=1, source_target_pairs={{16,0},{17,1},{18,2},{19,3},{12,4},{13,5},{14,6},{15,7},{24,8},{25... | collective-permute-start | bytes 393224 | tf_op jit(solution)/shard_map/ppermute | solution.py:291
  14.0 6.1 %collective-permute-start.5 = (bf16[512,128]{1,0:T(8,128)(2,1)S(1)}, bf16[512,128]{1,0:T(8,128)(2,1)S(1)}, u32[]{:S(2)}, u32[]{:S(2)}) collective-permute-start(bf16[512,128]{1,0:T(8,128)(2,1)S(1)} %constant_dynamic-update-slice_fusion.refs_6_), channel_id=1, source_target_pairs={{24,0},{25,1},{26,2},{27,3},{28,4},{29,5},{30,6},{31,7},{16,8},{17... | collective-permute-start | bytes 393224 | tf_op jit(solution)/shard_map/ppermute | solution.py:291
  23.0 6.9 %collective-permute-start.10 = (f32[2048,128]{1,0:T(8,128)S(1)}, f32[2048,128]{1,0:T(8,128)S(1)}, u32[]{:S(2)}, u32[]{:S(2)}) collective-permute-start(f32[2048,128]{1,0:T(8,128)S(1)} %get-tuple-element.46), channel_id=1, source_target_pairs={{4,0},{5,1},{6,2},{7,3},{0,4},{1,5},{2,6},{3,7},{12,8},{13,9},{14,... | collective-permute-start | bytes 3145736 | tf_op jit(solution)/shard_map/ppermute | solution.py:291

commit v7 on v6

--- a/solution.py
+++ b/solution.py
@@ -19,15 +19,15 @@
 SMEM = pl.BlockSpec(memory_space=pltpu.SMEM)
 
 
-def combine(rows, keys, values, sums, to_log2, mask=None, last_counts=None):
+def combine(rows, keys, values, sums, to_log2, mask=None, skip_last=False):
     score = lax.dot_general(
         rows, keys, (((1,), (1,)), ((), ())), preferred_element_type=jnp.float32
     )
     if mask is not None:
         score = jnp.where(mask, score, BIG)
     parts = [score[:, at : at + HD] for at in range(0, keys.shape[0], HD)]
-    if last_counts is not None:
-        parts[-1] = jnp.where(last_counts, parts[-1], BIG)
+    if skip_last:
+        parts[-1] = jnp.full_like(parts[-1], BIG)
     top = jnp.max(functools.reduce(jnp.maximum, parts), axis=1, keepdims=True)
     if sums is None:
         top = jnp.broadcast_to(top, (rows.shape[0], HD))
@@ -134,7 +134,7 @@
         return seen
 
     def attend_group(rows_ref, state, seen):
-        def update(first, number, last_counts=None):
+        def update(first, number, skip_last=False):
             part = pl.ds(pl.multiple_of(first * token, token), number * token)
             sums = [held[...] for held in state]
             new = combine(
@@ -143,22 +143,21 @@
                 values_ref[part, :],
                 sums,
                 TO_LOG2,
-                last_counts=last_counts,
+                skip_last=skip_last,
             )
             for held, value in zip(state, new):
                 held[...] = value
 
         def many(index, _):
-            first = index * STEP
-            update(first, STEP, first + STEP <= seen)
+            update(index * STEP, STEP)
             return 0
 
-        left = seen % STEP
-        full = (seen + 1) // STEP
+        full, left = seen // STEP, seen % STEP
         lax.fori_loop(0, full, many, 0)
         done = full * STEP
         pl.when(left == 1)(functools.partial(update, done, 1))
         pl.when(left == 2)(functools.partial(update, done, 2))
+        pl.when(left == 3)(functools.partial(update, done, STEP, True))
 
     for (group, places), rows_ref, state in zip(groups, rows_refs, states):
         if group in fresh:
@@ -347,8 +346,8 @@
         far = (move(lower[0], both, both, 0), shifted(lower[1], both, both))
         near_up, side_up = spread_near(upper, (one, two))
         far_up = (move(upper[0], both, both, 0), shifted(upper[1], both, both))
-        steps = [[(0, [lower]), (1, [lower])], [(0, [near, side, far, upper]), (1, [near, side, far, upper])], [(1, [near_up, side_up, far_up])]]
-        rest = [near_up, side_up, far_up]
+        steps = [[(1, [lower])], [(0, [near, side, far, upper]), (1, [near, side, far, upper])], [(1, [near_up, side_up, far_up])]]
+        rest = [lower, near_up, side_up, far_up]
     else:
         shared = [held]
         for bits in plan:

time: 31.5 us -> 31.2 us (level)
  no operation moved by 1% of the time
where the time goes in v7:
time: 31.2 us; the launch traced here: 31 us
  Pallas kernels  16.2 us (52%)
  starting transfers between devices  14.1 us (45%)
  waiting for transfers between devices  0.51 us (2%)
    ppermute x11, starting transfers between devices, move(): return lax.ppermute(array, AXES, pairs)  14.1 us
    pallas_call x4, Pallas kernels, attend(): pl.pallas_call(kernel, out_shape=outs, in_specs=[SMEM] + [VMEM] * (len(op...  13.3 us
    pallas_call x1, Pallas kernels, finish(): pl.pallas_call(finish_kernel, out_shape=jax.ShapeDtypeStruct(shape, jnp.f...  1.44 us
    pallas_call x1, Pallas kernels, packed_blocks(): pl.pallas_call(pack_kernel, out_shape=jax.ShapeDtypeStruct((2 * token, wi...  0.8 us
    pallas_call x1, Pallas kernels, attend_own(): pl.pallas_call(own_kernel, out_shape=[rows, rows, sums, sums, sums], in_s...  0.68 us
  transfers between devices with their start and end apart: 11, of which 1 were waited for; matrix products, arithmetic and copies ran while one was open for 0% of the time, Pallas kernels for 36%

profile of v7, /device:TPU:9, one launch (start us, length us, event | category | flops | bytes accessed | tf_op | source)
XLA Modules:
  0.0 31.0 jit_solution(6488770883841114188)
XLA Ops:
  0.0 0.8 %shard_map.46.own_ref = bf16[256,128]{1,0:T(8,128)(2,1)S(1)} custom-call(bf16[128,128]{1,0:T(8,128)(2,1)} %keys_ref.1, bf16[128,128]{1,0:T(8,128)(2,1)} %values_ref.1), custom_call_target="tpu_custom_call" | custom-call | tf_op jit(solution)/shard_map/pallas_call | solution.py:208
  0.8 0.1 collective-permute-start.1
  0.9 2.5 %collective-permute-start.2 = (bf16[256,128]{1,0:T(8,128)(2,1)S(1)}, bf16[256,128]{1,0:T(8,128)(2,1)S(1)}, u32[]{:S(2)}, u32[]{:S(2)}) collective-permute-start(bf16[256,128]{1,0:T(8,128)(2,1)S(1)} %shard_map.46.own_ref), channel_id=1, source_target_pairs={{2,0},{3,1},{0,2},{1,3},{6,4},{7,5},{4,6},{5,7},{10,8},{11,9},{8,1... | collective-permute-start | bytes 196616 | tf_op jit(solution)/shard_map/ppermute | solution.py:290
  3.4 0.2 collective-permute-start.3
  3.5 1.5 %collective-permute-start = (bf16[128,1024]{1,0:T(8,128)(2,1)}, bf16[128,1024]{1,0:T(8,128)(2,1)S(1)}, u32[]{:S(2)}, u32[]{:S(2)}) collective-permute-start(bf16[128,1024]{1,0:T(8,128)(2,1)} %queries_ref.1), channel_id=1, source_target_pairs={{4,0},{5,1},{6,2},{7,3},{0,4},{1,5},{2,6},{3,7},{12,8},{13,9},{14,... | collective-permute-start | bytes 786440 | tf_op jit(solution)/shard_map/ppermute | solution.py:290
  5.0 0.1 slice_reduce_fusion.refs_0_
  5.2 0.0 collective-permute-done.1
  5.2 1.3 %collective-permute-start.7 = (bf16[512,128]{1,0:T(8,128)(2,1)S(1)}, bf16[512,128]{1,0:T(8,128)(2,1)S(1)}, u32[]{:S(2)}, u32[]{:S(2)}) collective-permute-start(bf16[512,128]{1,0:T(8,128)(2,1)S(1)} %pad_maximum_fusion.refs_2_), channel_id=1, source_target_pairs={{8,0},{9,1},{10,2},{11,3},{20,4},{21,5},{22,6},{23,7},{0,8},{1,9},... | collective-permute-start | bytes 393224 | tf_op jit(solution)/shard_map/ppermute | solution.py:290
  6.5 1.2 %collective-permute-start.8 = (bf16[512,128]{1,0:T(8,128)(2,1)S(1)}, bf16[512,128]{1,0:T(8,128)(2,1)S(1)}, u32[]{:S(2)}, u32[]{:S(2)}) collective-permute-start(bf16[512,128]{1,0:T(8,128)(2,1)S(1)} %pad_maximum_fusion.refs_2_), channel_id=1, source_target_pairs={{16,0},{17,1},{18,2},{19,3},{12,4},{13,5},{14,6},{15,7},{24,8},{25... | collective-permute-start | bytes 393224 | tf_op jit(solution)/shard_map/ppermute | solution.py:290
  7.7 0.0 collective-permute-done.2
  7.7 0.4 %collective-permute-start.9 = (bf16[512,128]{1,0:T(8,128)(2,1)S(1)}, bf16[512,128]{1,0:T(8,128)(2,1)S(1)}, u32[]{:S(2)}, u32[]{:S(2)}) collective-permute-start(bf16[512,128]{1,0:T(8,128)(2,1)S(1)} %pad_maximum_fusion.refs_2_), channel_id=1, source_target_pairs={{24,0},{25,1},{26,2},{27,3},{28,4},{29,5},{30,6},{31,7},{16,8},{17... | collective-permute-start | bytes 393224 | tf_op jit(solution)/shard_map/ppermute | solution.py:290
  8.1 0.5 %collective-permute-done.3 = bf16[256,128]{1,0:T(8,128)(2,1)S(1)} collective-permute-done((bf16[256,128]{1,0:T(8,128)(2,1)S(1)}, bf16[256,128]{1,0:T(8,128)(2,1)S(1)}, u32[]{:S(2)}, u32[]{:S(2)}) %collective-permute-start.3) | collective-permute-done | bytes 65568 | tf_op jit(solution)/shard_map/ppermute | solution.py:290
  8.6 1.3 %collective-permute-start.4 = (bf16[512,128]{1,0:T(8,128)(2,1)S(1)}, bf16[512,128]{1,0:T(8,128)(2,1)S(1)}, u32[]{:S(2)}, u32[]{:S(2)}) collective-permute-start(bf16[512,128]{1,0:T(8,128)(2,1)S(1)} %constant_dynamic-update-slice_fusion.refs_6_), channel_id=1, source_target_pairs={{8,0},{9,1},{10,2},{11,3},{20,4},{21,5},{22,6},{23,7},{0,8},{1,9},... | collective-permute-start | bytes 393224 | tf_op jit(solution)/shard_map/ppermute | solution.py:290
  10.0 1.2 %collective-permute-start.5 = (bf16[512,128]{1,0:T(8,128)(2,1)S(1)}, bf16[512,128]{1,0:T(8,128)(2,1)S(1)}, u32[]{:S(2)}, u32[]{:S(2)}) collective-permute-start(bf16[512,128]{1,0:T(8,128)(2,1)S(1)} %constant_dynamic-update-slice_fusion.refs_6_), channel_id=1, source_target_pairs={{16,0},{17,1},{18,2},{19,3},{12,4},{13,5},{14,6},{15,7},{24,8},{25... | collective-permute-start | bytes 393224 | tf_op jit(solution)/shard_map/ppermute | solution.py:290
  11.2 0.7 %shard_map.47 = (bf16[1024,128]{1,0:T(8,128)(2,1)S(1)}, bf16[1024,128]{1,0:T(8,128)(2,1)S(1)}, f32[1024,128]{1,0:T(8,128)S(1)}, f32[1024,128]{1,0:T(8,128)S(1)}, f32[1024,128]{1,0:T(8,128)S(1)}) custom-call(bf16[128,1024]{1,0:T(8,128)(2,1)S(1)} %copy-done, bf16[128,1024]{1,0:T(8,128)(2,1)S(1)} %collective-permute-done.other_ref, ...), custom_call_target="tpu_custom_call" | custom-call | flops 100663296 | bytes 1048576 | tf_op jit(solution)/shard_map/pallas_call | solution.py:223
  11.8 1.4 %shard_map.48 = (f32[1024,128]{1,0:T(8,128)S(1)}, f32[1024,128]{1,0:T(8,128)S(1)}, f32[1024,128]{1,0:T(8,128)S(1)}) custom-call(s32[32]{0:T(128)S(1)} %slice_reduce_fusion.refs_0_, bf16[1024,128]{1,0:T(8,128)(2,1)S(1)} %get-tuple-element.24.refs_1_.refs_2_, bf16[512,128]{1,0:T(8,128)(2,1)S(1)} %pad_maximum_fusion.refs_2_), custom_call_target="tpu_custom_call" | custom-call | flops 201326592 | bytes 1048576 | tf_op jit(solution)/shard_map/pallas_call | solution.py:257
  13.2 0.3 collective-permute-start.6
  13.5 5.9 %shard_map.49 = (f32[1024,128]{1,0:T(8,128)S(1)}, f32[1024,128]{1,0:T(8,128)S(1)}, f32[1024,128]{1,0:T(8,128)S(1)}, f32[1024,128]{1,0:T(8,128)S(1)}, f32[1024,128]{1,0:T(8,128)S(1)}, /*index=5*/f32[1024,128]{1,0:T(8,128)S(1)}) custom-call(s32[32]{0:T(128)S(1)} %slice_reduce_fusion.refs_0_, ...), custom_call_target="tpu_custom_call", output_to_operand_aliasing={{0}: (7, {}), {1}: (8, {}), {2}: (9, {}), {3}: (10, {}), {4... | custom-call | flops 1610612736 | bytes 1048576 | tf_op jit(solution)/shard_map/pallas_call | solution.py:257
  19.5 0.0 collective-permute-done.4.refs_3_.refs_2_
  19.5 0.0 collective-permute-done.5.refs_4_.refs_3_
  19.5 2.8 %shard_map.51 = (f32[1024,128]{1,0:T(8,128)S(1)}, f32[1024,128]{1,0:T(8,128)S(1)}, f32[1024,128]{1,0:T(8,128)S(1)}, f32[2048,128]{1,0:T(8,128)S(1)}) custom-call(s32[32]{0:T(128)S(1)} %slice_reduce_fusion.refs_0_, bf16[1024,128]{1,0:T(8,128)(2,1)S(1)} %get-tuple-element.24.refs_1_.refs_2_, ...), custom_call_target="tpu_custom_call", output_to_operand_aliasing={{0}: (5, {}), {1}: (6, {}), {2}: (7, {})} | custom-call | flops 603979776 | bytes 1048576 | tf_op jit(solution)/shard_map/pallas_call | solution.py:257
  22.3 4.1 %collective-permute-start.10 = (f32[2048,128]{1,0:T(8,128)S(1)}, f32[2048,128]{1,0:T(8,128)S(1)}, u32[]{:S(2)}, u32[]{:S(2)}) collective-permute-start(f32[2048,128]{1,0:T(8,128)S(1)} %get-tuple-element.40), channel_id=1, source_target_pairs={{4,0},{5,1},{6,2},{7,3},{0,4},{1,5},{2,6},{3,7},{12,8},{13,9},{14,... | collective-permute-start | bytes 3145736 | tf_op jit(solution)/shard_map/ppermute | solution.py:290
  26.5 3.1 %shard_map.50 = (f32[1024,128]{1,0:T(8,128)S(1)}, f32[1024,128]{1,0:T(8,128)S(1)}, f32[1024,128]{1,0:T(8,128)S(1)}) custom-call(s32[32]{0:T(128)S(1)} %slice_reduce_fusion.refs_0_, bf16[1024,128]{1,0:T(8,128)(2,1)S(1)} %get-tuple-element.23.refs_1_, ...), custom_call_target="tpu_custom_call", output_to_operand_aliasing={{0}: (6, {}), {1}: (7, {}), {2}: (8, {})} | custom-call | flops 805306368 | bytes 1048576 | tf_op jit(solution)/shard_map/pallas_call | solution.py:257
  29.6 1.4 %shard_map.52 = f32[128,1024]{1,0:T(8,128)} custom-call(f32[1024,128]{1,0:T(8,128)S(1)} %get-tuple-element.34.largest_ref, f32[1024,128]{1,0:T(8,128)S(1)} %get-tuple-element.35.totals_ref, f32[1024,128]{1,0:T(8,128)S(1)} %get-tuple-element.36.summed_ref, f32[2048,128]{1,0:T(8,128)S(1)} %collective-permute-done.10.packed_ref), custom_call_target="tpu_custom_call" | custom-call | flops 100663296 | bytes 1048576 | tf_op jit(solution)/shard_map/pallas_call | solution.py:274
  (13 shorter events, 0.1 us)
Async XLA Ops:
  0.0 5.0 %copy-start.1 = (s32[4096]{0:T(1024)S(1)}, s32[4096]{0:T(1024)}, u32[]{:S(2)}) copy-start(s32[4096]{0:T(1024)} %param.7) | copy-start | bytes 49156
  0.8 4.4 %collective-permute-start.1 = (bf16[256,128]{1,0:T(8,128)(2,1)S(1)}, bf16[256,128]{1,0:T(8,128)(2,1)S(1)}, u32[]{:S(2)}, u32[]{:S(2)}) collective-permute-start(bf16[256,128]{1,0:T(8,128)(2,1)S(1)} %shard_map.46.own_ref), channel_id=1, source_target_pairs={{1,0},{0,1},{3,2},{2,3},{5,4},{4,5},{7,6},{6,7},{9,8},{8,9},{11,10... | collective-permute-start | bytes 196616 | tf_op jit(solution)/shard_map/ppermute | solution.py:290
  0.9 6.8 %collective-permute-start.2 = (bf16[256,128]{1,0:T(8,128)(2,1)S(1)}, bf16[256,128]{1,0:T(8,128)(2,1)S(1)}, u32[]{:S(2)}, u32[]{:S(2)}) collective-permute-start(bf16[256,128]{1,0:T(8,128)(2,1)S(1)} %shard_map.46.own_ref), channel_id=1, source_target_pairs={{2,0},{3,1},{0,2},{1,3},{6,4},{7,5},{4,6},{5,7},{10,8},{11,9},{8,1... | collective-permute-start | bytes 196616 | tf_op jit(solution)/shard_map/ppermute | solution.py:290
  3.4 5.3 %collective-permute-start.3 = (bf16[256,128]{1,0:T(8,128)(2,1)S(1)}, bf16[256,128]{1,0:T(8,128)(2,1)S(1)}, u32[]{:S(2)}, u32[]{:S(2)}) collective-permute-start(bf16[256,128]{1,0:T(8,128)(2,1)S(1)} %shard_map.46.own_ref), channel_id=1, source_target_pairs={{3,0},{2,1},{1,2},{0,3},{7,4},{6,5},{5,6},{4,7},{11,8},{10,9},{9,1... | collective-permute-start | bytes 196616 | tf_op jit(solution)/shard_map/ppermute | solution.py:290
  3.5 6.4 %collective-permute-start = (bf16[128,1024]{1,0:T(8,128)(2,1)}, bf16[128,1024]{1,0:T(8,128)(2,1)S(1)}, u32[]{:S(2)}, u32[]{:S(2)}) collective-permute-start(bf16[128,1024]{1,0:T(8,128)(2,1)} %queries_ref.1), channel_id=1, source_target_pairs={{4,0},{5,1},{6,2},{7,3},{0,4},{1,5},{2,6},{3,7},{12,8},{13,9},{14,... | collective-permute-start | bytes 786440 | tf_op jit(solution)/shard_map/ppermute | solution.py:290
  5.2 6.0 %copy-start = (bf16[128,1024]{1,0:T(8,128)(2,1)S(1)}, bf16[128,1024]{1,0:T(8,128)(2,1)}, u32[]{:S(2)}) copy-start(bf16[128,1024]{1,0:T(8,128)(2,1)} %queries_ref.1) | copy-start | bytes 786436
  5.2 8.0 %collective-permute-start.7 = (bf16[512,128]{1,0:T(8,128)(2,1)S(1)}, bf16[512,128]{1,0:T(8,128)(2,1)S(1)}, u32[]{:S(2)}, u32[]{:S(2)}) collective-permute-start(bf16[512,128]{1,0:T(8,128)(2,1)S(1)} %pad_maximum_fusion.refs_2_), channel_id=1, source_target_pairs={{8,0},{9,1},{10,2},{11,3},{20,4},{21,5},{22,6},{23,7},{0,8},{1,9},... | collective-permute-start | bytes 393224 | tf_op jit(solution)/shard_map/ppermute | solution.py:290
  6.5 7.0 %collective-permute-start.8 = (bf16[512,128]{1,0:T(8,128)(2,1)S(1)}, bf16[512,128]{1,0:T(8,128)(2,1)S(1)}, u32[]{:S(2)}, u32[]{:S(2)}) collective-permute-start(bf16[512,128]{1,0:T(8,128)(2,1)S(1)} %pad_maximum_fusion.refs_2_), channel_id=1, source_target_pairs={{16,0},{17,1},{18,2},{19,3},{12,4},{13,5},{14,6},{15,7},{24,8},{25... | collective-permute-start | bytes 393224 | tf_op jit(solution)/shard_map/ppermute | solution.py:290
  7.7 5.8 %collective-permute-start.9 = (bf16[512,128]{1,0:T(8,128)(2,1)S(1)}, bf16[512,128]{1,0:T(8,128)(2,1)S(1)}, u32[]{:S(2)}, u32[]{:S(2)}) collective-permute-start(bf16[512,128]{1,0:T(8,128)(2,1)S(1)} %pad_maximum_fusion.refs_2_), channel_id=1, source_target_pairs={{24,0},{25,1},{26,2},{27,3},{28,4},{29,5},{30,6},{31,7},{16,8},{17... | collective-permute-start | bytes 393224 | tf_op jit(solution)/shard_map/ppermute | solution.py:290
  8.6 10.8 %collective-permute-start.4 = (bf16[512,128]{1,0:T(8,128)(2,1)S(1)}, bf16[512,128]{1,0:T(8,128)(2,1)S(1)}, u32[]{:S(2)}, u32[]{:S(2)}) collective-permute-start(bf16[512,128]{1,0:T(8,128)(2,1)S(1)} %constant_dynamic-update-slice_fusion.refs_6_), channel_id=1, source_target_pairs={{8,0},{9,1},{10,2},{11,3},{20,4},{21,5},{22,6},{23,7},{0,8},{1,9},... | collective-permute-start | bytes 393224 | tf_op jit(solution)/shard_map/ppermute | solution.py:290
  10.0 9.5 %collective-permute-start.5 = (bf16[512,128]{1,0:T(8,128)(2,1)S(1)}, bf16[512,128]{1,0:T(8,128)(2,1)S(1)}, u32[]{:S(2)}, u32[]{:S(2)}) collective-permute-start(bf16[512,128]{1,0:T(8,128)(2,1)S(1)} %constant_dynamic-update-slice_fusion.refs_6_), channel_id=1, source_target_pairs={{16,0},{17,1},{18,2},{19,3},{12,4},{13,5},{14,6},{15,7},{24,8},{25... | collective-permute-start | bytes 393224 | tf_op jit(solution)/shard_map/ppermute | solution.py:290
  13.2 6.2 %collective-permute-start.6 = (bf16[512,128]{1,0:T(8,128)(2,1)S(1)}, bf16[512,128]{1,0:T(8,128)(2,1)S(1)}, u32[]{:S(2)}, u32[]{:S(2)}) collective-permute-start(bf16[512,128]{1,0:T(8,128)(2,1)S(1)} %constant_dynamic-update-slice_fusion.refs_6_), channel_id=1, source_target_pairs={{24,0},{25,1},{26,2},{27,3},{28,4},{29,5},{30,6},{31,7},{16,8},{17... | collective-permute-start | bytes 393224 | tf_op jit(solution)/shard_map/ppermute | solution.py:290
  22.3 7.3 %collective-permute-start.10 = (f32[2048,128]{1,0:T(8,128)S(1)}, f32[2048,128]{1,0:T(8,128)S(1)}, u32[]{:S(2)}, u32[]{:S(2)}) collective-permute-start(f32[2048,128]{1,0:T(8,128)S(1)} %get-tuple-element.40), channel_id=1, source_target_pairs={{4,0},{5,1},{6,2},{7,3},{0,4},{1,5},{2,6},{3,7},{12,8},{13,9},{14,... | collective-permute-start | bytes 3145736 | tf_op jit(solution)/shard_map/ppermute | solution.py:290

commit v8 on v7

--- a/solution.py
+++ b/solution.py
@@ -34,8 +34,6 @@
     else:
         top = jnp.maximum(sums[0], top)
     weights = [jnp.exp2((part - top) * to_log2) for part in parts]
-    if mask is not None:
-        weights = [jnp.where(mask, weight, 0.0) for weight in weights]
     total = functools.reduce(jnp.add, weights)
     highs = [weight.astype(jnp.bfloat16) for weight in weights]
     lows = [
@@ -346,8 +344,8 @@
         far = (move(lower[0], both, both, 0), shifted(lower[1], both, both))
         near_up, side_up = spread_near(upper, (one, two))
         far_up = (move(upper[0], both, both, 0), shifted(upper[1], both, both))
-        steps = [[(1, [lower])], [(0, [near, side, far, upper]), (1, [near, side, far, upper])], [(1, [near_up, side_up, far_up])]]
-        rest = [lower, near_up, side_up, far_up]
+        steps = [[(0, [lower]), (1, [lower])], [(0, [near, side, far, upper]), (1, [near, side, far, upper])], [(1, [near_up, side_up, far_up])]]
+        rest = [near_up, side_up, far_up]
     else:
         shared = [held]
         for bits in plan:

time: 31.2 us -> 31.5 us (level)
  no operation moved by 1% of the time
where the time goes in v8:
time: 31.5 us; the launch traced here: 31.3 us
  Pallas kernels  16.4 us (52%)
  starting transfers between devices  14.1 us (45%)
  waiting for transfers between devices  0.51 us (2%)
    ppermute x11, starting transfers between devices, move(): return lax.ppermute(array, AXES, pairs)  14.1 us
    pallas_call x4, Pallas kernels, attend(): pl.pallas_call(kernel, out_shape=outs, in_specs=[SMEM] + [VMEM] * (len(op...  13.5 us
    pallas_call x1, Pallas kernels, finish(): pl.pallas_call(finish_kernel, out_shape=jax.ShapeDtypeStruct(shape, jnp.f...  1.44 us
    pallas_call x1, Pallas kernels, packed_blocks(): pl.pallas_call(pack_kernel, out_shape=jax.ShapeDtypeStruct((2 * token, wi...  0.8 us
    pallas_call x1, Pallas kernels, attend_own(): pl.pallas_call(own_kernel, out_shape=[rows, rows, sums, sums, sums], in_s...  0.67 us
  transfers between devices with their start and end apart: 11, of which 1 were waited for; matrix products, arithmetic and copies ran while one was open for 0% of the time, Pallas kernels for 36%

profile of v8, /device:TPU:9, one launch (start us, length us, event | category | flops | bytes accessed | tf_op | source)
XLA Modules:
  0.0 31.3 jit_solution(18030889591288839634)
XLA Ops:
  0.0 0.8 %shard_map.46.own_ref = bf16[256,128]{1,0:T(8,128)(2,1)S(1)} custom-call(bf16[128,128]{1,0:T(8,128)(2,1)} %keys_ref.1, bf16[128,128]{1,0:T(8,128)(2,1)} %values_ref.1), custom_call_target="tpu_custom_call" | custom-call | tf_op jit(solution)/shard_map/pallas_call | solution.py:206
  0.8 0.1 collective-permute-start.6
  0.9 2.5 %collective-permute-start.1 = (bf16[256,128]{1,0:T(8,128)(2,1)S(1)}, bf16[256,128]{1,0:T(8,128)(2,1)S(1)}, u32[]{:S(2)}, u32[]{:S(2)}) collective-permute-start(bf16[256,128]{1,0:T(8,128)(2,1)S(1)} %shard_map.46.own_ref), channel_id=1, source_target_pairs={{2,0},{3,1},{0,2},{1,3},{6,4},{7,5},{4,6},{5,7},{10,8},{11,9},{8,1... | collective-permute-start | bytes 196616 | tf_op jit(solution)/shard_map/ppermute | solution.py:288
  3.4 0.2 collective-permute-start.2
  3.5 1.5 %collective-permute-start = (bf16[128,1024]{1,0:T(8,128)(2,1)}, bf16[128,1024]{1,0:T(8,128)(2,1)S(1)}, u32[]{:S(2)}, u32[]{:S(2)}) collective-permute-start(bf16[128,1024]{1,0:T(8,128)(2,1)} %queries_ref.1), channel_id=1, source_target_pairs={{4,0},{5,1},{6,2},{7,3},{0,4},{1,5},{2,6},{3,7},{12,8},{13,9},{14,... | collective-permute-start | bytes 786440 | tf_op jit(solution)/shard_map/ppermute | solution.py:288
  5.0 0.1 slice_reduce_fusion.refs_0_
  5.2 0.0 collective-permute-done.6
  5.2 1.3 %collective-permute-start.7 = (bf16[512,128]{1,0:T(8,128)(2,1)S(1)}, bf16[512,128]{1,0:T(8,128)(2,1)S(1)}, u32[]{:S(2)}, u32[]{:S(2)}) collective-permute-start(bf16[512,128]{1,0:T(8,128)(2,1)S(1)} %pad_maximum_fusion.refs_3_), channel_id=1, source_target_pairs={{8,0},{9,1},{10,2},{11,3},{20,4},{21,5},{22,6},{23,7},{0,8},{1,9},... | collective-permute-start | bytes 393224 | tf_op jit(solution)/shard_map/ppermute | solution.py:288
  6.5 1.2 %collective-permute-start.8 = (bf16[512,128]{1,0:T(8,128)(2,1)S(1)}, bf16[512,128]{1,0:T(8,128)(2,1)S(1)}, u32[]{:S(2)}, u32[]{:S(2)}) collective-permute-start(bf16[512,128]{1,0:T(8,128)(2,1)S(1)} %pad_maximum_fusion.refs_3_), channel_id=1, source_target_pairs={{16,0},{17,1},{18,2},{19,3},{12,4},{13,5},{14,6},{15,7},{24,8},{25... | collective-permute-start | bytes 393224 | tf_op jit(solution)/shard_map/ppermute | solution.py:288
  7.7 0.4 %collective-permute-start.9 = (bf16[512,128]{1,0:T(8,128)(2,1)S(1)}, bf16[512,128]{1,0:T(8,128)(2,1)S(1)}, u32[]{:S(2)}, u32[]{:S(2)}) collective-permute-start(bf16[512,128]{1,0:T(8,128)(2,1)S(1)} %pad_maximum_fusion.refs_3_), channel_id=1, source_target_pairs={{24,0},{25,1},{26,2},{27,3},{28,4},{29,5},{30,6},{31,7},{16,8},{17... | collective-permute-start | bytes 393224 | tf_op jit(solution)/shard_map/ppermute | solution.py:288
  8.1 0.5 %collective-permute-done.2 = bf16[256,128]{1,0:T(8,128)(2,1)S(1)} collective-permute-done((bf16[256,128]{1,0:T(8,128)(2,1)S(1)}, bf16[256,128]{1,0:T(8,128)(2,1)S(1)}, u32[]{:S(2)}, u32[]{:S(2)}) %collective-permute-start.2) | collective-permute-done | bytes 65568 | tf_op jit(solution)/shard_map/ppermute | solution.py:288
  8.6 1.3 %collective-permute-start.3 = (bf16[512,128]{1,0:T(8,128)(2,1)S(1)}, bf16[512,128]{1,0:T(8,128)(2,1)S(1)}, u32[]{:S(2)}, u32[]{:S(2)}) collective-permute-start(bf16[512,128]{1,0:T(8,128)(2,1)S(1)} %constant_dynamic-update-slice_fusion.refs_6_), channel_id=1, source_target_pairs={{8,0},{9,1},{10,2},{11,3},{20,4},{21,5},{22,6},{23,7},{0,8},{1,9},... | collective-permute-start | bytes 393224 | tf_op jit(solution)/shard_map/ppermute | solution.py:288
  10.0 1.2 %collective-permute-start.4 = (bf16[512,128]{1,0:T(8,128)(2,1)S(1)}, bf16[512,128]{1,0:T(8,128)(2,1)S(1)}, u32[]{:S(2)}, u32[]{:S(2)}) collective-permute-start(bf16[512,128]{1,0:T(8,128)(2,1)S(1)} %constant_dynamic-update-slice_fusion.refs_6_), channel_id=1, source_target_pairs={{16,0},{17,1},{18,2},{19,3},{12,4},{13,5},{14,6},{15,7},{24,8},{25... | collective-permute-start | bytes 393224 | tf_op jit(solution)/shard_map/ppermute | solution.py:288
  11.2 0.7 %shard_map.47 = (bf16[1024,128]{1,0:T(8,128)(2,1)S(1)}, bf16[1024,128]{1,0:T(8,128)(2,1)S(1)}, f32[1024,128]{1,0:T(8,128)S(1)}, f32[1024,128]{1,0:T(8,128)S(1)}, f32[1024,128]{1,0:T(8,128)S(1)}) custom-call(bf16[128,1024]{1,0:T(8,128)(2,1)S(1)} %copy-done, bf16[128,1024]{1,0:T(8,128)(2,1)S(1)} %collective-permute-done.other_ref, ...), custom_call_target="tpu_custom_call" | custom-call | flops 100663296 | bytes 1048576 | tf_op jit(solution)/shard_map/pallas_call | solution.py:221
  11.8 2.1 %shard_map.48 = (f32[1024,128]{1,0:T(8,128)S(1)}, f32[1024,128]{1,0:T(8,128)S(1)}, f32[1024,128]{1,0:T(8,128)S(1)}, f32[1024,128]{1,0:T(8,128)S(1)}, f32[1024,128]{1,0:T(8,128)S(1)}, /*index=5*/f32[1024,128]{1,0:T(8,128)S(1)}) custom-call(s32[32]{0:T(128)S(1)} %slice_reduce_fusion.refs_0_, ...), custom_call_target="tpu_custom_call", output_to_operand_aliasing={{0}: (4, {}), {1}: (5, {}), {2}: (6, {})} | custom-call | flops 402653184 | bytes 1048576 | tf_op jit(solution)/shard_map/pallas_call | solution.py:255
  14.0 0.0 collective-permute-done.7.refs_3_
  14.0 0.3 collective-permute-start.5
  14.3 0.0 collective-permute-done.8.refs_4_
  14.3 0.0 collective-permute-done.9.refs_5_
  14.3 5.9 %shard_map.49 = (f32[1024,128]{1,0:T(8,128)S(1)}, f32[1024,128]{1,0:T(8,128)S(1)}, f32[1024,128]{1,0:T(8,128)S(1)}, f32[1024,128]{1,0:T(8,128)S(1)}, f32[1024,128]{1,0:T(8,128)S(1)}, /*index=5*/f32[1024,128]{1,0:T(8,128)S(1)}) custom-call(s32[32]{0:T(128)S(1)} %slice_reduce_fusion.refs_0_, ...), custom_call_target="tpu_custom_call", output_to_operand_aliasing={{0}: (7, {}), {1}: (8, {}), {2}: (9, {}), {3}: (10, {}), {4... | custom-call | flops 1610612736 | bytes 1048576 | tf_op jit(solution)/shard_map/pallas_call | solution.py:255
  20.2 2.8 %shard_map.51 = (f32[1024,128]{1,0:T(8,128)S(1)}, f32[1024,128]{1,0:T(8,128)S(1)}, f32[1024,128]{1,0:T(8,128)S(1)}, f32[2048,128]{1,0:T(8,128)S(1)}) custom-call(s32[32]{0:T(128)S(1)} %slice_reduce_fusion.refs_0_, bf16[1024,128]{1,0:T(8,128)(2,1)S(1)} %get-tuple-element.27.refs_2_.refs_1_, ...), custom_call_target="tpu_custom_call", output_to_operand_aliasing={{0}: (5, {}), {1}: (6, {}), {2}: (7, {})} | custom-call | flops 603979776 | bytes 1048576 | tf_op jit(solution)/shard_map/pallas_call | solution.py:255
  23.0 4.1 %collective-permute-start.10 = (f32[2048,128]{1,0:T(8,128)S(1)}, f32[2048,128]{1,0:T(8,128)S(1)}, u32[]{:S(2)}, u32[]{:S(2)}) collective-permute-start(f32[2048,128]{1,0:T(8,128)S(1)} %get-tuple-element.46), channel_id=1, source_target_pairs={{4,0},{5,1},{6,2},{7,3},{0,4},{1,5},{2,6},{3,7},{12,8},{13,9},{14,... | collective-permute-start | bytes 3145736 | tf_op jit(solution)/shard_map/ppermute | solution.py:288
  27.1 2.7 %shard_map.50 = (f32[1024,128]{1,0:T(8,128)S(1)}, f32[1024,128]{1,0:T(8,128)S(1)}, f32[1024,128]{1,0:T(8,128)S(1)}) custom-call(s32[32]{0:T(128)S(1)} %slice_reduce_fusion.refs_0_, bf16[1024,128]{1,0:T(8,128)(2,1)S(1)} %get-tuple-element.26.refs_1_, ...), custom_call_target="tpu_custom_call", output_to_operand_aliasing={{0}: (5, {}), {1}: (6, {}), {2}: (7, {})} | custom-call | flops 603979776 | bytes 1048576 | tf_op jit(solution)/shard_map/pallas_call | solution.py:255
  29.9 1.4 %shard_map.52 = f32[128,1024]{1,0:T(8,128)} custom-call(f32[1024,128]{1,0:T(8,128)S(1)} %get-tuple-element.40.largest_ref, f32[1024,128]{1,0:T(8,128)S(1)} %get-tuple-element.41.totals_ref, f32[1024,128]{1,0:T(8,128)S(1)} %get-tuple-element.42.summed_ref, f32[2048,128]{1,0:T(8,128)S(1)} %collective-permute-done.10.packed_ref), custom_call_target="tpu_custom_call" | custom-call | flops 100663296 | bytes 1048576 | tf_op jit(solution)/shard_map/pallas_call | solution.py:272
  (13 shorter events, 0.1 us)
Async XLA Ops:
  0.0 5.0 %copy-start.1 = (s32[4096]{0:T(1024)S(1)}, s32[4096]{0:T(1024)}, u32[]{:S(2)}) copy-start(s32[4096]{0:T(1024)} %param.7) | copy-start | bytes 49156
  0.8 4.4 %collective-permute-start.6 = (bf16[256,128]{1,0:T(8,128)(2,1)S(1)}, bf16[256,128]{1,0:T(8,128)(2,1)S(1)}, u32[]{:S(2)}, u32[]{:S(2)}) collective-permute-start(bf16[256,128]{1,0:T(8,128)(2,1)S(1)} %shard_map.46.own_ref), channel_id=1, source_target_pairs={{1,0},{0,1},{3,2},{2,3},{5,4},{4,5},{7,6},{6,7},{9,8},{8,9},{11,10... | collective-permute-start | bytes 196616 | tf_op jit(solution)/shard_map/ppermute | solution.py:288
  0.9 6.8 %collective-permute-start.1 = (bf16[256,128]{1,0:T(8,128)(2,1)S(1)}, bf16[256,128]{1,0:T(8,128)(2,1)S(1)}, u32[]{:S(2)}, u32[]{:S(2)}) collective-permute-start(bf16[256,128]{1,0:T(8,128)(2,1)S(1)} %shard_map.46.own_ref), channel_id=1, source_target_pairs={{2,0},{3,1},{0,2},{1,3},{6,4},{7,5},{4,6},{5,7},{10,8},{11,9},{8,1... | collective-permute-start | bytes 196616 | tf_op jit(solution)/shard_map/ppermute | solution.py:288
  3.4 5.3 %collective-permute-start.2 = (bf16[256,128]{1,0:T(8,128)(2,1)S(1)}, bf16[256,128]{1,0:T(8,128)(2,1)S(1)}, u32[]{:S(2)}, u32[]{:S(2)}) collective-permute-start(bf16[256,128]{1,0:T(8,128)(2,1)S(1)} %shard_map.46.own_ref), channel_id=1, source_target_pairs={{3,0},{2,1},{1,2},{0,3},{7,4},{6,5},{5,6},{4,7},{11,8},{10,9},{9,1... | collective-permute-start | bytes 196616 | tf_op jit(solution)/shard_map/ppermute | solution.py:288
  3.5 6.4 %collective-permute-start = (bf16[128,1024]{1,0:T(8,128)(2,1)}, bf16[128,1024]{1,0:T(8,128)(2,1)S(1)}, u32[]{:S(2)}, u32[]{:S(2)}) collective-permute-start(bf16[128,1024]{1,0:T(8,128)(2,1)} %queries_ref.1), channel_id=1, source_target_pairs={{4,0},{5,1},{6,2},{7,3},{0,4},{1,5},{2,6},{3,7},{12,8},{13,9},{14,... | collective-permute-start | bytes 786440 | tf_op jit(solution)/shard_map/ppermute | solution.py:288
  5.2 6.0 %copy-start = (bf16[128,1024]{1,0:T(8,128)(2,1)S(1)}, bf16[128,1024]{1,0:T(8,128)(2,1)}, u32[]{:S(2)}) copy-start(bf16[128,1024]{1,0:T(8,128)(2,1)} %queries_ref.1) | copy-start | bytes 786436
  5.2 8.8 %collective-permute-start.7 = (bf16[512,128]{1,0:T(8,128)(2,1)S(1)}, bf16[512,128]{1,0:T(8,128)(2,1)S(1)}, u32[]{:S(2)}, u32[]{:S(2)}) collective-permute-start(bf16[512,128]{1,0:T(8,128)(2,1)S(1)} %pad_maximum_fusion.refs_3_), channel_id=1, source_target_pairs={{8,0},{9,1},{10,2},{11,3},{20,4},{21,5},{22,6},{23,7},{0,8},{1,9},... | collective-permute-start | bytes 393224 | tf_op jit(solution)/shard_map/ppermute | solution.py:288
  6.5 7.8 %collective-permute-start.8 = (bf16[512,128]{1,0:T(8,128)(2,1)S(1)}, bf16[512,128]{1,0:T(8,128)(2,1)S(1)}, u32[]{:S(2)}, u32[]{:S(2)}) collective-permute-start(bf16[512,128]{1,0:T(8,128)(2,1)S(1)} %pad_maximum_fusion.refs_3_), channel_id=1, source_target_pairs={{16,0},{17,1},{18,2},{19,3},{12,4},{13,5},{14,6},{15,7},{24,8},{25... | collective-permute-start | bytes 393224 | tf_op jit(solution)/shard_map/ppermute | solution.py:288
  7.7 6.5 %collective-permute-start.9 = (bf16[512,128]{1,0:T(8,128)(2,1)S(1)}, bf16[512,128]{1,0:T(8,128)(2,1)S(1)}, u32[]{:S(2)}, u32[]{:S(2)}) collective-permute-start(bf16[512,128]{1,0:T(8,128)(2,1)S(1)} %pad_maximum_fusion.refs_3_), channel_id=1, source_target_pairs={{24,0},{25,1},{26,2},{27,3},{28,4},{29,5},{30,6},{31,7},{16,8},{17... | collective-permute-start | bytes 393224 | tf_op jit(solution)/shard_map/ppermute | solution.py:288
  8.6 11.5 %collective-permute-start.3 = (bf16[512,128]{1,0:T(8,128)(2,1)S(1)}, bf16[512,128]{1,0:T(8,128)(2,1)S(1)}, u32[]{:S(2)}, u32[]{:S(2)}) collective-permute-start(bf16[512,128]{1,0:T(8,128)(2,1)S(1)} %constant_dynamic-update-slice_fusion.refs_6_), channel_id=1, source_target_pairs={{8,0},{9,1},{10,2},{11,3},{20,4},{21,5},{22,6},{23,7},{0,8},{1,9},... | collective-permute-start | bytes 393224 | tf_op jit(solution)/shard_map/ppermute | solution.py:288
  10.0 10.2 %collective-permute-start.4 = (bf16[512,128]{1,0:T(8,128)(2,1)S(1)}, bf16[512,128]{1,0:T(8,128)(2,1)S(1)}, u32[]{:S(2)}, u32[]{:S(2)}) collective-permute-start(bf16[512,128]{1,0:T(8,128)(2,1)S(1)} %constant_dynamic-update-slice_fusion.refs_6_), channel_id=1, source_target_pairs={{16,0},{17,1},{18,2},{19,3},{12,4},{13,5},{14,6},{15,7},{24,8},{25... | collective-permute-start | bytes 393224 | tf_op jit(solution)/shard_map/ppermute | solution.py:288
  14.0 6.2 %collective-permute-start.5 = (bf16[512,128]{1,0:T(8,128)(2,1)S(1)}, bf16[512,128]{1,0:T(8,128)(2,1)S(1)}, u32[]{:S(2)}, u32[]{:S(2)}) collective-permute-start(bf16[512,128]{1,0:T(8,128)(2,1)S(1)} %constant_dynamic-update-slice_fusion.refs_6_), channel_id=1, source_target_pairs={{24,0},{25,1},{26,2},{27,3},{28,4},{29,5},{30,6},{31,7},{16,8},{17... | collective-permute-start | bytes 393224 | tf_op jit(solution)/shard_map/ppermute | solution.py:288
  23.0 6.9 %collective-permute-start.10 = (f32[2048,128]{1,0:T(8,128)S(1)}, f32[2048,128]{1,0:T(8,128)S(1)}, u32[]{:S(2)}, u32[]{:S(2)}) collective-permute-start(f32[2048,128]{1,0:T(8,128)S(1)} %get-tuple-element.46), channel_id=1, source_target_pairs={{4,0},{5,1},{6,2},{7,3},{0,4},{1,5},{2,6},{3,7},{12,8},{13,9},{14,... | collective-permute-start | bytes 3145736 | tf_op jit(solution)/shard_map/ppermute | solution.py:288
